TPU v7x, 32 devices: a whole 2x2x4 slice. The times are simulated.
32 devices in a mesh: gx: 4 (over y, x), gy: 8 (over z, core).
Axes of the slice: x: 2, y: 2, z: 4, core: 2. Of those that a mesh axis runs over, the one named last changes fastest.
Arguments:
- forcing: float32 [3, 64, 128, 128], P(None, 'gx', 'gy'), may hold values from -6 to 6
- phase_index: int32 [64, 128, 128], P('gx', 'gy'), may hold values from 0 to 7
- visc_table: float32 [8], replicated, may hold values from 0.001 to 1000
- lower_bound: float32 [1], replicated, may hold values from 0.1 to 0.4
- upper_bound: float32 [1], replicated, may hold values from 1.9 to 2.3
Outputs:
- residual: float32 [3, 64, 128, 128], P(None, 'gx', 'gy')
Inputs may be any that keep to these rules, and one draw needn't show every extreme that they name: `phase_index`: each entry names a row of visc_table.
All inputs are finite; a program needn't handle non-finite values.
Results may differ from a plain program's by a relative error of at most 0.000027.
Values sent between devices are 32-bit elements; how exact they have to be, the bound alone decides.
No kernel may reach another device: no remote copies, remote signals or barrier semaphores. Data moves between devices by JAX's collectives and lax.ppermute only.
A program may use at most 128 MiB of HBM per device.

v0:
```python
import jax
import jax.numpy as jnp
from jax import lax
from jax.sharding import PartitionSpec as P

CHEB = 4
COARSE_STEPS = 4


def padded_2(shard, sides, width):
    for axis, dim in sides:
        devices, length = (lax.axis_size(axis), shard.shape[dim])
        up = [(i, (i + 1) % devices) for i in range(devices - 1)]
        down = [(j, i) for i, j in up]
        last = lax.slice_in_dim(shard, length - width, length, axis=dim)
        first = lax.slice_in_dim(shard, 0, width, axis=dim)
        before = lax.ppermute(last, axis, up)
        after = lax.ppermute(first, axis, down)
        shard = jnp.concatenate([before, shard, after], axis=dim)
    return shard


def diagonal_sum(faces):
    return faces[0] + faces[1] + faces[2] + faces[3] + faces[4] + faces[5]


def build_terms(eta_wide):
    centre = eta_wide[1:-1, 1:-1]
    depth_pad = jnp.pad(centre, ((0, 0), (0, 0), (1, 1)))
    lower_x = 0.5 * (centre + eta_wide[:-2, 1:-1])
    upper_x = 0.5 * (centre + eta_wide[2:, 1:-1])
    lower_y = 0.5 * (centre + eta_wide[1:-1, :-2])
    upper_y = 0.5 * (centre + eta_wide[1:-1, 2:])
    lower_z = 0.5 * (centre + depth_pad[:, :, :-2])
    upper_z = 0.5 * (centre + depth_pad[:, :, 2:])
    faces = (lower_x, upper_x, lower_y, upper_y, lower_z, upper_z)
    return faces + (diagonal_sum(faces),)


def apply_local(padded, face_terms):
    lower_x, upper_x, lower_y, upper_y, lower_z, upper_z, diagonal = face_terms
    centre = padded[..., 1:-1, 1:-1, :]
    widths = [(0, 0)] * (centre.ndim - 1) + [(1, 1)]
    depth_pad = jnp.pad(centre, widths)
    beside = lower_x * padded[..., :-2, 1:-1, :] + upper_x * padded[..., 2:, 1:-1, :]
    beside = beside + lower_y * padded[..., 1:-1, :-2, :] + upper_y * padded[..., 1:-1, 2:, :]
    beside = beside + lower_z * depth_pad[..., :-2] + upper_z * depth_pad[..., 2:]
    return diagonal * centre - beside


def pick_child(face_term, along, which_child):
    row_count, col_count, depth_count = face_term.shape
    blocks = face_term.reshape(row_count // 2, 2, col_count // 2, 2, depth_count // 2, 2)
    selector = jnp.array([1.0 - which_child, 1.0 * which_child], jnp.float32)
    layout = [1, 1, 1, 1, 1, 1]
    layout[2 * along + 1] = 2
    return 0.0625 * jnp.sum(blocks * selector.reshape(layout), axis=(1, 3, 5))


def coarse_terms(face_terms):
    faces = (
        pick_child(face_terms[0], 0, 0),
        pick_child(face_terms[1], 0, 1),
        pick_child(face_terms[2], 1, 0),
        pick_child(face_terms[3], 1, 1),
        pick_child(face_terms[4], 2, 0),
        pick_child(face_terms[5], 2, 1),
    )
    return faces + (diagonal_sum(faces),)


def restrict(field):
    row_count, col_count, depth_count = field.shape[-3:]
    blocks = field.reshape(
        field.shape[:-3] + (row_count // 2, 2, col_count // 2, 2, depth_count // 2, 2)
    )
    return 0.125 * jnp.sum(blocks, axis=(-5, -3, -1))


def prolong(field):
    for along in (-3, -2, -1):
        field = jnp.repeat(field, 2, axis=along)
    return field


def chebyshev_constants(lower_value, upper_value, count):
    centre = 0.5 * (upper_value + lower_value)
    radius = 0.5 * (upper_value - lower_value)
    spread = centre / radius
    damping = 1.0 / spread
    carried = []
    scaled = []
    for number in range(count - 1):
        renewed = 1.0 / (2.0 * spread - damping)
        carried.append(renewed * damping)
        scaled.append(2.0 * renewed / radius)
        damping = renewed
    return (1.0 / centre, carried, scaled)


def fine_rim(field):
    return padded_2(field, (("gx", 1), ("gy", 2)), 1)


def coarse_rim(field):
    return padded_2(field, (("gx", 1), ("gy", 2)), 1)


def coarse_smooth(source, coarse_set, rim_call, first_scale, carried, scaled):
    coarse_inverse = 1.0 / coarse_set[6]
    direction = first_scale * coarse_inverse * source
    correction = direction
    for number in range(COARSE_STEPS - 1):
        source = source - apply_local(rim_call(direction), coarse_set)
        direction = carried[number] * direction + scaled[number] * coarse_inverse * source
        correction = correction + direction
    return correction


def local(forcing, phase_index, visc_table, lower_bound, upper_bound):
    viscosity = jnp.zeros(phase_index.shape, jnp.float32)
    for table_row in range(visc_table.shape[0]):
        viscosity = jnp.where(phase_index == table_row, visc_table[table_row], viscosity)
    eta_wide = padded_2(viscosity, (("gx", 0), ("gy", 1)), 2)
    terms_wide = build_terms(eta_wide)
    face_terms = tuple((term[1:-1, 1:-1] for term in terms_wide))
    inverse = 1.0 / face_terms[6]
    coarse_set = coarse_terms(face_terms)
    first_scale, carried, scaled = chebyshev_constants(
        lower_bound[0], upper_bound[0], max(CHEB, COARSE_STEPS)
    )

    def smooth(residual):
        direction = first_scale * inverse * residual
        for number in range(CHEB):
            residual = residual - apply_local(fine_rim(direction), face_terms)
            if number + 1 < CHEB:
                direction = carried[number] * direction + scaled[number] * inverse * residual
        return residual

    residual = smooth(forcing)
    source = restrict(residual)
    correction = coarse_smooth(source, coarse_set, coarse_rim, first_scale, carried, scaled)
    prolonged = prolong(correction)
    padded = padded_2(prolonged, (("gx", 1), ("gy", 2)), 1)
    residual = residual - apply_local(padded, face_terms)
    return smooth(residual)


def solution(mesh):
    in_specs = (P(None, "gx", "gy", None), P("gx", "gy", None), P(), P(), P())
    out_specs = P(None, "gx", "gy", None)
    return jax.shard_map(local, mesh=mesh, in_specs=in_specs, out_specs=out_specs, check_vma=False)
```

profile of v0, /device:TPU:1, one launch (start us, length us, event | category | flops | bytes accessed | tf_op | source)
XLA Modules:
  0.0 328.8 jit_solution(11193157744100796052)
XLA Ops:
  0.0 1.6 fusion.190
  1.6 5.9 %select_select_fusion = f32[16,16,128]{2,1,0:T(8,128)S(1)} fusion(s32[16,16,128]{2,1,0:T(8,128)} %param.12, f32[]{:T(128)} %bitcast.7, f32[]{:T(128)} %bitcast.6, f32[]{:T(128)} %bitcast.5, f32[]{:T(128)} %bitcast.4, f32[]{:T(128)} %bitcast.3, f32[]{:T(128)} %bitcast.2, f32[]{:T(128)} %bitcast.1, f32[]{:T(128)} %bitcast), kind=kLoop, calls=%fused_computation.248 | loop fusion | flops 524288 | bytes 262176 | tf_op jit(solution)/shard_map/jit(_where)/select_n | solution.py:123
  7.6 1.3 collective-permute-start.1
  8.9 4.6 %collective-permute-start = (f32[2,16,128]{2,1,0:T(8,128)S(1)}, f32[2,16,128]{2,1,0:T(8,128)S(1)}, u32[]{:S(2)}, u32[]{:S(2)}) collective-permute-start(f32[2,16,128]{2,1,0:T(8,128)S(1)} %get-tuple-element.86), channel_id=1, source_target_pairs={{0,8},{8,16},{16,24},{1,9},{9,17},{17,25},{2,10},{10,18},{18,26},{... | collective-permute-start | bytes 49160 | tf_op jit(solution)/shard_map/ppermute | solution.py:17
  14.3 5.1 %collective-permute-start.2 = (f32[20,2,128]{2,1,0:T(2,128)S(1)}, f32[20,2,128]{2,1,0:T(2,128)S(1)}, u32[]{:S(2)}, u32[]{:S(2)}) collective-permute-start(f32[20,2,128]{2,1,0:T(2,128)S(1)} %get-tuple-element.81), channel_id=1, source_target_pairs={{0,1},{1,2},{2,3},{3,4},{4,5},{5,6},{6,7},{8,9},{9,10},{10,11},{11... | collective-permute-start | bytes 61448 | tf_op jit(solution)/shard_map/ppermute | solution.py:17
  19.5 1.9 collective-permute-start.3
  23.1 1.5 collective-permute-done.3
  26.2 1.3 collective-permute-start.5
  27.5 4.6 %collective-permute-start.4 = (f32[3,1,16,128]{3,2,1,0:T(8,128)S(1)}, f32[3,1,16,128]{3,2,1,0:T(8,128)S(1)}, u32[]{:S(2)}, u32[]{:S(2)}) collective-permute-start(f32[3,1,16,128]{3,2,1,0:T(8,128)S(1)} %get-tuple-element.67), channel_id=1, source_target_pairs={{0,8},{8,16},{16,24},{1,9},{9,17},{17,25},{2,10},{10,18},{18,26},{... | collective-permute-start | bytes 73736 | tf_op jit(solution)/shard_map/ppermute | solution.py:17
  33.2 1.9 collective-permute-start.7
  35.1 3.6 %collective-permute-start.6 = (f32[3,18,1,128]{3,2,1,0:T(1,128)S(1)}, f32[3,18,1,128]{3,2,1,0:T(1,128)S(1)}, u32[]{:S(2)}, u32[]{:S(2)}) collective-permute-start(f32[3,18,1,128]{3,2,1,0:T(1,128)S(1)} %get-tuple-element.47), channel_id=1, source_target_pairs={{0,1},{1,2},{2,3},{3,4},{4,5},{5,6},{6,7},{8,9},{9,10},{10,11},{11... | collective-permute-start | bytes 82952 | tf_op jit(solution)/shard_map/ppermute | solution.py:17
  40.1 1.3 collective-permute-start.9
  41.4 5.4 %collective-permute-start.8 = (f32[3,1,16,128]{3,2,1,0:T(8,128)S(1)}, f32[3,1,16,128]{3,2,1,0:T(8,128)S(1)}, u32[]{:S(2)}, u32[]{:S(2)}) collective-permute-start(f32[3,1,16,128]{3,2,1,0:T(8,128)S(1)} %get-tuple-element.65), channel_id=1, source_target_pairs={{0,8},{8,16},{16,24},{1,9},{9,17},{17,25},{2,10},{10,18},{18,26},{... | collective-permute-start | bytes 73736 | tf_op jit(solution)/shard_map/ppermute | solution.py:17
  46.8 9.8 %reshape.152 = f32[8,2,8,2,64,2]{5,4,3,2,1,0:T(8,128)} reshape(f32[16,16,128]{2,1,0:T(8,128)S(1)} %get-tuple-element.73) | data formatting | bytes 262144 | tf_op jit(solution)/shard_map/reshape | solution.py:53
  56.6 9.7 %reshape.148 = f32[8,2,8,2,64,2]{5,4,3,2,1,0:T(8,128)} reshape(f32[16,16,128]{2,1,0:T(8,128)S(1)} %get-tuple-element.75) | data formatting | bytes 262144 | tf_op jit(solution)/shard_map/reshape | solution.py:53
  66.3 9.8 %reshape.150 = f32[8,2,8,2,64,2]{5,4,3,2,1,0:T(8,128)} reshape(f32[16,16,128]{2,1,0:T(8,128)S(1)} %get-tuple-element.77) | data formatting | bytes 262144 | tf_op jit(solution)/shard_map/reshape | solution.py:53
  76.1 1.9 collective-permute-start.11
  78.1 4.5 %collective-permute-start.10 = (f32[3,18,1,128]{3,2,1,0:T(1,128)S(1)}, f32[3,18,1,128]{3,2,1,0:T(1,128)S(1)}, u32[]{:S(2)}, u32[]{:S(2)}) collective-permute-start(f32[3,18,1,128]{3,2,1,0:T(1,128)S(1)} %get-tuple-element.45), channel_id=1, source_target_pairs={{0,1},{1,2},{2,3},{3,4},{4,5},{5,6},{6,7},{8,9},{9,10},{10,11},{11... | collective-permute-start | bytes 82952 | tf_op jit(solution)/shard_map/ppermute | solution.py:17
  82.6 10.1 %multiply_reduce_fusion = (f32[8,8,64]{2,1,0:T(8,128)S(1)}, f32[8,8,64]{2,1,0:T(8,128)S(1)}, f32[8,8,64]{2,1,0:T(8,128)S(1)}) fusion(f32[8,2,8,2,64,2]{5,4,3,2,1,0:T(8,128)} %reshape.152, f32[2]{0:T(128)S(1)} %copy-done.5, f32[8,2,8,2,64,2]{5,4,3,2,1,0:T(8,128)} %reshape.148, f32[8,2,8,2,64,2]{5,4,3,2,1,0:T(8,128)} %reshape.150), kind=kLoop, calls=%fused_computation.6 | loop fusion | flops 184320 | bytes 442376 | tf_op jit(solution)/shard_map/reduce_sum | solution.py:57
  92.7 9.8 %reshape.153 = f32[8,2,8,2,64,2]{5,4,3,2,1,0:T(8,128)} reshape(f32[16,16,128]{2,1,0:T(8,128)S(1)} %get-tuple-element.74) | data formatting | bytes 262144 | tf_op jit(solution)/shard_map/reshape | solution.py:53
  102.5 9.7 %reshape.151 = f32[8,2,8,2,64,2]{5,4,3,2,1,0:T(8,128)} reshape(f32[16,16,128]{2,1,0:T(8,128)S(1)} %get-tuple-element.78) | data formatting | bytes 262144 | tf_op jit(solution)/shard_map/reshape | solution.py:53
  112.6 1.3 collective-permute-start.13
  113.9 5.3 %collective-permute-start.12 = (f32[3,1,16,128]{3,2,1,0:T(8,128)S(1)}, f32[3,1,16,128]{3,2,1,0:T(8,128)S(1)}, u32[]{:S(2)}, u32[]{:S(2)}) collective-permute-start(f32[3,1,16,128]{3,2,1,0:T(8,128)S(1)} %get-tuple-element.63), channel_id=1, source_target_pairs={{0,8},{8,16},{16,24},{1,9},{9,17},{17,25},{2,10},{10,18},{18,26},{... | collective-permute-start | bytes 73736 | tf_op jit(solution)/shard_map/ppermute | solution.py:17
  119.2 7.4 %fusion = (f32[8,8,64]{2,1,0:T(8,128)S(1)}, f32[8,8,64]{2,1,0:T(8,128)S(1)}) fusion(f32[8,2,8,2,64,2]{5,4,3,2,1,0:T(8,128)} %reshape.153, f32[8,2,8,2,64,2]{5,4,3,2,1,0:T(8,128)} %reshape.151), kind=kLoop, calls=%fused_computation.1 | loop fusion | flops 122880 | bytes 294912 | tf_op jit(solution)/shard_map/reduce_sum | solution.py:57
  126.6 9.8 %reshape.149 = f32[8,2,8,2,64,2]{5,4,3,2,1,0:T(8,128)} reshape(f32[16,16,128]{2,1,0:T(8,128)S(1)} %get-tuple-element.76) | data formatting | bytes 262144 | tf_op jit(solution)/shard_map/reshape | solution.py:53
  136.4 1.9 collective-permute-start.15
  138.3 3.6 %collective-permute-start.14 = (f32[3,18,1,128]{3,2,1,0:T(1,128)S(1)}, f32[3,18,1,128]{3,2,1,0:T(1,128)S(1)}, u32[]{:S(2)}, u32[]{:S(2)}) collective-permute-start(f32[3,18,1,128]{3,2,1,0:T(1,128)S(1)} %get-tuple-element.43), channel_id=1, source_target_pairs={{0,1},{1,2},{2,3},{3,4},{4,5},{5,6},{6,7},{8,9},{9,10},{10,11},{11... | collective-permute-start | bytes 82952 | tf_op jit(solution)/shard_map/ppermute | solution.py:17
  142.0 4.1 %fusion.2 = f32[8,8,64]{2,1,0:T(8,128)S(1)} fusion(f32[8,2,8,2,64,2]{5,4,3,2,1,0:T(8,128)} %reshape.149), kind=kLoop, calls=%fused_computation.5 | loop fusion | flops 61440 | bytes 147456 | tf_op jit(solution)/shard_map/reduce_sum | solution.py:57
  146.5 1.3 collective-permute-start.17
  147.8 4.9 %collective-permute-start.16 = (f32[3,1,16,128]{3,2,1,0:T(8,128)S(1)}, f32[3,1,16,128]{3,2,1,0:T(8,128)S(1)}, u32[]{:S(2)}, u32[]{:S(2)}) collective-permute-start(f32[3,1,16,128]{3,2,1,0:T(8,128)S(1)} %get-tuple-element.61), channel_id=1, source_target_pairs={{0,8},{8,16},{16,24},{1,9},{9,17},{17,25},{2,10},{10,18},{18,26},{... | collective-permute-start | bytes 73736 | tf_op jit(solution)/shard_map/ppermute | solution.py:17
  153.7 1.9 collective-permute-start.19
  155.6 3.6 %collective-permute-start.18 = (f32[3,18,1,128]{3,2,1,0:T(1,128)S(1)}, f32[3,18,1,128]{3,2,1,0:T(1,128)S(1)}, u32[]{:S(2)}, u32[]{:S(2)}) collective-permute-start(f32[3,18,1,128]{3,2,1,0:T(1,128)S(1)} %get-tuple-element.41), channel_id=1, source_target_pairs={{0,1},{1,2},{2,3},{3,4},{4,5},{5,6},{6,7},{8,9},{9,10},{10,11},{11... | collective-permute-start | bytes 82952 | tf_op jit(solution)/shard_map/ppermute | solution.py:17
  160.6 26.5 %reshape.147 = f32[3,8,2,8,2,64,2]{6,5,4,3,2,1,0:T(8,128)} reshape(f32[3,16,16,128]{3,2,1,0:T(8,128)S(1)} %fusion.25) | data formatting | bytes 786432 | tf_op jit(solution)/shard_map/reshape | solution.py:74
  187.1 9.4 %reduce_sum.63 = f32[3,8,8,64]{3,2,1,0:T(8,128)S(1)} reduce(f32[3,8,2,8,2,64,2]{6,5,4,3,2,1,0:T(8,128)} %reshape.147, f32[]{:T(128)} %constant.8.clone.1), dimensions={2,4,6}, to_apply=%region_0.1 | reduce | flops 86016 | bytes 442372 | tf_op jit(solution)/shard_map/reduce_sum | solution.py:77
  196.6 1.3 collective-permute-start.21
  197.9 4.9 %collective-permute-start.20 = (f32[3,1,8,64]{3,2,1,0:T(8,128)S(1)}, f32[3,1,8,64]{3,2,1,0:T(8,128)S(1)}, u32[]{:S(2)}, u32[]{:S(2)}) collective-permute-start(f32[3,1,8,64]{3,2,1,0:T(8,128)S(1)} %get-tuple-element.98), channel_id=1, source_target_pairs={{0,8},{8,16},{16,24},{1,9},{9,17},{17,25},{2,10},{10,18},{18,26},{... | collective-permute-start | bytes 18440 | tf_op jit(solution)/shard_map/ppermute | solution.py:17
  203.6 1.9 collective-permute-start.23
  205.6 5.1 %collective-permute-start.22 = (f32[3,10,1,64]{3,2,1,0:T(1,128)S(1)}, f32[3,10,1,64]{3,2,1,0:T(1,128)S(1)}, u32[]{:S(2)}, u32[]{:S(2)}) collective-permute-start(f32[3,10,1,64]{3,2,1,0:T(1,128)S(1)} %get-tuple-element.92), channel_id=1, source_target_pairs={{0,1},{1,2},{2,3},{3,4},{4,5},{5,6},{6,7},{8,9},{9,10},{10,11},{11... | collective-permute-start | bytes 23048 | tf_op jit(solution)/shard_map/ppermute | solution.py:17
  211.6 1.3 collective-permute-start.25
  212.9 5.2 %collective-permute-start.24 = (f32[3,1,8,64]{3,2,1,0:T(8,128)S(1)}, f32[3,1,8,64]{3,2,1,0:T(8,128)S(1)}, u32[]{:S(2)}, u32[]{:S(2)}) collective-permute-start(f32[3,1,8,64]{3,2,1,0:T(8,128)S(1)} %get-tuple-element.96), channel_id=1, source_target_pairs={{0,8},{8,16},{16,24},{1,9},{9,17},{17,25},{2,10},{10,18},{18,26},{... | collective-permute-start | bytes 18440 | tf_op jit(solution)/shard_map/ppermute | solution.py:17
  218.9 1.9 collective-permute-start.27
  220.9 5.1 %collective-permute-start.26 = (f32[3,10,1,64]{3,2,1,0:T(1,128)S(1)}, f32[3,10,1,64]{3,2,1,0:T(1,128)S(1)}, u32[]{:S(2)}, u32[]{:S(2)}) collective-permute-start(f32[3,10,1,64]{3,2,1,0:T(1,128)S(1)} %get-tuple-element.90), channel_id=1, source_target_pairs={{0,1},{1,2},{2,3},{3,4},{4,5},{5,6},{6,7},{8,9},{9,10},{10,11},{11... | collective-permute-start | bytes 23048 | tf_op jit(solution)/shard_map/ppermute | solution.py:17
  226.9 1.3 collective-permute-start.29
  228.2 5.4 %collective-permute-start.28 = (f32[3,1,8,64]{3,2,1,0:T(8,128)S(1)}, f32[3,1,8,64]{3,2,1,0:T(8,128)S(1)}, u32[]{:S(2)}, u32[]{:S(2)}) collective-permute-start(f32[3,1,8,64]{3,2,1,0:T(8,128)S(1)} %get-tuple-element.94), channel_id=1, source_target_pairs={{0,8},{8,16},{16,24},{1,9},{9,17},{17,25},{2,10},{10,18},{18,26},{... | collective-permute-start | bytes 18440 | tf_op jit(solution)/shard_map/ppermute | solution.py:17
  234.5 1.9 collective-permute-start.31
  236.4 5.1 %collective-permute-start.30 = (f32[3,10,1,64]{3,2,1,0:T(1,128)S(1)}, f32[3,10,1,64]{3,2,1,0:T(1,128)S(1)}, u32[]{:S(2)}, u32[]{:S(2)}) collective-permute-start(f32[3,10,1,64]{3,2,1,0:T(1,128)S(1)} %get-tuple-element.88), channel_id=1, source_target_pairs={{0,1},{1,2},{2,3},{3,4},{4,5},{5,6},{6,7},{8,9},{9,10},{10,11},{11... | collective-permute-start | bytes 23048 | tf_op jit(solution)/shard_map/ppermute | solution.py:17
  243.4 1.9 broadcast_in_dim.44
  245.3 2.3 copy.476
  247.6 1.3 collective-permute-start.33
  248.9 5.4 %collective-permute-start.32 = (f32[3,1,16,128]{3,2,1,0:T(8,128)S(1)}, f32[3,1,16,128]{3,2,1,0:T(8,128)S(1)}, u32[]{:S(2)}, u32[]{:S(2)}) collective-permute-start(f32[3,1,16,128]{3,2,1,0:T(8,128)S(1)} %get-tuple-element.59), channel_id=1, source_target_pairs={{0,8},{8,16},{16,24},{1,9},{9,17},{17,25},{2,10},{10,18},{18,26},{... | collective-permute-start | bytes 73736 | tf_op jit(solution)/shard_map/ppermute | solution.py:17
  255.3 1.9 collective-permute-start.35
  257.3 5.1 %collective-permute-start.34 = (f32[3,18,1,128]{3,2,1,0:T(1,128)S(1)}, f32[3,18,1,128]{3,2,1,0:T(1,128)S(1)}, u32[]{:S(2)}, u32[]{:S(2)}) collective-permute-start(f32[3,18,1,128]{3,2,1,0:T(1,128)S(1)} %get-tuple-element.39), channel_id=1, source_target_pairs={{0,1},{1,2},{2,3},{3,4},{4,5},{5,6},{6,7},{8,9},{9,10},{10,11},{11... | collective-permute-start | bytes 82952 | tf_op jit(solution)/shard_map/ppermute | solution.py:17
  264.9 5.4 %collective-permute-start.36 = (f32[3,1,16,128]{3,2,1,0:T(8,128)S(1)}, f32[3,1,16,128]{3,2,1,0:T(8,128)S(1)}, u32[]{:S(2)}, u32[]{:S(2)}) collective-permute-start(f32[3,1,16,128]{3,2,1,0:T(8,128)S(1)} %get-tuple-element.57), channel_id=1, source_target_pairs={{0,8},{8,16},{16,24},{1,9},{9,17},{17,25},{2,10},{10,18},{18,26},{... | collective-permute-start | bytes 73736 | tf_op jit(solution)/shard_map/ppermute | solution.py:17
  271.4 1.9 collective-permute-start.39
  273.3 5.1 %collective-permute-start.38 = (f32[3,18,1,128]{3,2,1,0:T(1,128)S(1)}, f32[3,18,1,128]{3,2,1,0:T(1,128)S(1)}, u32[]{:S(2)}, u32[]{:S(2)}) collective-permute-start(f32[3,18,1,128]{3,2,1,0:T(1,128)S(1)} %get-tuple-element.37), channel_id=1, source_target_pairs={{0,1},{1,2},{2,3},{3,4},{4,5},{5,6},{6,7},{8,9},{9,10},{10,11},{11... | collective-permute-start | bytes 82952 | tf_op jit(solution)/shard_map/ppermute | solution.py:17
  281.0 5.5 %collective-permute-start.40 = (f32[3,1,16,128]{3,2,1,0:T(8,128)S(1)}, f32[3,1,16,128]{3,2,1,0:T(8,128)S(1)}, u32[]{:S(2)}, u32[]{:S(2)}) collective-permute-start(f32[3,1,16,128]{3,2,1,0:T(8,128)S(1)} %get-tuple-element.55), channel_id=1, source_target_pairs={{0,8},{8,16},{16,24},{1,9},{9,17},{17,25},{2,10},{10,18},{18,26},{... | collective-permute-start | bytes 73736 | tf_op jit(solution)/shard_map/ppermute | solution.py:17
  287.5 1.9 collective-permute-start.43
  289.4 5.1 %collective-permute-start.42 = (f32[3,18,1,128]{3,2,1,0:T(1,128)S(1)}, f32[3,18,1,128]{3,2,1,0:T(1,128)S(1)}, u32[]{:S(2)}, u32[]{:S(2)}) collective-permute-start(f32[3,18,1,128]{3,2,1,0:T(1,128)S(1)} %get-tuple-element.35), channel_id=1, source_target_pairs={{0,1},{1,2},{2,3},{3,4},{4,5},{5,6},{6,7},{8,9},{9,10},{10,11},{11... | collective-permute-start | bytes 82952 | tf_op jit(solution)/shard_map/ppermute | solution.py:17
  297.2 5.5 %collective-permute-start.44 = (f32[3,1,16,128]{3,2,1,0:T(8,128)S(1)}, f32[3,1,16,128]{3,2,1,0:T(8,128)S(1)}, u32[]{:S(2)}, u32[]{:S(2)}) collective-permute-start(f32[3,1,16,128]{3,2,1,0:T(8,128)S(1)} %get-tuple-element.53), channel_id=1, source_target_pairs={{0,8},{8,16},{16,24},{1,9},{9,17},{17,25},{2,10},{10,18},{18,26},{... | collective-permute-start | bytes 73736 | tf_op jit(solution)/shard_map/ppermute | solution.py:17
  303.6 1.9 collective-permute-start.47
  305.5 5.1 %collective-permute-start.46 = (f32[3,18,1,128]{3,2,1,0:T(1,128)S(1)}, f32[3,18,1,128]{3,2,1,0:T(1,128)S(1)}, u32[]{:S(2)}, u32[]{:S(2)}) collective-permute-start(f32[3,18,1,128]{3,2,1,0:T(1,128)S(1)} %get-tuple-element.33), channel_id=1, source_target_pairs={{0,1},{1,2},{2,3},{3,4},{4,5},{5,6},{6,7},{8,9},{9,10},{10,11},{11... | collective-permute-start | bytes 82952 | tf_op jit(solution)/shard_map/ppermute | solution.py:17
  313.3 5.5 %collective-permute-start.48 = (f32[3,1,16,128]{3,2,1,0:T(8,128)S(1)}, f32[3,1,16,128]{3,2,1,0:T(8,128)S(1)}, u32[]{:S(2)}, u32[]{:S(2)}) collective-permute-start(f32[3,1,16,128]{3,2,1,0:T(8,128)S(1)} %get-tuple-element.51), channel_id=1, source_target_pairs={{0,8},{8,16},{16,24},{1,9},{9,17},{17,25},{2,10},{10,18},{18,26},{... | collective-permute-start | bytes 73736 | tf_op jit(solution)/shard_map/ppermute | solution.py:17
  319.7 1.9 collective-permute-start.51
  321.7 5.1 %collective-permute-start.50 = (f32[3,18,1,128]{3,2,1,0:T(1,128)S(1)}, f32[3,18,1,128]{3,2,1,0:T(1,128)S(1)}, u32[]{:S(2)}, u32[]{:S(2)}) collective-permute-start(f32[3,18,1,128]{3,2,1,0:T(1,128)S(1)} %get-tuple-element.31), channel_id=1, source_target_pairs={{0,1},{1,2},{2,3},{3,4},{4,5},{5,6},{6,7},{8,9},{9,10},{10,11},{11... | collective-permute-start | bytes 82952 | tf_op jit(solution)/shard_map/ppermute | solution.py:17
  (119 shorter events, 31.5 us)
Async XLA Ops:
  0.0 39.7 %copy-start = (f32[3,16,16,128]{3,2,1,0:T(8,128)S(1)}, f32[3,16,16,128]{3,2,1,0:T(8,128)}, u32[]{:S(2)}) copy-start(f32[3,16,16,128]{3,2,1,0:T(8,128)} %param.11) | copy-start | bytes 1179652
  7.6 5.9 %collective-permute-start.1 = (f32[2,16,128]{2,1,0:T(8,128)S(1)}, f32[2,16,128]{2,1,0:T(8,128)S(1)}, u32[]{:S(2)}, u32[]{:S(2)}) collective-permute-start(f32[2,16,128]{2,1,0:T(8,128)S(1)} %get-tuple-element.87), channel_id=1, source_target_pairs={{8,0},{16,8},{24,16},{9,1},{17,9},{25,17},{10,2},{18,10},{26,18},{... | collective-permute-start | bytes 49160 | tf_op jit(solution)/shard_map/ppermute | solution.py:18
  8.9 5.4 %collective-permute-start = (f32[2,16,128]{2,1,0:T(8,128)S(1)}, f32[2,16,128]{2,1,0:T(8,128)S(1)}, u32[]{:S(2)}, u32[]{:S(2)}) collective-permute-start(f32[2,16,128]{2,1,0:T(8,128)S(1)} %get-tuple-element.86), channel_id=1, source_target_pairs={{0,8},{8,16},{16,24},{1,9},{9,17},{17,25},{2,10},{10,18},{18,26},{... | collective-permute-start | bytes 49160 | tf_op jit(solution)/shard_map/ppermute | solution.py:17
  14.3 8.7 %collective-permute-start.2 = (f32[20,2,128]{2,1,0:T(2,128)S(1)}, f32[20,2,128]{2,1,0:T(2,128)S(1)}, u32[]{:S(2)}, u32[]{:S(2)}) collective-permute-start(f32[20,2,128]{2,1,0:T(2,128)S(1)} %get-tuple-element.81), channel_id=1, source_target_pairs={{0,1},{1,2},{2,3},{3,4},{4,5},{5,6},{6,7},{8,9},{9,10},{10,11},{11... | collective-permute-start | bytes 61448 | tf_op jit(solution)/shard_map/ppermute | solution.py:17
  19.5 5.1 %collective-permute-start.3 = (f32[20,2,128]{2,1,0:T(2,128)S(1)}, f32[20,2,128]{2,1,0:T(2,128)S(1)}, u32[]{:S(2)}, u32[]{:S(2)}) collective-permute-start(f32[20,2,128]{2,1,0:T(2,128)S(1)} %get-tuple-element.82), channel_id=1, source_target_pairs={{1,0},{2,1},{3,2},{4,3},{5,4},{6,5},{7,6},{9,8},{10,9},{11,10},{12... | collective-permute-start | bytes 61448 | tf_op jit(solution)/shard_map/ppermute | solution.py:18
  25.1 14.6 %copy-start.3 = (f32[16,16,128]{2,1,0:T(8,128)}, f32[16,16,128]{2,1,0:T(8,128)S(1)}, u32[]{:S(2)}) copy-start(f32[16,16,128]{2,1,0:T(8,128)S(1)} %get-tuple-element.85) | copy-start | bytes 393220
  25.1 41.2 %copy-start.1 = (f32[16,16,128]{2,1,0:T(8,128)}, f32[16,16,128]{2,1,0:T(8,128)S(1)}, u32[]{:S(2)}) copy-start(f32[16,16,128]{2,1,0:T(8,128)S(1)} %get-tuple-element.84) | copy-start | bytes 393220
  26.2 6.0 %collective-permute-start.5 = (f32[3,1,16,128]{3,2,1,0:T(8,128)S(1)}, f32[3,1,16,128]{3,2,1,0:T(8,128)S(1)}, u32[]{:S(2)}, u32[]{:S(2)}) collective-permute-start(f32[3,1,16,128]{3,2,1,0:T(8,128)S(1)} %get-tuple-element.68), channel_id=1, source_target_pairs={{8,0},{16,8},{24,16},{9,1},{17,9},{25,17},{10,2},{18,10},{26,18},{... | collective-permute-start | bytes 73736 | tf_op jit(solution)/shard_map/ppermute | solution.py:18
  27.5 5.6 %collective-permute-start.4 = (f32[3,1,16,128]{3,2,1,0:T(8,128)S(1)}, f32[3,1,16,128]{3,2,1,0:T(8,128)S(1)}, u32[]{:S(2)}, u32[]{:S(2)}) collective-permute-start(f32[3,1,16,128]{3,2,1,0:T(8,128)S(1)} %get-tuple-element.67), channel_id=1, source_target_pairs={{0,8},{8,16},{16,24},{1,9},{9,17},{17,25},{2,10},{10,18},{18,26},{... | collective-permute-start | bytes 73736 | tf_op jit(solution)/shard_map/ppermute | solution.py:17
  33.2 5.6 %collective-permute-start.7 = (f32[3,18,1,128]{3,2,1,0:T(1,128)S(1)}, f32[3,18,1,128]{3,2,1,0:T(1,128)S(1)}, u32[]{:S(2)}, u32[]{:S(2)}) collective-permute-start(f32[3,18,1,128]{3,2,1,0:T(1,128)S(1)} %get-tuple-element.48), channel_id=1, source_target_pairs={{1,0},{2,1},{3,2},{4,3},{5,4},{6,5},{7,6},{9,8},{10,9},{11,10},{12... | collective-permute-start | bytes 82952 | tf_op jit(solution)/shard_map/ppermute | solution.py:18
  35.1 4.6 %collective-permute-start.6 = (f32[3,18,1,128]{3,2,1,0:T(1,128)S(1)}, f32[3,18,1,128]{3,2,1,0:T(1,128)S(1)}, u32[]{:S(2)}, u32[]{:S(2)}) collective-permute-start(f32[3,18,1,128]{3,2,1,0:T(1,128)S(1)} %get-tuple-element.47), channel_id=1, source_target_pairs={{0,1},{1,2},{2,3},{3,4},{4,5},{5,6},{6,7},{8,9},{9,10},{10,11},{11... | collective-permute-start | bytes 82952 | tf_op jit(solution)/shard_map/ppermute | solution.py:17
  40.1 36.0 %collective-permute-start.9 = (f32[3,1,16,128]{3,2,1,0:T(8,128)S(1)}, f32[3,1,16,128]{3,2,1,0:T(8,128)S(1)}, u32[]{:S(2)}, u32[]{:S(2)}) collective-permute-start(f32[3,1,16,128]{3,2,1,0:T(8,128)S(1)} %get-tuple-element.66), channel_id=1, source_target_pairs={{8,0},{16,8},{24,16},{9,1},{17,9},{25,17},{10,2},{18,10},{26,18},{... | collective-permute-start | bytes 73736 | tf_op jit(solution)/shard_map/ppermute | solution.py:18
  41.4 34.7 %collective-permute-start.8 = (f32[3,1,16,128]{3,2,1,0:T(8,128)S(1)}, f32[3,1,16,128]{3,2,1,0:T(8,128)S(1)}, u32[]{:S(2)}, u32[]{:S(2)}) collective-permute-start(f32[3,1,16,128]{3,2,1,0:T(8,128)S(1)} %get-tuple-element.65), channel_id=1, source_target_pairs={{0,8},{8,16},{16,24},{1,9},{9,17},{17,25},{2,10},{10,18},{18,26},{... | collective-permute-start | bytes 73736 | tf_op jit(solution)/shard_map/ppermute | solution.py:17
  56.6 25.9 %copy-start.5 = (f32[2]{0:T(128)S(1)}, f32[2]{0:T(128)}, u32[]{:S(2)}) copy-start(f32[2]{0:T(128)} %constant.15.clone) | copy-start | bytes 28
  76.1 36.0 %collective-permute-start.11 = (f32[3,18,1,128]{3,2,1,0:T(1,128)S(1)}, f32[3,18,1,128]{3,2,1,0:T(1,128)S(1)}, u32[]{:S(2)}, u32[]{:S(2)}) collective-permute-start(f32[3,18,1,128]{3,2,1,0:T(1,128)S(1)} %get-tuple-element.46), channel_id=1, source_target_pairs={{1,0},{2,1},{3,2},{4,3},{5,4},{6,5},{7,6},{9,8},{10,9},{11,10},{12... | collective-permute-start | bytes 82952 | tf_op jit(solution)/shard_map/ppermute | solution.py:18
  78.1 34.1 %collective-permute-start.10 = (f32[3,18,1,128]{3,2,1,0:T(1,128)S(1)}, f32[3,18,1,128]{3,2,1,0:T(1,128)S(1)}, u32[]{:S(2)}, u32[]{:S(2)}) collective-permute-start(f32[3,18,1,128]{3,2,1,0:T(1,128)S(1)} %get-tuple-element.45), channel_id=1, source_target_pairs={{0,1},{1,2},{2,3},{3,4},{4,5},{5,6},{6,7},{8,9},{9,10},{10,11},{11... | collective-permute-start | bytes 82952 | tf_op jit(solution)/shard_map/ppermute | solution.py:17
  112.6 23.8 %collective-permute-start.13 = (f32[3,1,16,128]{3,2,1,0:T(8,128)S(1)}, f32[3,1,16,128]{3,2,1,0:T(8,128)S(1)}, u32[]{:S(2)}, u32[]{:S(2)}) collective-permute-start(f32[3,1,16,128]{3,2,1,0:T(8,128)S(1)} %get-tuple-element.64), channel_id=1, source_target_pairs={{8,0},{16,8},{24,16},{9,1},{17,9},{25,17},{10,2},{18,10},{26,18},{... | collective-permute-start | bytes 73736 | tf_op jit(solution)/shard_map/ppermute | solution.py:18
  113.9 22.5 %collective-permute-start.12 = (f32[3,1,16,128]{3,2,1,0:T(8,128)S(1)}, f32[3,1,16,128]{3,2,1,0:T(8,128)S(1)}, u32[]{:S(2)}, u32[]{:S(2)}) collective-permute-start(f32[3,1,16,128]{3,2,1,0:T(8,128)S(1)} %get-tuple-element.63), channel_id=1, source_target_pairs={{0,8},{8,16},{16,24},{1,9},{9,17},{17,25},{2,10},{10,18},{18,26},{... | collective-permute-start | bytes 73736 | tf_op jit(solution)/shard_map/ppermute | solution.py:17
  136.4 9.7 %collective-permute-start.15 = (f32[3,18,1,128]{3,2,1,0:T(1,128)S(1)}, f32[3,18,1,128]{3,2,1,0:T(1,128)S(1)}, u32[]{:S(2)}, u32[]{:S(2)}) collective-permute-start(f32[3,18,1,128]{3,2,1,0:T(1,128)S(1)} %get-tuple-element.44), channel_id=1, source_target_pairs={{1,0},{2,1},{3,2},{4,3},{5,4},{6,5},{7,6},{9,8},{10,9},{11,10},{12... | collective-permute-start | bytes 82952 | tf_op jit(solution)/shard_map/ppermute | solution.py:18
  138.3 7.8 %collective-permute-start.14 = (f32[3,18,1,128]{3,2,1,0:T(1,128)S(1)}, f32[3,18,1,128]{3,2,1,0:T(1,128)S(1)}, u32[]{:S(2)}, u32[]{:S(2)}) collective-permute-start(f32[3,18,1,128]{3,2,1,0:T(1,128)S(1)} %get-tuple-element.43), channel_id=1, source_target_pairs={{0,1},{1,2},{2,3},{3,4},{4,5},{5,6},{6,7},{8,9},{9,10},{10,11},{11... | collective-permute-start | bytes 82952 | tf_op jit(solution)/shard_map/ppermute | solution.py:17
  146.5 6.2 %collective-permute-start.17 = (f32[3,1,16,128]{3,2,1,0:T(8,128)S(1)}, f32[3,1,16,128]{3,2,1,0:T(8,128)S(1)}, u32[]{:S(2)}, u32[]{:S(2)}) collective-permute-start(f32[3,1,16,128]{3,2,1,0:T(8,128)S(1)} %get-tuple-element.62), channel_id=1, source_target_pairs={{8,0},{16,8},{24,16},{9,1},{17,9},{25,17},{10,2},{18,10},{26,18},{... | collective-permute-start | bytes 73736 | tf_op jit(solution)/shard_map/ppermute | solution.py:18
  147.8 5.8 %collective-permute-start.16 = (f32[3,1,16,128]{3,2,1,0:T(8,128)S(1)}, f32[3,1,16,128]{3,2,1,0:T(8,128)S(1)}, u32[]{:S(2)}, u32[]{:S(2)}) collective-permute-start(f32[3,1,16,128]{3,2,1,0:T(8,128)S(1)} %get-tuple-element.61), channel_id=1, source_target_pairs={{0,8},{8,16},{16,24},{1,9},{9,17},{17,25},{2,10},{10,18},{18,26},{... | collective-permute-start | bytes 73736 | tf_op jit(solution)/shard_map/ppermute | solution.py:17
  153.7 5.6 %collective-permute-start.19 = (f32[3,18,1,128]{3,2,1,0:T(1,128)S(1)}, f32[3,18,1,128]{3,2,1,0:T(1,128)S(1)}, u32[]{:S(2)}, u32[]{:S(2)}) collective-permute-start(f32[3,18,1,128]{3,2,1,0:T(1,128)S(1)} %get-tuple-element.42), channel_id=1, source_target_pairs={{1,0},{2,1},{3,2},{4,3},{5,4},{6,5},{7,6},{9,8},{10,9},{11,10},{12... | collective-permute-start | bytes 82952 | tf_op jit(solution)/shard_map/ppermute | solution.py:18
  155.6 4.6 %collective-permute-start.18 = (f32[3,18,1,128]{3,2,1,0:T(1,128)S(1)}, f32[3,18,1,128]{3,2,1,0:T(1,128)S(1)}, u32[]{:S(2)}, u32[]{:S(2)}) collective-permute-start(f32[3,18,1,128]{3,2,1,0:T(1,128)S(1)} %get-tuple-element.41), channel_id=1, source_target_pairs={{0,1},{1,2},{2,3},{3,4},{4,5},{5,6},{6,7},{8,9},{9,10},{10,11},{11... | collective-permute-start | bytes 82952 | tf_op jit(solution)/shard_map/ppermute | solution.py:17
  196.6 6.2 %collective-permute-start.21 = (f32[3,1,8,64]{3,2,1,0:T(8,128)S(1)}, f32[3,1,8,64]{3,2,1,0:T(8,128)S(1)}, u32[]{:S(2)}, u32[]{:S(2)}) collective-permute-start(f32[3,1,8,64]{3,2,1,0:T(8,128)S(1)} %get-tuple-element.99), channel_id=1, source_target_pairs={{8,0},{16,8},{24,16},{9,1},{17,9},{25,17},{10,2},{18,10},{26,18},{... | collective-permute-start | bytes 18440 | tf_op jit(solution)/shard_map/ppermute | solution.py:18
  197.9 5.7 %collective-permute-start.20 = (f32[3,1,8,64]{3,2,1,0:T(8,128)S(1)}, f32[3,1,8,64]{3,2,1,0:T(8,128)S(1)}, u32[]{:S(2)}, u32[]{:S(2)}) collective-permute-start(f32[3,1,8,64]{3,2,1,0:T(8,128)S(1)} %get-tuple-element.98), channel_id=1, source_target_pairs={{0,8},{8,16},{16,24},{1,9},{9,17},{17,25},{2,10},{10,18},{18,26},{... | collective-permute-start | bytes 18440 | tf_op jit(solution)/shard_map/ppermute | solution.py:17
  203.6 7.0 %collective-permute-start.23 = (f32[3,10,1,64]{3,2,1,0:T(1,128)S(1)}, f32[3,10,1,64]{3,2,1,0:T(1,128)S(1)}, u32[]{:S(2)}, u32[]{:S(2)}) collective-permute-start(f32[3,10,1,64]{3,2,1,0:T(1,128)S(1)} %get-tuple-element.93), channel_id=1, source_target_pairs={{1,0},{2,1},{3,2},{4,3},{5,4},{6,5},{7,6},{9,8},{10,9},{11,10},{12... | collective-permute-start | bytes 23048 | tf_op jit(solution)/shard_map/ppermute | solution.py:18
  205.6 5.9 %collective-permute-start.22 = (f32[3,10,1,64]{3,2,1,0:T(1,128)S(1)}, f32[3,10,1,64]{3,2,1,0:T(1,128)S(1)}, u32[]{:S(2)}, u32[]{:S(2)}) collective-permute-start(f32[3,10,1,64]{3,2,1,0:T(1,128)S(1)} %get-tuple-element.92), channel_id=1, source_target_pairs={{0,1},{1,2},{2,3},{3,4},{4,5},{5,6},{6,7},{8,9},{9,10},{10,11},{11... | collective-permute-start | bytes 23048 | tf_op jit(solution)/shard_map/ppermute | solution.py:17
  211.6 6.5 %collective-permute-start.25 = (f32[3,1,8,64]{3,2,1,0:T(8,128)S(1)}, f32[3,1,8,64]{3,2,1,0:T(8,128)S(1)}, u32[]{:S(2)}, u32[]{:S(2)}) collective-permute-start(f32[3,1,8,64]{3,2,1,0:T(8,128)S(1)} %get-tuple-element.97), channel_id=1, source_target_pairs={{8,0},{16,8},{24,16},{9,1},{17,9},{25,17},{10,2},{18,10},{26,18},{... | collective-permute-start | bytes 18440 | tf_op jit(solution)/shard_map/ppermute | solution.py:18
  212.9 6.0 %collective-permute-start.24 = (f32[3,1,8,64]{3,2,1,0:T(8,128)S(1)}, f32[3,1,8,64]{3,2,1,0:T(8,128)S(1)}, u32[]{:S(2)}, u32[]{:S(2)}) collective-permute-start(f32[3,1,8,64]{3,2,1,0:T(8,128)S(1)} %get-tuple-element.96), channel_id=1, source_target_pairs={{0,8},{8,16},{16,24},{1,9},{9,17},{17,25},{2,10},{10,18},{18,26},{... | collective-permute-start | bytes 18440 | tf_op jit(solution)/shard_map/ppermute | solution.py:17
  218.9 7.0 %collective-permute-start.27 = (f32[3,10,1,64]{3,2,1,0:T(1,128)S(1)}, f32[3,10,1,64]{3,2,1,0:T(1,128)S(1)}, u32[]{:S(2)}, u32[]{:S(2)}) collective-permute-start(f32[3,10,1,64]{3,2,1,0:T(1,128)S(1)} %get-tuple-element.91), channel_id=1, source_target_pairs={{1,0},{2,1},{3,2},{4,3},{5,4},{6,5},{7,6},{9,8},{10,9},{11,10},{12... | collective-permute-start | bytes 23048 | tf_op jit(solution)/shard_map/ppermute | solution.py:18
  220.9 5.9 %collective-permute-start.26 = (f32[3,10,1,64]{3,2,1,0:T(1,128)S(1)}, f32[3,10,1,64]{3,2,1,0:T(1,128)S(1)}, u32[]{:S(2)}, u32[]{:S(2)}) collective-permute-start(f32[3,10,1,64]{3,2,1,0:T(1,128)S(1)} %get-tuple-element.90), channel_id=1, source_target_pairs={{0,1},{1,2},{2,3},{3,4},{4,5},{5,6},{6,7},{8,9},{9,10},{10,11},{11... | collective-permute-start | bytes 23048 | tf_op jit(solution)/shard_map/ppermute | solution.py:17
  226.9 6.8 %collective-permute-start.29 = (f32[3,1,8,64]{3,2,1,0:T(8,128)S(1)}, f32[3,1,8,64]{3,2,1,0:T(8,128)S(1)}, u32[]{:S(2)}, u32[]{:S(2)}) collective-permute-start(f32[3,1,8,64]{3,2,1,0:T(8,128)S(1)} %get-tuple-element.95), channel_id=1, source_target_pairs={{8,0},{16,8},{24,16},{9,1},{17,9},{25,17},{10,2},{18,10},{26,18},{... | collective-permute-start | bytes 18440 | tf_op jit(solution)/shard_map/ppermute | solution.py:18
  228.2 6.3 %collective-permute-start.28 = (f32[3,1,8,64]{3,2,1,0:T(8,128)S(1)}, f32[3,1,8,64]{3,2,1,0:T(8,128)S(1)}, u32[]{:S(2)}, u32[]{:S(2)}) collective-permute-start(f32[3,1,8,64]{3,2,1,0:T(8,128)S(1)} %get-tuple-element.94), channel_id=1, source_target_pairs={{0,8},{8,16},{16,24},{1,9},{9,17},{17,25},{2,10},{10,18},{18,26},{... | collective-permute-start | bytes 18440 | tf_op jit(solution)/shard_map/ppermute | solution.py:17
  234.5 7.0 %collective-permute-start.31 = (f32[3,10,1,64]{3,2,1,0:T(1,128)S(1)}, f32[3,10,1,64]{3,2,1,0:T(1,128)S(1)}, u32[]{:S(2)}, u32[]{:S(2)}) collective-permute-start(f32[3,10,1,64]{3,2,1,0:T(1,128)S(1)} %get-tuple-element.89), channel_id=1, source_target_pairs={{1,0},{2,1},{3,2},{4,3},{5,4},{6,5},{7,6},{9,8},{10,9},{11,10},{12... | collective-permute-start | bytes 23048 | tf_op jit(solution)/shard_map/ppermute | solution.py:18
  236.4 5.9 %collective-permute-start.30 = (f32[3,10,1,64]{3,2,1,0:T(1,128)S(1)}, f32[3,10,1,64]{3,2,1,0:T(1,128)S(1)}, u32[]{:S(2)}, u32[]{:S(2)}) collective-permute-start(f32[3,10,1,64]{3,2,1,0:T(1,128)S(1)} %get-tuple-element.88), channel_id=1, source_target_pairs={{0,1},{1,2},{2,3},{3,4},{4,5},{5,6},{6,7},{8,9},{9,10},{10,11},{11... | collective-permute-start | bytes 23048 | tf_op jit(solution)/shard_map/ppermute | solution.py:17
  243.4 19.9 %copy-start.4 = (f32[16,16,128]{2,1,0:T(8,128)S(1)}, f32[16,16,128]{2,1,0:T(8,128)}, u32[]{:S(2)}) copy-start(f32[16,16,128]{2,1,0:T(8,128)} %copy-done.3) | copy-start | bytes 393220
  243.4 36.0 %copy-start.2 = (f32[16,16,128]{2,1,0:T(8,128)S(1)}, f32[16,16,128]{2,1,0:T(8,128)}, u32[]{:S(2)}) copy-start(f32[16,16,128]{2,1,0:T(8,128)} %copy-done.1) | copy-start | bytes 393220
  247.6 6.8 %collective-permute-start.33 = (f32[3,1,16,128]{3,2,1,0:T(8,128)S(1)}, f32[3,1,16,128]{3,2,1,0:T(8,128)S(1)}, u32[]{:S(2)}, u32[]{:S(2)}) collective-permute-start(f32[3,1,16,128]{3,2,1,0:T(8,128)S(1)} %get-tuple-element.60), channel_id=1, source_target_pairs={{8,0},{16,8},{24,16},{9,1},{17,9},{25,17},{10,2},{18,10},{26,18},{... | collective-permute-start | bytes 73736 | tf_op jit(solution)/shard_map/ppermute | solution.py:18
  248.9 6.4 %collective-permute-start.32 = (f32[3,1,16,128]{3,2,1,0:T(8,128)S(1)}, f32[3,1,16,128]{3,2,1,0:T(8,128)S(1)}, u32[]{:S(2)}, u32[]{:S(2)}) collective-permute-start(f32[3,1,16,128]{3,2,1,0:T(8,128)S(1)} %get-tuple-element.59), channel_id=1, source_target_pairs={{0,8},{8,16},{16,24},{1,9},{9,17},{17,25},{2,10},{10,18},{18,26},{... | collective-permute-start | bytes 73736 | tf_op jit(solution)/shard_map/ppermute | solution.py:17
  255.3 7.0 %collective-permute-start.35 = (f32[3,18,1,128]{3,2,1,0:T(1,128)S(1)}, f32[3,18,1,128]{3,2,1,0:T(1,128)S(1)}, u32[]{:S(2)}, u32[]{:S(2)}) collective-permute-start(f32[3,18,1,128]{3,2,1,0:T(1,128)S(1)} %get-tuple-element.40), channel_id=1, source_target_pairs={{1,0},{2,1},{3,2},{4,3},{5,4},{6,5},{7,6},{9,8},{10,9},{11,10},{12... | collective-permute-start | bytes 82952 | tf_op jit(solution)/shard_map/ppermute | solution.py:18
  257.3 6.0 %collective-permute-start.34 = (f32[3,18,1,128]{3,2,1,0:T(1,128)S(1)}, f32[3,18,1,128]{3,2,1,0:T(1,128)S(1)}, u32[]{:S(2)}, u32[]{:S(2)}) collective-permute-start(f32[3,18,1,128]{3,2,1,0:T(1,128)S(1)} %get-tuple-element.39), channel_id=1, source_target_pairs={{0,1},{1,2},{2,3},{3,4},{4,5},{5,6},{6,7},{8,9},{9,10},{10,11},{11... | collective-permute-start | bytes 82952 | tf_op jit(solution)/shard_map/ppermute | solution.py:17
  263.6 6.8 %collective-permute-start.37 = (f32[3,1,16,128]{3,2,1,0:T(8,128)S(1)}, f32[3,1,16,128]{3,2,1,0:T(8,128)S(1)}, u32[]{:S(2)}, u32[]{:S(2)}) collective-permute-start(f32[3,1,16,128]{3,2,1,0:T(8,128)S(1)} %get-tuple-element.58), channel_id=1, source_target_pairs={{8,0},{16,8},{24,16},{9,1},{17,9},{25,17},{10,2},{18,10},{26,18},{... | collective-permute-start | bytes 73736 | tf_op jit(solution)/shard_map/ppermute | solution.py:18
  264.9 6.4 %collective-permute-start.36 = (f32[3,1,16,128]{3,2,1,0:T(8,128)S(1)}, f32[3,1,16,128]{3,2,1,0:T(8,128)S(1)}, u32[]{:S(2)}, u32[]{:S(2)}) collective-permute-start(f32[3,1,16,128]{3,2,1,0:T(8,128)S(1)} %get-tuple-element.57), channel_id=1, source_target_pairs={{0,8},{8,16},{16,24},{1,9},{9,17},{17,25},{2,10},{10,18},{18,26},{... | collective-permute-start | bytes 73736 | tf_op jit(solution)/shard_map/ppermute | solution.py:17
  271.4 7.0 %collective-permute-start.39 = (f32[3,18,1,128]{3,2,1,0:T(1,128)S(1)}, f32[3,18,1,128]{3,2,1,0:T(1,128)S(1)}, u32[]{:S(2)}, u32[]{:S(2)}) collective-permute-start(f32[3,18,1,128]{3,2,1,0:T(1,128)S(1)} %get-tuple-element.38), channel_id=1, source_target_pairs={{1,0},{2,1},{3,2},{4,3},{5,4},{6,5},{7,6},{9,8},{10,9},{11,10},{12... | collective-permute-start | bytes 82952 | tf_op jit(solution)/shard_map/ppermute | solution.py:18
  273.3 6.0 %collective-permute-start.38 = (f32[3,18,1,128]{3,2,1,0:T(1,128)S(1)}, f32[3,18,1,128]{3,2,1,0:T(1,128)S(1)}, u32[]{:S(2)}, u32[]{:S(2)}) collective-permute-start(f32[3,18,1,128]{3,2,1,0:T(1,128)S(1)} %get-tuple-element.37), channel_id=1, source_target_pairs={{0,1},{1,2},{2,3},{3,4},{4,5},{5,6},{6,7},{8,9},{9,10},{10,11},{11... | collective-permute-start | bytes 82952 | tf_op jit(solution)/shard_map/ppermute | solution.py:17
  279.7 6.8 %collective-permute-start.41 = (f32[3,1,16,128]{3,2,1,0:T(8,128)S(1)}, f32[3,1,16,128]{3,2,1,0:T(8,128)S(1)}, u32[]{:S(2)}, u32[]{:S(2)}) collective-permute-start(f32[3,1,16,128]{3,2,1,0:T(8,128)S(1)} %get-tuple-element.56), channel_id=1, source_target_pairs={{8,0},{16,8},{24,16},{9,1},{17,9},{25,17},{10,2},{18,10},{26,18},{... | collective-permute-start | bytes 73736 | tf_op jit(solution)/shard_map/ppermute | solution.py:18
  281.0 6.4 %collective-permute-start.40 = (f32[3,1,16,128]{3,2,1,0:T(8,128)S(1)}, f32[3,1,16,128]{3,2,1,0:T(8,128)S(1)}, u32[]{:S(2)}, u32[]{:S(2)}) collective-permute-start(f32[3,1,16,128]{3,2,1,0:T(8,128)S(1)} %get-tuple-element.55), channel_id=1, source_target_pairs={{0,8},{8,16},{16,24},{1,9},{9,17},{17,25},{2,10},{10,18},{18,26},{... | collective-permute-start | bytes 73736 | tf_op jit(solution)/shard_map/ppermute | solution.py:17
  287.5 7.0 %collective-permute-start.43 = (f32[3,18,1,128]{3,2,1,0:T(1,128)S(1)}, f32[3,18,1,128]{3,2,1,0:T(1,128)S(1)}, u32[]{:S(2)}, u32[]{:S(2)}) collective-permute-start(f32[3,18,1,128]{3,2,1,0:T(1,128)S(1)} %get-tuple-element.36), channel_id=1, source_target_pairs={{1,0},{2,1},{3,2},{4,3},{5,4},{6,5},{7,6},{9,8},{10,9},{11,10},{12... | collective-permute-start | bytes 82952 | tf_op jit(solution)/shard_map/ppermute | solution.py:18
  289.4 6.0 %collective-permute-start.42 = (f32[3,18,1,128]{3,2,1,0:T(1,128)S(1)}, f32[3,18,1,128]{3,2,1,0:T(1,128)S(1)}, u32[]{:S(2)}, u32[]{:S(2)}) collective-permute-start(f32[3,18,1,128]{3,2,1,0:T(1,128)S(1)} %get-tuple-element.35), channel_id=1, source_target_pairs={{0,1},{1,2},{2,3},{3,4},{4,5},{5,6},{6,7},{8,9},{9,10},{10,11},{11... | collective-permute-start | bytes 82952 | tf_op jit(solution)/shard_map/ppermute | solution.py:17
  295.9 6.8 %collective-permute-start.45 = (f32[3,1,16,128]{3,2,1,0:T(8,128)S(1)}, f32[3,1,16,128]{3,2,1,0:T(8,128)S(1)}, u32[]{:S(2)}, u32[]{:S(2)}) collective-permute-start(f32[3,1,16,128]{3,2,1,0:T(8,128)S(1)} %get-tuple-element.54), channel_id=1, source_target_pairs={{8,0},{16,8},{24,16},{9,1},{17,9},{25,17},{10,2},{18,10},{26,18},{... | collective-permute-start | bytes 73736 | tf_op jit(solution)/shard_map/ppermute | solution.py:18
  297.2 6.4 %collective-permute-start.44 = (f32[3,1,16,128]{3,2,1,0:T(8,128)S(1)}, f32[3,1,16,128]{3,2,1,0:T(8,128)S(1)}, u32[]{:S(2)}, u32[]{:S(2)}) collective-permute-start(f32[3,1,16,128]{3,2,1,0:T(8,128)S(1)} %get-tuple-element.53), channel_id=1, source_target_pairs={{0,8},{8,16},{16,24},{1,9},{9,17},{17,25},{2,10},{10,18},{18,26},{... | collective-permute-start | bytes 73736 | tf_op jit(solution)/shard_map/ppermute | solution.py:17
  303.6 7.0 %collective-permute-start.47 = (f32[3,18,1,128]{3,2,1,0:T(1,128)S(1)}, f32[3,18,1,128]{3,2,1,0:T(1,128)S(1)}, u32[]{:S(2)}, u32[]{:S(2)}) collective-permute-start(f32[3,18,1,128]{3,2,1,0:T(1,128)S(1)} %get-tuple-element.34), channel_id=1, source_target_pairs={{1,0},{2,1},{3,2},{4,3},{5,4},{6,5},{7,6},{9,8},{10,9},{11,10},{12... | collective-permute-start | bytes 82952 | tf_op jit(solution)/shard_map/ppermute | solution.py:18
  305.5 6.0 %collective-permute-start.46 = (f32[3,18,1,128]{3,2,1,0:T(1,128)S(1)}, f32[3,18,1,128]{3,2,1,0:T(1,128)S(1)}, u32[]{:S(2)}, u32[]{:S(2)}) collective-permute-start(f32[3,18,1,128]{3,2,1,0:T(1,128)S(1)} %get-tuple-element.33), channel_id=1, source_target_pairs={{0,1},{1,2},{2,3},{3,4},{4,5},{5,6},{6,7},{8,9},{9,10},{10,11},{11... | collective-permute-start | bytes 82952 | tf_op jit(solution)/shard_map/ppermute | solution.py:17
  312.0 6.8 %collective-permute-start.49 = (f32[3,1,16,128]{3,2,1,0:T(8,128)S(1)}, f32[3,1,16,128]{3,2,1,0:T(8,128)S(1)}, u32[]{:S(2)}, u32[]{:S(2)}) collective-permute-start(f32[3,1,16,128]{3,2,1,0:T(8,128)S(1)} %get-tuple-element.52), channel_id=1, source_target_pairs={{8,0},{16,8},{24,16},{9,1},{17,9},{25,17},{10,2},{18,10},{26,18},{... | collective-permute-start | bytes 73736 | tf_op jit(solution)/shard_map/ppermute | solution.py:18
  313.3 6.4 %collective-permute-start.48 = (f32[3,1,16,128]{3,2,1,0:T(8,128)S(1)}, f32[3,1,16,128]{3,2,1,0:T(8,128)S(1)}, u32[]{:S(2)}, u32[]{:S(2)}) collective-permute-start(f32[3,1,16,128]{3,2,1,0:T(8,128)S(1)} %get-tuple-element.51), channel_id=1, source_target_pairs={{0,8},{8,16},{16,24},{1,9},{9,17},{17,25},{2,10},{10,18},{18,26},{... | collective-permute-start | bytes 73736 | tf_op jit(solution)/shard_map/ppermute | solution.py:17
  319.7 7.0 %collective-permute-start.51 = (f32[3,18,1,128]{3,2,1,0:T(1,128)S(1)}, f32[3,18,1,128]{3,2,1,0:T(1,128)S(1)}, u32[]{:S(2)}, u32[]{:S(2)}) collective-permute-start(f32[3,18,1,128]{3,2,1,0:T(1,128)S(1)} %get-tuple-element.32), channel_id=1, source_target_pairs={{1,0},{2,1},{3,2},{4,3},{5,4},{6,5},{7,6},{9,8},{10,9},{11,10},{12... | collective-permute-start | bytes 82952 | tf_op jit(solution)/shard_map/ppermute | solution.py:18
  321.7 6.0 %collective-permute-start.50 = (f32[3,18,1,128]{3,2,1,0:T(1,128)S(1)}, f32[3,18,1,128]{3,2,1,0:T(1,128)S(1)}, u32[]{:S(2)}, u32[]{:S(2)}) collective-permute-start(f32[3,18,1,128]{3,2,1,0:T(1,128)S(1)} %get-tuple-element.31), channel_id=1, source_target_pairs={{0,1},{1,2},{2,3},{3,4},{4,5},{5,6},{6,7},{8,9},{9,10},{10,11},{11... | collective-permute-start | bytes 82952 | tf_op jit(solution)/shard_map/ppermute | solution.py:17
where the time goes:
time: 334 us; the launch traced here: 329 us
  starting transfers between devices  171 us (51%)
  local copies, waits for them, and re-layouts  91.9 us (28%)
  other arithmetic  43.6 us (13%)
  waiting for transfers between devices  20.2 us (6%)
    ppermute x26, starting transfers between devices, padded_2(): before = lax.ppermute(last, axis, up)  129 us
    reshape x6, local copies, waits for them, and re-layouts, pick_child(): face_term.reshape(row_count // 2, 2, col_count // 2, 2, depth_count // 2, 2)  58.5 us
    ppermute x26, starting transfers between devices, padded_2(): after = lax.ppermute(first, axis, down)  41.8 us
    reshape x1, local copies, waits for them, and re-layouts, restrict(): field.reshape(field.shape[:-3] + (row_count // 2, 2, col_count // 2, 2, d...  26.5 us
    reduce_sum x3, other arithmetic, pick_child(): return 0.0625 * jnp.sum(blocks * selector.reshape(layout), axis=(1, 3, 5))  21.6 us
    ppermute x26, waiting for transfers between devices, padded_2(): before = lax.ppermute(last, axis, up)  18.7 us
    reduce_sum x1, other arithmetic, restrict(): return 0.125 * jnp.sum(blocks, axis=(-5, -3, -1))  9.43 us
  transfers between devices with their start and end apart: 52, of which 22 were waited for; matrix products, arithmetic and copies ran while one was open for 24% of the time, Pallas kernels for 0%

commit v1 on v0

v1 whole, which is shorter than its diff:
```python
import functools

import jax
import jax.numpy as jnp
from jax import lax
from jax.experimental import pallas as pl
from jax.experimental.pallas import tpu as pltpu
from jax.sharding import PartitionSpec as P

CHEB = 4
COARSE_STEPS = 4
HALO = CHEB
VISC_HALO = HALO + 1
COARSE_REACH = (HALO + 2) // 2
COARSE_HALO = COARSE_REACH + COARSE_STEPS - 1
ROW0 = 8
VMEM_LIMIT = 48 * 1024 * 1024


def chebyshev_constants(lower_value, upper_value, count):
    centre = 0.5 * (upper_value + lower_value)
    radius = 0.5 * (upper_value - lower_value)
    spread = centre / radius
    damping = 1.0 / spread
    carried = []
    scaled = []
    for number in range(count - 1):
        renewed = 1.0 / (2.0 * spread - damping)
        carried.append(renewed * damping)
        scaled.append(2.0 * renewed / radius)
        damping = renewed
    return (1.0 / centre, carried, scaled)


def constants_of(lower_ref, upper_ref):
    lower_value = jnp.full((1, 128), lower_ref[0], jnp.float32)
    upper_value = jnp.full((1, 128), upper_ref[0], jnp.float32)
    return chebyshev_constants(lower_value, upper_value, max(CHEB, COARSE_STEPS))


def lookup(table_ref, phases):
    viscosity = jnp.full(phases.shape, table_ref[0], jnp.float32)
    for table_row in range(1, table_ref.shape[0]):
        viscosity = jnp.where(phases == table_row, table_ref[table_row], viscosity)
    return viscosity


def lanes(rows, depth):
    return lax.broadcasted_iota(jnp.int32, (rows, depth), 1)


def below(value, by=1):
    return pltpu.roll(value, by, 1)


def above(value, by=1):
    return pltpu.roll(value, value.shape[1] - by, 1)


def is_odd(axis):
    return lax.rem(lax.axis_index(axis), 2) == 1


def pack_x_kernel(forcing_ref, phase_ref, table_ref, low_ref, high_ref):
    parts, nx = forcing_ref.shape[:2]
    for c in range(parts):
        for i in range(HALO):
            low_ref[c * HALO + i] = forcing_ref[c, i]
            high_ref[c * HALO + i] = forcing_ref[c, nx - HALO + i]
    for i in range(VISC_HALO):
        low_ref[parts * HALO + i] = lookup(table_ref, phase_ref[i])
        high_ref[parts * HALO + i] = lookup(table_ref, phase_ref[nx - VISC_HALO + i])


def pack_y_kernel(forcing_ref, phase_ref, table_ref, left_ref, right_ref, same_ref, cross_ref):
    parts, nx, ny = forcing_ref.shape[:3]
    odd = is_odd("gy")

    def put(row, low, high):
        count = low.shape[0]
        same_ref[pl.ds(row, count), :] = jnp.where(odd, low, high)
        cross_ref[pl.ds(row, count), :] = jnp.where(odd, high, low)

    row = 0
    for c in range(parts):
        for x in range(-HALO, nx + HALO):
            if x < 0:
                ref, at = left_ref, (c * HALO + x + HALO,)
            elif x < nx:
                ref, at = forcing_ref, (c, x)
            else:
                ref, at = right_ref, (c * HALO + x - nx,)
            put(row, ref[at + (slice(0, HALO),)], ref[at + (slice(ny - HALO, ny),)])
            row += HALO
    for x in range(-VISC_HALO, nx + VISC_HALO):
        first, last = slice(0, VISC_HALO), slice(ny - VISC_HALO, ny)
        if x < 0:
            at = parts * HALO + x + VISC_HALO
            put(row, left_ref[at, first], left_ref[at, last])
        elif x < nx:
            put(row, lookup(table_ref, phase_ref[x, first]), lookup(table_ref, phase_ref[x, last]))
        else:
            at = parts * HALO + x - nx
            put(row, right_ref[at, first], right_ref[at, last])
        row += VISC_HALO


def fine_steps(weight_ref, residual_ref, d_refs, constants, width):
    first_scale, carried, scaled = constants
    parts, rows = residual_ref.shape[0], residual_ref.shape[2]
    mid = pl.ds(ROW0, rows)

    def start(x, _):
        for c in range(parts):
            d_refs[0][c, x, mid, :] = first_scale * residual_ref[c, x]
        return 0

    lax.fori_loop(0, width, start, 0)
    for number in range(CHEB):
        old, new = d_refs[number % 2], d_refs[(number + 1) % 2]

        def step(x, _, number=number, old=old, new=new):
            weights = [weight_ref[f, x] for f in range(6)]
            for c in range(parts):
                own = old[c, x, mid, :]
                beside = weights[0] * old[c, x - 1, mid, :] + weights[1] * old[c, x + 1, mid, :]
                beside = beside + weights[2] * old[c, x, pl.ds(ROW0 - 1, rows), :]
                beside = beside + weights[3] * old[c, x, pl.ds(ROW0 + 1, rows), :]
                beside = beside + weights[4] * below(own) + weights[5] * above(own)
                fresh = residual_ref[c, x] - own + beside
                residual_ref[c, x] = fresh
                if number + 1 < CHEB:
                    new[c, x, mid, :] = carried[number] * own + scaled[number] * fresh
            return 0

        lax.fori_loop(number + 1, width - 1 - number, step, 0)


def clear_rims(ref, rows):
    planes = ref.shape[1]
    for c in range(ref.shape[0]):
        for x in range(planes):
            ref[c, x, pl.ds(0, ROW0), :] = jnp.zeros((ROW0, ref.shape[3]), jnp.float32)
            ref[c, x, pl.ds(ROW0 + rows, ROW0), :] = jnp.zeros((ROW0, ref.shape[3]), jnp.float32)


def pre_kernel(
    shape_x,
    shape_y,
    forcing_ref, phase_ref, table_ref, lower_ref, upper_ref, left_ref, right_ref, same_ref, cross_ref,
    weight_ref, diagonal_ref, smoothed_ref, coarse_ref, low_ref, high_ref,
    visc_ref, inverse_ref, residual_ref, d0_ref, d1_ref, pair_ref, row_ref,
):
    parts, nx, ny, depth = forcing_ref.shape
    width, rows = nx + 2 * HALO, ny + 2 * HALO
    at_x, at_y = lax.axis_index("gx"), lax.axis_index("gy")
    odd = is_odd("gy")
    has_left, has_right = at_x > 0, at_x < shape_x - 1
    has_low, has_high = at_y > 0, at_y < shape_y - 1
    visc_base = parts * width * HALO

    def low_rows(row, count):
        here = pl.ds(row, count)
        return jnp.where(odd, same_ref[here, :], cross_ref[here, :])

    def high_rows(row, count):
        here = pl.ds(row, count)
        return jnp.where(odd, cross_ref[here, :], same_ref[here, :])

    for i in range(nx + 2 * VISC_HALO):
        x = i - VISC_HALO
        if x < 0:
            own = left_ref[parts * HALO + i]
            inside = has_left
        elif x < nx:
            own = lookup(table_ref, phase_ref[x])
            inside = None
        else:
            own = right_ref[parts * HALO + x - nx]
            inside = has_right
        low = low_rows(visc_base + i * VISC_HALO, VISC_HALO)
        high = high_rows(visc_base + i * VISC_HALO, VISC_HALO)
        ok_low, ok_high = has_low, has_high
        if inside is not None:
            own = jnp.where(inside, own, 0.0)
            ok_low, ok_high = jnp.logical_and(ok_low, inside), jnp.logical_and(ok_high, inside)
        visc_ref[i, pl.ds(VISC_HALO, ny), :] = own
        visc_ref[i, pl.ds(0, VISC_HALO), :] = jnp.where(ok_low, low, 0.0)
        visc_ref[i, pl.ds(VISC_HALO + ny, VISC_HALO), :] = jnp.where(ok_high, high, 0.0)

    lane = lanes(rows, depth)

    def weigh(x, _):
        centre = visc_ref[x + 1, pl.ds(1, rows), :]
        halved = 0.5 * centre
        z_below = jnp.where(lane == 0, 0.0, below(halved))
        z_above = jnp.where(lane == depth - 1, 0.0, above(halved))
        faces = [
            halved + 0.5 * visc_ref[x, pl.ds(1, rows), :],
            halved + 0.5 * visc_ref[x + 2, pl.ds(1, rows), :],
            halved + 0.5 * visc_ref[x + 1, pl.ds(0, rows), :],
            halved + 0.5 * visc_ref[x + 1, pl.ds(2, rows), :],
            halved + z_below,
            halved + z_above,
        ]
        diagonal = faces[0] + faces[1] + faces[2] + faces[3] + faces[4] + faces[5]
        inside = centre > 0.0
        inverse = jnp.where(inside, 1.0 / jnp.where(inside, diagonal, 1.0), 0.0)
        for f in range(4):
            weight_ref[f, x] = faces[f] * inverse
        weight_ref[4, x] = jnp.where(lane == 0, 0.0, faces[4] * inverse)
        weight_ref[5, x] = jnp.where(lane == depth - 1, 0.0, faces[5] * inverse)
        inverse_ref[x] = inverse
        pair_ref[x] = diagonal
        return 0

    lax.fori_loop(0, width, weigh, 0)
    for x in range(nx):
        diagonal_ref[x] = pair_ref[x + HALO, pl.ds(HALO, ny), :]

    for c in range(parts):
        for i in range(width):
            x = i - HALO
            if x < 0:
                own = left_ref[c * HALO + i]
            elif x < nx:
                own = forcing_ref[c, x]
            else:
                own = right_ref[c * HALO + x - nx]
            at = (c * width + i) * HALO
            residual_ref[c, i, pl.ds(HALO, ny), :] = own * inverse_ref[i, pl.ds(HALO, ny), :]
            residual_ref[c, i, pl.ds(0, HALO), :] = low_rows(at, HALO) * inverse_ref[i, pl.ds(0, HALO), :]
            residual_ref[c, i, pl.ds(HALO + ny, HALO), :] = (
                high_rows(at, HALO) * inverse_ref[i, pl.ds(HALO + ny, HALO), :]
            )

    clear_rims(d0_ref, rows)
    clear_rims(d1_ref, rows)
    fine_steps(weight_ref, residual_ref, (d0_ref, d1_ref), constants_of(lower_ref, upper_ref), width)

    half = ny // 2
    even_own = lanes(ny, depth) % 2 == 0
    even_wide = lanes(ny + 2, depth) % 2 == 0
    even = lanes(half, depth) % 2 == 0
    lane_half = lanes(half, depth)

    def z_pair(value, even_mask):
        return value + jnp.where(even_mask, above(value), below(value))

    def y_sum(value, slot):
        row_ref[slot, pl.ds(0, value.shape[0]), :] = value
        return row_ref[slot, pl.ds(0, half, 2), :] + row_ref[slot, pl.ds(1, half, 2), :]

    def visc_own(x):
        return visc_ref[x + VISC_HALO, pl.ds(VISC_HALO, ny), :]

    inverses = []
    for i in range(nx // 2):
        faces_x = []
        for x in (2 * i - 1, 2 * i, 2 * i + 1, 2 * i + 2):
            faces_x.append(y_sum(z_pair(visc_own(x), even_own), 0))
        lower_x = faces_x[0] + faces_x[1]
        upper_x = faces_x[2] + faces_x[3]
        wide = pl.ds(VISC_HALO - 1, ny + 2)
        both = visc_ref[2 * i + VISC_HALO, wide, :] + visc_ref[2 * i + 1 + VISC_HALO, wide, :]
        row_ref[1, pl.ds(0, ny + 2), :] = z_pair(both, even_wide)
        picks = [row_ref[1, pl.ds(start, half, 2), :] for start in range(4)]
        lower_y = picks[0] + picks[1]
        upper_y = picks[2] + picks[3]
        column = y_sum(both[1 : ny + 1], 2)
        lower_z = column + jnp.where(lane_half == 0, 0.0, below(column))
        lower_z = jnp.where(even, lower_z, below(lower_z))
        upper_z = column + jnp.where(lane_half == depth - 1, 0.0, above(column))
        upper_z = jnp.where(even, above(upper_z), upper_z)
        inverse = 1.0 / (lower_x + upper_x + lower_y + upper_y + lower_z + upper_z)
        inverses.append(32.0 * inverse)
        sources = []
        for c in range(parts):
            total = 0.0
            for x in (2 * i, 2 * i + 1):
                total = total + residual_ref[c, x + HALO, pl.ds(HALO, ny), :] * diagonal_ref[x]
            sources.append(y_sum(z_pair(total, even_own), 3 + c) * (4.0 * inverse))
        faces = [upper_x * (1.0 / 32.0), upper_y * (1.0 / 32.0), upper_z * (1.0 / 32.0)]
        coarse_ref[0, i] = jnp.where(even, sources[0], sources[1])
        coarse_ref[1, i] = jnp.where(even, sources[2], faces[0])
        coarse_ref[2, i] = jnp.where(even, faces[1], faces[2])
        if i % 2 == 1:
            coarse_ref[3, i // 2] = jnp.where(even, inverses[i - 1], inverses[i])

    for c in range(parts):
        for x in range(nx):
            smoothed_ref[c, x] = residual_ref[c, x + HALO, pl.ds(HALO, ny), :]

    at = 0
    ncx = nx // 2
    for f in range(4):
        shared = 2 if f == 3 else 1
        count = COARSE_HALO // shared
        for i in range(count):
            low_ref[at] = coarse_ref[f, i]
            high_ref[at] = coarse_ref[f, ncx // shared - count + i]
            at += 1
    tiles = ny // half
    for c in range(parts):
        for i in range(HALO):
            for t in range(tiles):
                low_ref[at] = smoothed_ref[c, i, pl.ds(t * half, half), :]
                high_ref[at] = smoothed_ref[c, nx - HALO + i, pl.ds(t * half, half), :]
                at += 1


def coarse_spot(f, i, ncx):
    shared = 2 if f == 3 else 1
    count, own = COARSE_HALO // shared, ncx // shared
    base = f * COARSE_HALO
    if i < count:
        return "left", base + i
    if i < count + own:
        return "own", i - count
    return "right", base + i - count - own


def pack_y2_kernel(smoothed_ref, coarse_ref, left_ref, right_ref, same_ref, cross_ref):
    parts, nx, ny = smoothed_ref.shape[:3]
    ncx, half = nx // 2, ny // 2
    odd = is_odd("gy")
    sides = {"left": left_ref, "right": right_ref}

    def put(row, low, high):
        count = low.shape[0]
        same_ref[pl.ds(row, count), :] = jnp.where(odd, low, high)
        cross_ref[pl.ds(row, count), :] = jnp.where(odd, high, low)

    row = 0
    for f in range(4):
        shared = 2 if f == 3 else 1
        for i in range((ncx + 2 * COARSE_HALO) // shared):
            side, at = coarse_spot(f, i, ncx)
            if side == "own":
                ref, spot = coarse_ref, (f, at)
            else:
                ref, spot = sides[side], (at,)
            first, last = slice(0, COARSE_HALO), slice(half - COARSE_HALO, half)
            put(row, ref[spot + (first,)], ref[spot + (last,)])
            row += COARSE_HALO
    tiles = ny // half
    fine_base = 3 * COARSE_HALO + COARSE_HALO // 2
    for c in range(parts):
        for x in range(-HALO, nx + HALO):
            if 0 <= x < nx:
                put(row, smoothed_ref[c, x, pl.ds(0, HALO), :], smoothed_ref[c, x, pl.ds(ny - HALO, HALO), :])
            else:
                ref = left_ref if x < 0 else right_ref
                i = x + HALO if x < 0 else x - nx
                at = fine_base + (c * HALO + i) * tiles
                put(row, ref[at, pl.ds(0, HALO), :], ref[at + tiles - 1, pl.ds(half - HALO, HALO), :])
            row += HALO


def post_kernel(
    shape_x,
    shape_y,
    weight_ref, diagonal_ref, smoothed_ref, coarse_ref, lower_ref, upper_ref, left_ref, right_ref, same_ref, cross_ref,
    out_ref,
    field_ref, cweight_ref, source_ref, cd0_ref, cd1_ref, correction_ref, prolonged_ref, residual_ref, d0_ref, d1_ref,
):
    parts, nx, ny, depth = smoothed_ref.shape
    width, rows = nx + 2 * HALO, ny + 2 * HALO
    ncx, half = nx // 2, ny // 2
    cwidth, crows = ncx + 2 * COARSE_HALO, half + 2 * COARSE_HALO
    srows = source_ref.shape[2]
    at_x, at_y = lax.axis_index("gx"), lax.axis_index("gy")
    odd = is_odd("gy")
    has_left, has_right = at_x > 0, at_x < shape_x - 1
    has_low, has_high = at_y > 0, at_y < shape_y - 1
    sides = {"left": left_ref, "right": right_ref}
    constants = constants_of(lower_ref, upper_ref)
    first_scale, carried, scaled = constants

    def low_rows(row, count):
        here = pl.ds(row, count)
        return jnp.where(odd, same_ref[here, :], cross_ref[here, :])

    def high_rows(row, count):
        here = pl.ds(row, count)
        return jnp.where(odd, cross_ref[here, :], same_ref[here, :])

    def masked(inside, own, low, high):
        ok_low, ok_high = has_low, has_high
        if inside is not None:
            own = jnp.where(inside, own, 0.0)
            ok_low, ok_high = jnp.logical_and(ok_low, inside), jnp.logical_and(ok_high, inside)
        return own, jnp.where(ok_low, low, 0.0), jnp.where(ok_high, high, 0.0)

    insides = {"left": has_left, "own": None, "right": has_right}
    row = 0
    for f in range(4):
        shared = 2 if f == 3 else 1
        for i in range(cwidth // shared):
            side, at = coarse_spot(f, i, ncx)
            own = coarse_ref[f, at] if side == "own" else sides[side][at]
            low, high = low_rows(row, COARSE_HALO), high_rows(row, COARSE_HALO)
            own, low, high = masked(insides[side], own, low, high)
            field_ref[f, i, pl.ds(ROW0 + COARSE_HALO, half), :] = own
            field_ref[f, i, pl.ds(ROW0, COARSE_HALO), :] = low
            field_ref[f, i, pl.ds(ROW0 + COARSE_HALO + half, COARSE_HALO), :] = high
            field_ref[f, i, pl.ds(0, ROW0), :] = jnp.zeros((ROW0, depth), jnp.float32)
            tail = field_ref.shape[2] - ROW0 - crows
            field_ref[f, i, pl.ds(ROW0 + crows, tail), :] = jnp.zeros((tail, depth), jnp.float32)
            row += COARSE_HALO
    tiles = ny // half
    fine_base = 3 * COARSE_HALO + COARSE_HALO // 2
    for c in range(parts):
        for i in range(width):
            x = i - HALO
            if 0 <= x < nx:
                side = "own"
                own = smoothed_ref[c, x]
            else:
                side = "left" if x < 0 else "right"
                j = i if x < 0 else x - nx
                at = fine_base + (c * HALO + j) * tiles
                own = jnp.concatenate([sides[side][at + t] for t in range(tiles)], axis=0)
            own, low, high = masked(insides[side], own, low_rows(row, HALO), high_rows(row, HALO))
            residual_ref[c, i, pl.ds(HALO, ny), :] = own
            residual_ref[c, i, pl.ds(0, HALO), :] = low
            residual_ref[c, i, pl.ds(HALO + ny, HALO), :] = high
            row += HALO

    mid = pl.ds(ROW0, srows)
    lane = lanes(srows, depth)
    even = lane % 2 == 0

    def first_of(value):
        return jnp.where(even, value, below(value))

    def second_of(value):
        return jnp.where(even, above(value), value)

    even_low = lanes(field_ref.shape[2], depth) % 2 == 0
    for i in range(cwidth):
        packed = field_ref[3, i // 2, mid, :]
        inverse = first_of(packed) if i % 2 == 0 else second_of(packed)
        upper_x = second_of(field_ref[1, i, mid, :])
        faces_y = field_ref[2, i]
        upper_y = jnp.where(even_low, faces_y, below(faces_y))
        upper_z = second_of(field_ref[2, i, mid, :])
        source_ref[0, i] = field_ref[0, i, mid, :]
        source_ref[1, i] = first_of(field_ref[1, i, mid, :])
        if i > 0:
            cweight_ref[0, i] = second_of(field_ref[1, i - 1, mid, :]) * inverse
        cweight_ref[1, i] = upper_x * inverse
        cweight_ref[2, i] = upper_y[ROW0 - 1 : ROW0 - 1 + srows] * inverse
        cweight_ref[3, i] = upper_y[ROW0 : ROW0 + srows] * inverse
        cweight_ref[4, i] = jnp.where(lane < 2, 0.0, below(upper_z, 2) * inverse)
        cweight_ref[5, i] = jnp.where(lane >= depth - 2, 0.0, upper_z * inverse)

    clear_rims(cd0_ref, srows)
    clear_rims(cd1_ref, srows)

    def start(i, _):
        for s in range(2):
            value = first_scale * source_ref[s, i]
            cd0_ref[s, i, mid, :] = value
            correction_ref[s, i] = value
        return 0

    lax.fori_loop(0, cwidth, start, 0)
    for number in range(COARSE_STEPS - 1):
        old, new = ((cd0_ref, cd1_ref), (cd1_ref, cd0_ref))[number % 2]

        def step(i, _, number=number, old=old, new=new):
            weights = [cweight_ref[f, i] for f in range(6)]
            for s in range(2):
                own = old[s, i, mid, :]
                beside = weights[0] * old[s, i - 1, mid, :] + weights[1] * old[s, i + 1, mid, :]
                beside = beside + weights[2] * old[s, i, pl.ds(ROW0 - 1, srows), :]
                beside = beside + weights[3] * old[s, i, pl.ds(ROW0 + 1, srows), :]
                beside = beside + weights[4] * below(own, 2) + weights[5] * above(own, 2)
                fresh = source_ref[s, i] - own + beside
                source_ref[s, i] = fresh
                direction = carried[number] * own + scaled[number] * fresh
                new[s, i, mid, :] = direction
                correction_ref[s, i] = correction_ref[s, i] + direction
            return 0

        lax.fori_loop(number + 1, cwidth - 1 - number, step, 0)

    edge = COARSE_HALO - COARSE_REACH
    pwidth, prows = ncx + 2 * COARSE_REACH, half + 2 * COARSE_REACH
    prow0 = ROW0 - (2 * COARSE_REACH - HALO)
    even_p = lanes(prows, depth) % 2 == 0
    for i in range(pwidth):
        pair = correction_ref[0, i + edge, pl.ds(edge, prows), :]
        single = correction_ref[1, i + edge, pl.ds(edge, prows), :]
        values = [
            jnp.where(even_p, pair, below(pair)),
            jnp.where(even_p, above(pair), pair),
            single,
        ]
        for c in range(parts):
            prolonged_ref[c, i, pl.ds(prow0, prows, 2), :] = values[c]
            prolonged_ref[c, i, pl.ds(prow0 + 1, prows, 2), :] = values[c]

    fine = pl.ds(ROW0, rows)
    shift = 2 * COARSE_REACH - HALO
    for i in range(width):
        weights = [weight_ref[f, i] for f in range(6)]
        at, before, after = (i + shift) // 2, (i + shift - 1) // 2, (i + shift + 1) // 2
        for c in range(parts):
            own = prolonged_ref[c, at, fine, :]
            beside = weights[0] * prolonged_ref[c, before, fine, :] + weights[1] * prolonged_ref[c, after, fine, :]
            beside = beside + weights[2] * prolonged_ref[c, at, pl.ds(ROW0 - 1, rows), :]
            beside = beside + weights[3] * prolonged_ref[c, at, pl.ds(ROW0 + 1, rows), :]
            beside = beside + weights[4] * below(own) + weights[5] * above(own)
            residual_ref[c, i] = residual_ref[c, i] - own + beside

    clear_rims(d0_ref, rows)
    clear_rims(d1_ref, rows)
    fine_steps(weight_ref, residual_ref, (d0_ref, d1_ref), constants, width)
    for c in range(parts):
        for x in range(nx):
            out_ref[c, x] = residual_ref[c, x + HALO, pl.ds(HALO, ny), :] * diagonal_ref[x]


def call(kernel, outs, scratch, specs):
    return pl.pallas_call(
        kernel,
        out_shape=[jax.ShapeDtypeStruct(shape, jnp.float32) for shape in outs],
        in_specs=[pl.BlockSpec(memory_space=space) for space in specs],
        out_specs=[pl.BlockSpec(memory_space=pltpu.VMEM) for _ in outs],
        scratch_shapes=[pltpu.VMEM(shape, jnp.float32) for shape in scratch],
        compiler_params=pltpu.CompilerParams(vmem_limit_bytes=VMEM_LIMIT),
    )


def ring_x(low, high):
    devices = lax.axis_size("gx")
    up = [(i, (i + 1) % devices) for i in range(devices)]
    down = [(j, i) for i, j in up]
    return lax.ppermute(high, "gx", up), lax.ppermute(low, "gx", down)


def swap_y(same, cross):
    devices = lax.axis_size("gy")
    pairs = [(i, i ^ 1) for i in range(devices)]
    others = [(0, 0), (devices - 1, devices - 1)]
    others = others + [(i, ((i + 1) ^ 1) - 1) for i in range(1, devices - 1)]
    return lax.ppermute(same, "gy", pairs), lax.ppermute(cross, "gy", others)


def up_to(value, unit):
    return -(-value // unit) * unit


def local(forcing, phase_index, visc_table, lower_bound, upper_bound):
    vmem, smem = pltpu.VMEM, pltpu.SMEM
    parts, nx, ny, depth = forcing.shape
    shape_x, shape_y = lax.axis_size("gx"), lax.axis_size("gy")
    width, rows = nx + 2 * HALO, ny + 2 * HALO
    ncx, half = nx // 2, ny // 2
    cwidth, crows = ncx + 2 * COARSE_HALO, half + 2 * COARSE_HALO
    srows = up_to(crows, 8)

    slab = (parts * HALO + VISC_HALO, ny, depth)
    low, high = call(pack_x_kernel, [slab, slab], [], [vmem, vmem, smem])(forcing, phase_index, visc_table)
    left, right = ring_x(low, high)

    count = up_to(parts * width * HALO + (nx + 2 * VISC_HALO) * VISC_HALO, 8)
    slab = (count, depth)
    same, cross = call(pack_y_kernel, [slab, slab], [], [vmem, vmem, smem, vmem, vmem])(
        forcing, phase_index, visc_table, left, right
    )
    same, cross = swap_y(same, cross)

    tiles = 3 * COARSE_HALO + COARSE_HALO // 2 + parts * HALO * (ny // half)
    slab = (tiles, half, depth)
    fine_d = (parts, width, rows + 2 * ROW0, depth)
    weight, diagonal, smoothed, coarse, low, high = call(
        functools.partial(pre_kernel, shape_x, shape_y),
        [(6, width, rows, depth), (nx, ny, depth), (parts, nx, ny, depth), (4, ncx, half, depth), slab, slab],
        [
            (nx + 2 * VISC_HALO, up_to(ny + 2 * VISC_HALO, 8), depth),
            (width, rows, depth),
            (parts, width, rows, depth),
            fine_d,
            fine_d,
            (width, rows, depth),
            (6, up_to(ny + 2, 8), depth),
        ],
        [vmem, vmem, smem, smem, smem, vmem, vmem, vmem, vmem],
    )(forcing, phase_index, visc_table, lower_bound, upper_bound, left, right, same, cross)
    left, right = ring_x(low, high)

    count = up_to((3 * cwidth + cwidth // 2) * COARSE_HALO + parts * width * HALO, 8)
    slab = (count, depth)
    same, cross = call(pack_y2_kernel, [slab, slab], [], [vmem] * 4)(smoothed, coarse, left, right)
    same, cross = swap_y(same, cross)

    coarse_d = (2, cwidth, srows + 2 * ROW0, depth)
    (out,) = call(
        functools.partial(post_kernel, shape_x, shape_y),
        [(parts, nx, ny, depth)],
        [
            (4, cwidth, up_to(ROW0 + crows + 1, 8), depth),
            (6, cwidth, srows, depth),
            (2, cwidth, srows, depth),
            coarse_d,
            coarse_d,
            (2, cwidth, srows, depth),
            (parts, ncx + 2 * COARSE_REACH, rows + 2 * ROW0, depth),
            (parts, width, rows, depth),
            fine_d,
            fine_d,
        ],
        [vmem, vmem, vmem, vmem, smem, smem, vmem, vmem, vmem, vmem],
    )(weight, diagonal, smoothed, coarse, lower_bound, upper_bound, left, right, same, cross)
    return out


def solution(mesh):
    in_specs = (P(None, "gx", "gy", None), P("gx", "gy", None), P(), P(), P())
    out_specs = P(None, "gx", "gy", None)
    return jax.shard_map(local, mesh=mesh, in_specs=in_specs, out_specs=out_specs, check_vma=False)
```

time: 334 us -> 67.4 us (0.20); the launches traced: 329 us -> 67.2 us
  starting transfers between devices: 171 us -> 18.2 us
  local copies, waits for them, and re-layouts: 91.9 us -> 2.55 us
  other arithmetic: 43.6 us -> 0 us
  Pallas kernels: 0 us -> 27.1 us
    ppermute x52 -> x8, starting transfers between devices: 171 us -> 18.2 us  [the longest x4 12.7 us: swap_y(): return (lax.ppermute(same, 'gy', pairs), lax.ppermute(cross, 'gy', others))]
    reshape x9 -> x0, local copies, waits for them, and re-layouts: 88.1 us -> none  [the longest x6 58.5 us: pick_child(): face_term.reshape(row_count // 2, 2, col_count // 2, 2, depth_count // 2, 2)]
    reduce_sum x4 -> x0, other arithmetic: 31 us -> none  [the longest x3 21.6 us: pick_child(): return 0.0625 * jnp.sum(blocks * selector.reshape(layout), axis=(1, 3, 5))]
    pallas_call x0 -> x5, Pallas kernels: none -> 27.1 us  [the longest x1 14.8 us: local(): call(functools.partial(post_kernel, shape_x, shape_y), [(parts, nx, ny, d...]
    select_n x1 -> x0, other arithmetic: 5.94 us -> none  [local(): jnp.where(phase_index == table_row, visc_table[table_row], viscosity)]
    ppermute x52 -> x8, waiting for transfers between devices: 20.2 us -> 17.9 us  [the longest x4 10 us: ring_x(): return (lax.ppermute(high, 'gx', up), lax.ppermute(low, 'gx', down))]
  transfers between devices with their start and end apart: 52 -> 8, of which waited for: 22 -> 6; matrix products, arithmetic and copies ran while one was open for 24% -> 0% of each run, Pallas kernels for 0% -> 0%
where the time goes in v1:
time: 67.4 us; the launch traced here: 67.2 us
  Pallas kernels  27.1 us (40%)
  starting transfers between devices  18.2 us (27%)
  waiting for transfers between devices  17.9 us (27%)
  local copies, waits for them, and re-layouts  2.55 us (4%)
  between operations  1.37 us (2%)
    pallas_call x1, Pallas kernels, local(): call(functools.partial(post_kernel, shape_x, shape_y), [(parts, nx, ny, d...  14.8 us
    ppermute x4, starting transfers between devices, swap_y(): return (lax.ppermute(same, 'gy', pairs), lax.ppermute(cross, 'gy', others))  12.7 us
    pallas_call x1, Pallas kernels, local(): call(functools.partial(pre_kernel, shape_x, shape_y), [(6, width, rows, d...  10.9 us
    ppermute x4, waiting for transfers between devices, ring_x(): return (lax.ppermute(high, 'gx', up), lax.ppermute(low, 'gx', down))  10 us
    ppermute x4, waiting for transfers between devices, swap_y(): return (lax.ppermute(same, 'gy', pairs), lax.ppermute(cross, 'gy', others))  7.91 us
    ppermute x4, starting transfers between devices, ring_x(): return (lax.ppermute(high, 'gx', up), lax.ppermute(low, 'gx', down))  5.53 us
    unnamed x6, local copies, waits for them, and re-layouts  2.55 us
  transfers between devices with their start and end apart: 8, of which 6 were waited for; matrix products, arithmetic and copies ran while one was open for 0% of the time, Pallas kernels for 0%

profile of v1, /device:TPU:1, one launch (start us, length us, event | category | flops | bytes accessed | tf_op | source)
XLA Modules:
  0.0 67.2 jit_solution(5791552558539904202)
XLA Ops:
  0.0 0.0 copy-start
  0.0 1.0 %copy-done = f32[3,16,16,128]{3,2,1,0:T(8,128)S(1)} copy-done((f32[3,16,16,128]{3,2,1,0:T(8,128)S(1)}, f32[3,16,16,128]{3,2,1,0:T(8,128)}, u32[]{:S(2)}) %copy-start) | copy-done | bytes 393240
  1.0 0.0 copy-start.1
  1.0 0.9 %copy-done.1 = s32[16,16,128]{2,1,0:T(8,128)S(1)} copy-done((s32[16,16,128]{2,1,0:T(8,128)S(1)}, s32[16,16,128]{2,1,0:T(8,128)}, u32[]{:S(2)}) %copy-start.1) | copy-done | bytes 131096
  1.9 0.0 copy-start.2
  1.9 0.7 copy-done.2
  2.6 0.6 shard_map.55
  3.2 2.1 %collective-permute-start = (f32[17,16,128]{2,1,0:T(8,128)S(1)}, f32[17,16,128]{2,1,0:T(8,128)S(1)}, u32[]{:S(2)}, u32[]{:S(2)}) collective-permute-start(f32[17,16,128]{2,1,0:T(8,128)S(1)} %get-tuple-element.17), channel_id=1, source_target_pairs={{0,8},{8,16},{16,24},{24,0},{1,9},{9,17},{17,25},{25,1},{2,10},{10... | collective-permute-start | bytes 417800 | tf_op jit(solution)/shard_map/ppermute | solution.py:541
  5.3 1.0 %collective-permute-start.1 = (f32[17,16,128]{2,1,0:T(8,128)S(1)}, f32[17,16,128]{2,1,0:T(8,128)S(1)}, u32[]{:S(2)}, u32[]{:S(2)}) collective-permute-start(f32[17,16,128]{2,1,0:T(8,128)S(1)} %get-tuple-element.18), channel_id=1, source_target_pairs={{8,0},{16,8},{24,16},{0,24},{9,1},{17,9},{25,17},{1,25},{10,2},{18... | collective-permute-start | bytes 417800 | tf_op jit(solution)/shard_map/ppermute | solution.py:541
  6.3 3.3 %collective-permute-done.left_ref = f32[17,16,128]{2,1,0:T(8,128)S(1)} collective-permute-done((f32[17,16,128]{2,1,0:T(8,128)S(1)}, f32[17,16,128]{2,1,0:T(8,128)S(1)}, u32[]{:S(2)}, u32[]{:S(2)}) %collective-permute-start) | collective-permute-done | bytes 139296 | tf_op jit(solution)/shard_map/ppermute | solution.py:541
  9.6 2.9 %collective-permute-done.1.right_ref = f32[17,16,128]{2,1,0:T(8,128)S(1)} collective-permute-done((f32[17,16,128]{2,1,0:T(8,128)S(1)}, f32[17,16,128]{2,1,0:T(8,128)S(1)}, u32[]{:S(2)}, u32[]{:S(2)}) %collective-permute-start.1) | collective-permute-done | bytes 139296 | tf_op jit(solution)/shard_map/ppermute | solution.py:541
  12.5 0.7 shard_map.56
  13.2 1.6 %collective-permute-start.2 = (f32[424,128]{1,0:T(8,128)S(1)}, f32[424,128]{1,0:T(8,128)S(1)}, u32[]{:S(2)}, u32[]{:S(2)}) collective-permute-start(f32[424,128]{1,0:T(8,128)S(1)} %get-tuple-element.19), channel_id=1, source_target_pairs={{0,1},{1,0},{2,3},{3,2},{4,5},{5,4},{6,7},{7,6},{8,9},{9,8},{10,11... | collective-permute-start | bytes 651272 | tf_op jit(solution)/shard_map/ppermute | solution.py:549
  14.8 3.1 %collective-permute-start.3 = (f32[424,128]{1,0:T(8,128)S(1)}, f32[424,128]{1,0:T(8,128)S(1)}, u32[]{:S(2)}, u32[]{:S(2)}) collective-permute-start(f32[424,128]{1,0:T(8,128)S(1)} %get-tuple-element.20), channel_id=1, source_target_pairs={{0,0},{7,7},{1,2},{2,1},{3,4},{4,3},{5,6},{6,5},{8,8},{15,15},{9,1... | collective-permute-start | bytes 651272 | tf_op jit(solution)/shard_map/ppermute | solution.py:549
  19.2 0.0 collective-permute-done.2.same_ref
  19.2 2.8 %collective-permute-done.3.cross_ref = f32[424,128]{1,0:T(8,128)S(1)} collective-permute-done((f32[424,128]{1,0:T(8,128)S(1)}, f32[424,128]{1,0:T(8,128)S(1)}, u32[]{:S(2)}, u32[]{:S(2)}) %collective-permute-start.3) | collective-permute-done | bytes 217120 | tf_op jit(solution)/shard_map/ppermute | solution.py:549
  22.0 10.9 %shard_map.57 = (f32[6,24,24,128]{3,2,1,0:T(8,128)S(1)}, f32[16,16,128]{2,1,0:T(8,128)S(1)}, f32[3,16,16,128]{3,2,1,0:T(8,128)S(1)}, f32[4,8,8,128]{3,2,1,0:T(8,...) custom-call(f32[3,16,16,128]{3,2,1,0:T(8,128)S(1)} %copy-done, s32[16,16,128]{2,1,0:T(8,128)S(1)} %copy-done.1, ...), custom_call_target="tpu_custom_call" | custom-call | tf_op jit(solution)/shard_map/pallas_call | solution.py:579
  32.9 1.3 %collective-permute-start.4 = (f32[45,8,128]{2,1,0:T(8,128)S(1)}, f32[45,8,128]{2,1,0:T(8,128)S(1)}, u32[]{:S(2)}, u32[]{:S(2)}) collective-permute-start(f32[45,8,128]{2,1,0:T(8,128)S(1)} %get-tuple-element.25), channel_id=1, source_target_pairs={{0,8},{8,16},{16,24},{24,0},{1,9},{9,17},{17,25},{25,1},{2,10},{10... | collective-permute-start | bytes 552968 | tf_op jit(solution)/shard_map/ppermute | solution.py:541
  34.2 1.2 %collective-permute-start.5 = (f32[45,8,128]{2,1,0:T(8,128)S(1)}, f32[45,8,128]{2,1,0:T(8,128)S(1)}, u32[]{:S(2)}, u32[]{:S(2)}) collective-permute-start(f32[45,8,128]{2,1,0:T(8,128)S(1)} %get-tuple-element.26), channel_id=1, source_target_pairs={{8,0},{16,8},{24,16},{0,24},{9,1},{17,9},{25,17},{1,25},{10,2},{18... | collective-permute-start | bytes 552968 | tf_op jit(solution)/shard_map/ppermute | solution.py:541
  35.3 2.9 %collective-permute-done.4.left_ref = f32[45,8,128]{2,1,0:T(8,128)S(1)} collective-permute-done((f32[45,8,128]{2,1,0:T(8,128)S(1)}, f32[45,8,128]{2,1,0:T(8,128)S(1)}, u32[]{:S(2)}, u32[]{:S(2)}) %collective-permute-start.4) | collective-permute-done | bytes 184352 | tf_op jit(solution)/shard_map/ppermute | solution.py:541
  38.2 0.8 %collective-permute-done.5.right_ref = f32[45,8,128]{2,1,0:T(8,128)S(1)} collective-permute-done((f32[45,8,128]{2,1,0:T(8,128)S(1)}, f32[45,8,128]{2,1,0:T(8,128)S(1)}, u32[]{:S(2)}, u32[]{:S(2)}) %collective-permute-start.5) | collective-permute-done | bytes 184352 | tf_op jit(solution)/shard_map/ppermute | solution.py:541
  39.1 0.1 shard_map.58
  39.2 0.1 collective-permute-start.6
  39.2 7.9 %collective-permute-start.7 = (f32[712,128]{1,0:T(8,128)S(1)}, f32[712,128]{1,0:T(8,128)S(1)}, u32[]{:S(2)}, u32[]{:S(2)}) collective-permute-start(f32[712,128]{1,0:T(8,128)S(1)} %get-tuple-element.28), channel_id=1, source_target_pairs={{0,0},{7,7},{1,2},{2,1},{3,4},{4,3},{5,6},{6,5},{8,8},{15,15},{9,1... | collective-permute-start | bytes 1093640 | tf_op jit(solution)/shard_map/ppermute | solution.py:549
  47.2 0.0 collective-permute-done.6.same_ref
  47.2 5.1 %collective-permute-done.7.cross_ref = f32[712,128]{1,0:T(8,128)S(1)} collective-permute-done((f32[712,128]{1,0:T(8,128)S(1)}, f32[712,128]{1,0:T(8,128)S(1)}, u32[]{:S(2)}, u32[]{:S(2)}) %collective-permute-start.7) | collective-permute-done | bytes 364576 | tf_op jit(solution)/shard_map/ppermute | solution.py:549
  52.3 14.8 %shard_map.59 = f32[3,16,16,128]{3,2,1,0:T(8,128)} custom-call(f32[6,24,24,128]{3,2,1,0:T(8,128)S(1)} %get-tuple-element.21.weight_ref, f32[16,16,128]{2,1,0:T(8,128)S(1)} %get-tuple-element.22.diagonal_ref, f32[3,16,16,128]{3,2,1,0:T(8,128)S(1)} %get-tuple-element.23.smoothed_ref, f32[4,8,8,128]{3,2,1,0:T(8,128)S(1)} %get-tuple-element.24.coarse_ref, ...), custom_call_target="tpu_custom_call" | custom-call | tf_op jit(solution)/shard_map/pallas_call | solution.py:601
Async XLA Ops:
  0.0 1.0 %copy-start = (f32[3,16,16,128]{3,2,1,0:T(8,128)S(1)}, f32[3,16,16,128]{3,2,1,0:T(8,128)}, u32[]{:S(2)}) copy-start(f32[3,16,16,128]{3,2,1,0:T(8,128)} %forcing_ref.5) | copy-start | bytes 1179652
  1.0 0.9 %copy-start.1 = (s32[16,16,128]{2,1,0:T(8,128)S(1)}, s32[16,16,128]{2,1,0:T(8,128)}, u32[]{:S(2)}) copy-start(s32[16,16,128]{2,1,0:T(8,128)} %phase_ref.5) | copy-start | bytes 393220
  1.9 0.7 copy-start.2
  3.2 6.4 %collective-permute-start = (f32[17,16,128]{2,1,0:T(8,128)S(1)}, f32[17,16,128]{2,1,0:T(8,128)S(1)}, u32[]{:S(2)}, u32[]{:S(2)}) collective-permute-start(f32[17,16,128]{2,1,0:T(8,128)S(1)} %get-tuple-element.17), channel_id=1, source_target_pairs={{0,8},{8,16},{16,24},{24,0},{1,9},{9,17},{17,25},{25,1},{2,10},{10... | collective-permute-start | bytes 417800 | tf_op jit(solution)/shard_map/ppermute | solution.py:541
  5.3 7.3 %collective-permute-start.1 = (f32[17,16,128]{2,1,0:T(8,128)S(1)}, f32[17,16,128]{2,1,0:T(8,128)S(1)}, u32[]{:S(2)}, u32[]{:S(2)}) collective-permute-start(f32[17,16,128]{2,1,0:T(8,128)S(1)} %get-tuple-element.18), channel_id=1, source_target_pairs={{8,0},{16,8},{24,16},{0,24},{9,1},{17,9},{25,17},{1,25},{10,2},{18... | collective-permute-start | bytes 417800 | tf_op jit(solution)/shard_map/ppermute | solution.py:541
  13.2 6.0 %collective-permute-start.2 = (f32[424,128]{1,0:T(8,128)S(1)}, f32[424,128]{1,0:T(8,128)S(1)}, u32[]{:S(2)}, u32[]{:S(2)}) collective-permute-start(f32[424,128]{1,0:T(8,128)S(1)} %get-tuple-element.19), channel_id=1, source_target_pairs={{0,1},{1,0},{2,3},{3,2},{4,5},{5,4},{6,7},{7,6},{8,9},{9,8},{10,11... | collective-permute-start | bytes 651272 | tf_op jit(solution)/shard_map/ppermute | solution.py:549
  14.8 7.2 %collective-permute-start.3 = (f32[424,128]{1,0:T(8,128)S(1)}, f32[424,128]{1,0:T(8,128)S(1)}, u32[]{:S(2)}, u32[]{:S(2)}) collective-permute-start(f32[424,128]{1,0:T(8,128)S(1)} %get-tuple-element.20), channel_id=1, source_target_pairs={{0,0},{7,7},{1,2},{2,1},{3,4},{4,3},{5,6},{6,5},{8,8},{15,15},{9,1... | collective-permute-start | bytes 651272 | tf_op jit(solution)/shard_map/ppermute | solution.py:549
  32.9 5.3 %collective-permute-start.4 = (f32[45,8,128]{2,1,0:T(8,128)S(1)}, f32[45,8,128]{2,1,0:T(8,128)S(1)}, u32[]{:S(2)}, u32[]{:S(2)}) collective-permute-start(f32[45,8,128]{2,1,0:T(8,128)S(1)} %get-tuple-element.25), channel_id=1, source_target_pairs={{0,8},{8,16},{16,24},{24,0},{1,9},{9,17},{17,25},{25,1},{2,10},{10... | collective-permute-start | bytes 552968 | tf_op jit(solution)/shard_map/ppermute | solution.py:541
  34.2 4.9 %collective-permute-start.5 = (f32[45,8,128]{2,1,0:T(8,128)S(1)}, f32[45,8,128]{2,1,0:T(8,128)S(1)}, u32[]{:S(2)}, u32[]{:S(2)}) collective-permute-start(f32[45,8,128]{2,1,0:T(8,128)S(1)} %get-tuple-element.26), channel_id=1, source_target_pairs={{8,0},{16,8},{24,16},{0,24},{9,1},{17,9},{25,17},{1,25},{10,2},{18... | collective-permute-start | bytes 552968 | tf_op jit(solution)/shard_map/ppermute | solution.py:541
  39.2 8.0 %collective-permute-start.6 = (f32[712,128]{1,0:T(8,128)S(1)}, f32[712,128]{1,0:T(8,128)S(1)}, u32[]{:S(2)}, u32[]{:S(2)}) collective-permute-start(f32[712,128]{1,0:T(8,128)S(1)} %get-tuple-element.27), channel_id=1, source_target_pairs={{0,1},{1,0},{2,3},{3,2},{4,5},{5,4},{6,7},{7,6},{8,9},{9,8},{10,11... | collective-permute-start | bytes 1093640 | tf_op jit(solution)/shard_map/ppermute | solution.py:549
  39.2 13.1 %collective-permute-start.7 = (f32[712,128]{1,0:T(8,128)S(1)}, f32[712,128]{1,0:T(8,128)S(1)}, u32[]{:S(2)}, u32[]{:S(2)}) collective-permute-start(f32[712,128]{1,0:T(8,128)S(1)} %get-tuple-element.28), channel_id=1, source_target_pairs={{0,0},{7,7},{1,2},{2,1},{3,4},{4,3},{5,6},{6,5},{8,8},{15,15},{9,1... | collective-permute-start | bytes 1093640 | tf_op jit(solution)/shard_map/ppermute | solution.py:549

commit v2 on v1

--- a/solution.py
+++ b/solution.py
@@ -105,35 +105,34 @@
         row += VISC_HALO
 
 
-def fine_steps(weight_ref, residual_ref, d_refs, constants, width):
+def fine_steps(weight_ref, base_ref, residual_ref, d_refs, constants, width, finish):
     first_scale, carried, scaled = constants
     parts, rows = residual_ref.shape[0], residual_ref.shape[2]
-    mid = pl.ds(ROW0, rows)
-
-    def start(x, _):
-        for c in range(parts):
-            d_refs[0][c, x, mid, :] = first_scale * residual_ref[c, x]
-        return 0
-
-    lax.fori_loop(0, width, start, 0)
     for number in range(CHEB):
-        old, new = d_refs[number % 2], d_refs[(number + 1) % 2]
-
-        def step(x, _, number=number, old=old, new=new):
-            weights = [weight_ref[f, x] for f in range(6)]
+        old = base_ref if number == 0 else d_refs[number % 2]
+        new = d_refs[(number + 1) % 2]
+        last = number + 1 == CHEB
+        skip, count = (HALO, rows - 2 * HALO) if last else (0, rows)
+        inner = pl.ds(skip, count)
+        for x in range(number + 1, width - 1 - number):
+            weights = [weight_ref[f, x, inner, :] for f in range(6)]
             for c in range(parts):
-                own = old[c, x, mid, :]
-                beside = weights[0] * old[c, x - 1, mid, :] + weights[1] * old[c, x + 1, mid, :]
-                beside = beside + weights[2] * old[c, x, pl.ds(ROW0 - 1, rows), :]
-                beside = beside + weights[3] * old[c, x, pl.ds(ROW0 + 1, rows), :]
+                own = old[c, x, pl.ds(ROW0 + skip, count), :]
+                beside = weights[0] * old[c, x - 1, pl.ds(ROW0 + skip, count), :]
+                beside = beside + weights[1] * old[c, x + 1, pl.ds(ROW0 + skip, count), :]
+                beside = beside + weights[2] * old[c, x, pl.ds(ROW0 + skip - 1, count), :]
+                beside = beside + weights[3] * old[c, x, pl.ds(ROW0 + skip + 1, count), :]
                 beside = beside + weights[4] * below(own) + weights[5] * above(own)
-                fresh = residual_ref[c, x] - own + beside
-                residual_ref[c, x] = fresh
-                if number + 1 < CHEB:
-                    new[c, x, mid, :] = carried[number] * own + scaled[number] * fresh
-            return 0
-
-        lax.fori_loop(number + 1, width - 1 - number, step, 0)
+                if number == 0:
+                    fresh = own - first_scale * (own - beside)
+                    own = first_scale * own
+                else:
+                    fresh = residual_ref[c, x, inner, :] - own + beside
+                if last:
+                    finish(c, x, fresh)
+                else:
+                    residual_ref[c, x] = fresh
+                    new[c, x, pl.ds(ROW0, rows), :] = carried[number] * own + scaled[number] * fresh
 
 
 def clear_rims(ref, rows):
@@ -149,7 +148,7 @@
     shape_y,
     forcing_ref, phase_ref, table_ref, lower_ref, upper_ref, left_ref, right_ref, same_ref, cross_ref,
     weight_ref, diagonal_ref, smoothed_ref, coarse_ref, low_ref, high_ref,
-    visc_ref, inverse_ref, residual_ref, d0_ref, d1_ref, pair_ref, row_ref,
+    visc_ref, inverse_ref, residual_ref, base_ref, d0_ref, d1_ref, pair_ref, row_ref,
 ):
     parts, nx, ny, depth = forcing_ref.shape
     width, rows = nx + 2 * HALO, ny + 2 * HALO
@@ -190,7 +189,7 @@
 
     lane = lanes(rows, depth)
 
-    def weigh(x, _):
+    for x in range(width):
         centre = visc_ref[x + 1, pl.ds(1, rows), :]
         halved = 0.5 * centre
         z_below = jnp.where(lane == 0, 0.0, below(halved))
@@ -211,12 +210,9 @@
         weight_ref[4, x] = jnp.where(lane == 0, 0.0, faces[4] * inverse)
         weight_ref[5, x] = jnp.where(lane == depth - 1, 0.0, faces[5] * inverse)
         inverse_ref[x] = inverse
-        pair_ref[x] = diagonal
-        return 0
-
-    lax.fori_loop(0, width, weigh, 0)
-    for x in range(nx):
-        diagonal_ref[x] = pair_ref[x + HALO, pl.ds(HALO, ny), :]
+        if HALO <= x < HALO + nx:
+            pair_ref[...] = diagonal
+            diagonal_ref[x - HALO] = pair_ref[pl.ds(HALO, ny), :]
 
     for c in range(parts):
         for i in range(width):
@@ -228,15 +224,20 @@
             else:
                 own = right_ref[c * HALO + x - nx]
             at = (c * width + i) * HALO
-            residual_ref[c, i, pl.ds(HALO, ny), :] = own * inverse_ref[i, pl.ds(HALO, ny), :]
-            residual_ref[c, i, pl.ds(0, HALO), :] = low_rows(at, HALO) * inverse_ref[i, pl.ds(0, HALO), :]
-            residual_ref[c, i, pl.ds(HALO + ny, HALO), :] = (
+            base_ref[c, i, pl.ds(ROW0 + HALO, ny), :] = own * inverse_ref[i, pl.ds(HALO, ny), :]
+            base_ref[c, i, pl.ds(ROW0, HALO), :] = low_rows(at, HALO) * inverse_ref[i, pl.ds(0, HALO), :]
+            base_ref[c, i, pl.ds(ROW0 + HALO + ny, HALO), :] = (
                 high_rows(at, HALO) * inverse_ref[i, pl.ds(HALO + ny, HALO), :]
             )
 
-    clear_rims(d0_ref, rows)
-    clear_rims(d1_ref, rows)
-    fine_steps(weight_ref, residual_ref, (d0_ref, d1_ref), constants_of(lower_ref, upper_ref), width)
+    for ref in (base_ref, d0_ref, d1_ref):
+        clear_rims(ref, rows)
+
+    def finish(c, x, value):
+        smoothed_ref[c, x - HALO] = value
+
+    constants = constants_of(lower_ref, upper_ref)
+    fine_steps(weight_ref, base_ref, residual_ref, (d0_ref, d1_ref), constants, width, finish)
 
     half = ny // 2
     even_own = lanes(ny, depth) % 2 == 0
@@ -278,7 +279,7 @@
         for c in range(parts):
             total = 0.0
             for x in (2 * i, 2 * i + 1):
-                total = total + residual_ref[c, x + HALO, pl.ds(HALO, ny), :] * diagonal_ref[x]
+                total = total + smoothed_ref[c, x] * diagonal_ref[x]
             sources.append(y_sum(z_pair(total, even_own), 3 + c) * (4.0 * inverse))
         faces = [upper_x * (1.0 / 32.0), upper_y * (1.0 / 32.0), upper_z * (1.0 / 32.0)]
         coarse_ref[0, i] = jnp.where(even, sources[0], sources[1])
@@ -286,10 +287,6 @@
         coarse_ref[2, i] = jnp.where(even, faces[1], faces[2])
         if i % 2 == 1:
             coarse_ref[3, i // 2] = jnp.where(even, inverses[i - 1], inverses[i])
-
-    for c in range(parts):
-        for x in range(nx):
-            smoothed_ref[c, x] = residual_ref[c, x + HALO, pl.ds(HALO, ny), :]
 
     at = 0
     ncx = nx // 2
@@ -362,7 +359,7 @@
     shape_y,
     weight_ref, diagonal_ref, smoothed_ref, coarse_ref, lower_ref, upper_ref, left_ref, right_ref, same_ref, cross_ref,
     out_ref,
-    field_ref, cweight_ref, source_ref, cd0_ref, cd1_ref, correction_ref, prolonged_ref, residual_ref, d0_ref, d1_ref,
+    field_ref, cweight_ref, source_ref, cd0_ref, cd1_ref, correction_ref, prolonged_ref, residual_ref, base_ref, d0_ref, d1_ref,
 ):
     parts, nx, ny, depth = smoothed_ref.shape
     width, rows = nx + 2 * HALO, ny + 2 * HALO
@@ -458,18 +455,15 @@
     clear_rims(cd0_ref, srows)
     clear_rims(cd1_ref, srows)
 
-    def start(i, _):
+    for i in range(cwidth):
         for s in range(2):
             value = first_scale * source_ref[s, i]
             cd0_ref[s, i, mid, :] = value
             correction_ref[s, i] = value
-        return 0
-
-    lax.fori_loop(0, cwidth, start, 0)
     for number in range(COARSE_STEPS - 1):
         old, new = ((cd0_ref, cd1_ref), (cd1_ref, cd0_ref))[number % 2]
-
-        def step(i, _, number=number, old=old, new=new):
+        last = number + 2 == COARSE_STEPS
+        for i in range(number + 1, cwidth - 1 - number):
             weights = [cweight_ref[f, i] for f in range(6)]
             for s in range(2):
                 own = old[s, i, mid, :]
@@ -478,13 +472,11 @@
                 beside = beside + weights[3] * old[s, i, pl.ds(ROW0 + 1, srows), :]
                 beside = beside + weights[4] * below(own, 2) + weights[5] * above(own, 2)
                 fresh = source_ref[s, i] - own + beside
-                source_ref[s, i] = fresh
                 direction = carried[number] * own + scaled[number] * fresh
-                new[s, i, mid, :] = direction
+                if not last:
+                    source_ref[s, i] = fresh
+                    new[s, i, mid, :] = direction
                 correction_ref[s, i] = correction_ref[s, i] + direction
-            return 0
-
-        lax.fori_loop(number + 1, cwidth - 1 - number, step, 0)
 
     edge = COARSE_HALO - COARSE_REACH
     pwidth, prows = ncx + 2 * COARSE_REACH, half + 2 * COARSE_REACH
@@ -513,14 +505,15 @@
             beside = beside + weights[2] * prolonged_ref[c, at, pl.ds(ROW0 - 1, rows), :]
             beside = beside + weights[3] * prolonged_ref[c, at, pl.ds(ROW0 + 1, rows), :]
             beside = beside + weights[4] * below(own) + weights[5] * above(own)
-            residual_ref[c, i] = residual_ref[c, i] - own + beside
-
-    clear_rims(d0_ref, rows)
-    clear_rims(d1_ref, rows)
-    fine_steps(weight_ref, residual_ref, (d0_ref, d1_ref), constants, width)
-    for c in range(parts):
-        for x in range(nx):
-            out_ref[c, x] = residual_ref[c, x + HALO, pl.ds(HALO, ny), :] * diagonal_ref[x]
+            base_ref[c, i, fine, :] = residual_ref[c, i] - own + beside
+
+    for ref in (base_ref, d0_ref, d1_ref):
+        clear_rims(ref, rows)
+
+    def finish(c, x, value):
+        out_ref[c, x - HALO] = value * diagonal_ref[x - HALO]
+
+    fine_steps(weight_ref, base_ref, residual_ref, (d0_ref, d1_ref), constants, width, finish)
 
 
 def call(kernel, outs, scratch, specs):
@@ -585,7 +578,8 @@
             (parts, width, rows, depth),
             fine_d,
             fine_d,
-            (width, rows, depth),
+            fine_d,
+            (rows, depth),
             (6, up_to(ny + 2, 8), depth),
         ],
         [vmem, vmem, smem, smem, smem, vmem, vmem, vmem, vmem],
@@ -612,6 +606,7 @@
             (parts, width, rows, depth),
             fine_d,
             fine_d,
+            fine_d,
         ],
         [vmem, vmem, vmem, vmem, smem, smem, vmem, vmem, vmem, vmem],
     )(weight, diagonal, smoothed, coarse, lower_bound, upper_bound, left, right, same, cross)

time: 67.4 us -> 50.9 us (0.76)
  Pallas kernels: 27.1 us -> 10.7 us
    pallas_call x1, Pallas kernels: 14.8 us -> 5.71 us  [local(): call(functools.partial(post_kernel, shape_x, shape_y), [(parts, nx, ny, d...]
    pallas_call x1, Pallas kernels: 10.9 us -> 3.58 us  [local(): call(functools.partial(pre_kernel, shape_x, shape_y), [(6, width, rows, d...]
where the time goes in v2:
time: 50.9 us; the launch traced here: 50.7 us
  starting transfers between devices  18.2 us (36%)
  waiting for transfers between devices  17.9 us (35%)
  Pallas kernels  10.7 us (21%)
  local copies, waits for them, and re-layouts  2.55 us (5%)
  between operations  1.37 us (3%)
    ppermute x4, starting transfers between devices, swap_y(): return (lax.ppermute(same, 'gy', pairs), lax.ppermute(cross, 'gy', others))  12.7 us
    ppermute x4, waiting for transfers between devices, ring_x(): return (lax.ppermute(high, 'gx', up), lax.ppermute(low, 'gx', down))  10 us
    ppermute x4, waiting for transfers between devices, swap_y(): return (lax.ppermute(same, 'gy', pairs), lax.ppermute(cross, 'gy', others))  7.91 us
    pallas_call x1, Pallas kernels, local(): call(functools.partial(post_kernel, shape_x, shape_y), [(parts, nx, ny, d...  5.71 us
    ppermute x4, starting transfers between devices, ring_x(): return (lax.ppermute(high, 'gx', up), lax.ppermute(low, 'gx', down))  5.53 us
    pallas_call x1, Pallas kernels, local(): call(functools.partial(pre_kernel, shape_x, shape_y), [(6, width, rows, d...  3.58 us
    unnamed x6, local copies, waits for them, and re-layouts  2.55 us
  transfers between devices with their start and end apart: 8, of which 6 were waited for; matrix products, arithmetic and copies ran while one was open for 0% of the time, Pallas kernels for 0%

profile of v2, /device:TPU:1, one launch (start us, length us, event | category | flops | bytes accessed | tf_op | source)
XLA Modules:
  0.0 50.7 jit_solution(17354045834808889471)
XLA Ops:
  0.0 0.0 copy-start
  0.0 1.0 %copy-done = f32[3,16,16,128]{3,2,1,0:T(8,128)S(1)} copy-done((f32[3,16,16,128]{3,2,1,0:T(8,128)S(1)}, f32[3,16,16,128]{3,2,1,0:T(8,128)}, u32[]{:S(2)}) %copy-start) | copy-done | bytes 393240
  1.0 0.0 copy-start.1
  1.0 0.9 %copy-done.1 = s32[16,16,128]{2,1,0:T(8,128)S(1)} copy-done((s32[16,16,128]{2,1,0:T(8,128)S(1)}, s32[16,16,128]{2,1,0:T(8,128)}, u32[]{:S(2)}) %copy-start.1) | copy-done | bytes 131096
  1.9 0.0 copy-start.2
  1.9 0.7 %copy-done.2 = f32[8]{0:T(128)S(1)} copy-done((f32[8]{0:T(128)S(1)}, f32[8]{0:T(128)}, u32[]{:S(2)}) %copy-start.2) | copy-done | bytes 56
  2.6 0.6 %shard_map.55 = (f32[17,16,128]{2,1,0:T(8,128)S(1)}, f32[17,16,128]{2,1,0:T(8,128)S(1)}) custom-call(f32[3,16,16,128]{3,2,1,0:T(8,128)S(1)} %copy-done, s32[16,16,128]{2,1,0:T(8,128)S(1)} %copy-done.1, f32[8]{0:T(128)S(1)} %copy-done.2), custom_call_target="tpu_custom_call" | custom-call | tf_op jit(solution)/shard_map/pallas_call | solution.py:559
  3.2 2.1 %collective-permute-start = (f32[17,16,128]{2,1,0:T(8,128)S(1)}, f32[17,16,128]{2,1,0:T(8,128)S(1)}, u32[]{:S(2)}, u32[]{:S(2)}) collective-permute-start(f32[17,16,128]{2,1,0:T(8,128)S(1)} %get-tuple-element.17), channel_id=1, source_target_pairs={{0,8},{8,16},{16,24},{24,0},{1,9},{9,17},{17,25},{25,1},{2,10},{10... | collective-permute-start | bytes 417800 | tf_op jit(solution)/shard_map/ppermute | solution.py:534
  5.3 1.0 %collective-permute-start.1 = (f32[17,16,128]{2,1,0:T(8,128)S(1)}, f32[17,16,128]{2,1,0:T(8,128)S(1)}, u32[]{:S(2)}, u32[]{:S(2)}) collective-permute-start(f32[17,16,128]{2,1,0:T(8,128)S(1)} %get-tuple-element.18), channel_id=1, source_target_pairs={{8,0},{16,8},{24,16},{0,24},{9,1},{17,9},{25,17},{1,25},{10,2},{18... | collective-permute-start | bytes 417800 | tf_op jit(solution)/shard_map/ppermute | solution.py:534
  6.3 3.3 %collective-permute-done.left_ref = f32[17,16,128]{2,1,0:T(8,128)S(1)} collective-permute-done((f32[17,16,128]{2,1,0:T(8,128)S(1)}, f32[17,16,128]{2,1,0:T(8,128)S(1)}, u32[]{:S(2)}, u32[]{:S(2)}) %collective-permute-start) | collective-permute-done | bytes 139296 | tf_op jit(solution)/shard_map/ppermute | solution.py:534
  9.6 2.9 %collective-permute-done.1.right_ref = f32[17,16,128]{2,1,0:T(8,128)S(1)} collective-permute-done((f32[17,16,128]{2,1,0:T(8,128)S(1)}, f32[17,16,128]{2,1,0:T(8,128)S(1)}, u32[]{:S(2)}, u32[]{:S(2)}) %collective-permute-start.1) | collective-permute-done | bytes 139296 | tf_op jit(solution)/shard_map/ppermute | solution.py:534
  12.5 0.7 %shard_map.56 = (f32[424,128]{1,0:T(8,128)S(1)}, f32[424,128]{1,0:T(8,128)S(1)}) custom-call(f32[3,16,16,128]{3,2,1,0:T(8,128)S(1)} %copy-done, s32[16,16,128]{2,1,0:T(8,128)S(1)} %copy-done.1, f32[8]{0:T(128)S(1)} %copy-done.2, f32[17,16,128]{2,1,0:T(8,128)S(1)} %collective-permute-done.left_ref, f32[17,16,128]{2,1,0:T(8,128)S(1)} %collective-permute-done.1.right_ref), custom_call_target="tpu_custom_call" | custom-call | tf_op jit(solution)/shard_map/pallas_call | solution.py:564
  13.2 1.6 %collective-permute-start.2 = (f32[424,128]{1,0:T(8,128)S(1)}, f32[424,128]{1,0:T(8,128)S(1)}, u32[]{:S(2)}, u32[]{:S(2)}) collective-permute-start(f32[424,128]{1,0:T(8,128)S(1)} %get-tuple-element.19), channel_id=1, source_target_pairs={{0,1},{1,0},{2,3},{3,2},{4,5},{5,4},{6,7},{7,6},{8,9},{9,8},{10,11... | collective-permute-start | bytes 651272 | tf_op jit(solution)/shard_map/ppermute | solution.py:542
  14.8 3.1 %collective-permute-start.3 = (f32[424,128]{1,0:T(8,128)S(1)}, f32[424,128]{1,0:T(8,128)S(1)}, u32[]{:S(2)}, u32[]{:S(2)}) collective-permute-start(f32[424,128]{1,0:T(8,128)S(1)} %get-tuple-element.20), channel_id=1, source_target_pairs={{0,0},{7,7},{1,2},{2,1},{3,4},{4,3},{5,6},{6,5},{8,8},{15,15},{9,1... | collective-permute-start | bytes 651272 | tf_op jit(solution)/shard_map/ppermute | solution.py:542
  19.2 0.0 collective-permute-done.2.same_ref
  19.2 2.8 %collective-permute-done.3.cross_ref = f32[424,128]{1,0:T(8,128)S(1)} collective-permute-done((f32[424,128]{1,0:T(8,128)S(1)}, f32[424,128]{1,0:T(8,128)S(1)}, u32[]{:S(2)}, u32[]{:S(2)}) %collective-permute-start.3) | collective-permute-done | bytes 217120 | tf_op jit(solution)/shard_map/ppermute | solution.py:542
  22.0 3.6 %shard_map.57 = (f32[6,24,24,128]{3,2,1,0:T(8,128)S(1)}, f32[16,16,128]{2,1,0:T(8,128)S(1)}, f32[3,16,16,128]{3,2,1,0:T(8,128)S(1)}, f32[4,8,8,128]{3,2,1,0:T(8,...) custom-call(f32[3,16,16,128]{3,2,1,0:T(8,128)S(1)} %copy-done, s32[16,16,128]{2,1,0:T(8,128)S(1)} %copy-done.1, ...), custom_call_target="tpu_custom_call" | custom-call | tf_op jit(solution)/shard_map/pallas_call | solution.py:572
  25.6 1.3 %collective-permute-start.4 = (f32[45,8,128]{2,1,0:T(8,128)S(1)}, f32[45,8,128]{2,1,0:T(8,128)S(1)}, u32[]{:S(2)}, u32[]{:S(2)}) collective-permute-start(f32[45,8,128]{2,1,0:T(8,128)S(1)} %get-tuple-element.25), channel_id=1, source_target_pairs={{0,8},{8,16},{16,24},{24,0},{1,9},{9,17},{17,25},{25,1},{2,10},{10... | collective-permute-start | bytes 552968 | tf_op jit(solution)/shard_map/ppermute | solution.py:534
  26.9 1.2 %collective-permute-start.5 = (f32[45,8,128]{2,1,0:T(8,128)S(1)}, f32[45,8,128]{2,1,0:T(8,128)S(1)}, u32[]{:S(2)}, u32[]{:S(2)}) collective-permute-start(f32[45,8,128]{2,1,0:T(8,128)S(1)} %get-tuple-element.26), channel_id=1, source_target_pairs={{8,0},{16,8},{24,16},{0,24},{9,1},{17,9},{25,17},{1,25},{10,2},{18... | collective-permute-start | bytes 552968 | tf_op jit(solution)/shard_map/ppermute | solution.py:534
  28.0 2.9 %collective-permute-done.4.left_ref = f32[45,8,128]{2,1,0:T(8,128)S(1)} collective-permute-done((f32[45,8,128]{2,1,0:T(8,128)S(1)}, f32[45,8,128]{2,1,0:T(8,128)S(1)}, u32[]{:S(2)}, u32[]{:S(2)}) %collective-permute-start.4) | collective-permute-done | bytes 184352 | tf_op jit(solution)/shard_map/ppermute | solution.py:534
  30.9 0.8 %collective-permute-done.5.right_ref = f32[45,8,128]{2,1,0:T(8,128)S(1)} collective-permute-done((f32[45,8,128]{2,1,0:T(8,128)S(1)}, f32[45,8,128]{2,1,0:T(8,128)S(1)}, u32[]{:S(2)}, u32[]{:S(2)}) %collective-permute-start.5) | collective-permute-done | bytes 184352 | tf_op jit(solution)/shard_map/ppermute | solution.py:534
  31.8 0.1 shard_map.58
  31.9 0.1 collective-permute-start.6
  31.9 7.9 %collective-permute-start.7 = (f32[712,128]{1,0:T(8,128)S(1)}, f32[712,128]{1,0:T(8,128)S(1)}, u32[]{:S(2)}, u32[]{:S(2)}) collective-permute-start(f32[712,128]{1,0:T(8,128)S(1)} %get-tuple-element.28), channel_id=1, source_target_pairs={{0,0},{7,7},{1,2},{2,1},{3,4},{4,3},{5,6},{6,5},{8,8},{15,15},{9,1... | collective-permute-start | bytes 1093640 | tf_op jit(solution)/shard_map/ppermute | solution.py:542
  39.9 0.0 collective-permute-done.6.same_ref
  39.9 5.1 %collective-permute-done.7.cross_ref = f32[712,128]{1,0:T(8,128)S(1)} collective-permute-done((f32[712,128]{1,0:T(8,128)S(1)}, f32[712,128]{1,0:T(8,128)S(1)}, u32[]{:S(2)}, u32[]{:S(2)}) %collective-permute-start.7) | collective-permute-done | bytes 364576 | tf_op jit(solution)/shard_map/ppermute | solution.py:542
  45.0 5.7 %shard_map.59 = f32[3,16,16,128]{3,2,1,0:T(8,128)} custom-call(f32[6,24,24,128]{3,2,1,0:T(8,128)S(1)} %get-tuple-element.21.weight_ref, f32[16,16,128]{2,1,0:T(8,128)S(1)} %get-tuple-element.22.diagonal_ref, f32[3,16,16,128]{3,2,1,0:T(8,128)S(1)} %get-tuple-element.23.smoothed_ref, f32[4,8,8,128]{3,2,1,0:T(8,128)S(1)} %get-tuple-element.24.coarse_ref, ...), custom_call_target="tpu_custom_call" | custom-call | tf_op jit(solution)/shard_map/pallas_call | solution.py:595
Async XLA Ops:
  0.0 1.0 %copy-start = (f32[3,16,16,128]{3,2,1,0:T(8,128)S(1)}, f32[3,16,16,128]{3,2,1,0:T(8,128)}, u32[]{:S(2)}) copy-start(f32[3,16,16,128]{3,2,1,0:T(8,128)} %forcing_ref.5) | copy-start | bytes 1179652
  1.0 0.9 %copy-start.1 = (s32[16,16,128]{2,1,0:T(8,128)S(1)}, s32[16,16,128]{2,1,0:T(8,128)}, u32[]{:S(2)}) copy-start(s32[16,16,128]{2,1,0:T(8,128)} %phase_ref.5) | copy-start | bytes 393220
  1.9 0.7 %copy-start.2 = (f32[8]{0:T(128)S(1)}, f32[8]{0:T(128)}, u32[]{:S(2)}) copy-start(f32[8]{0:T(128)} %table_ref.5) | copy-start | bytes 100
  3.2 6.4 %collective-permute-start = (f32[17,16,128]{2,1,0:T(8,128)S(1)}, f32[17,16,128]{2,1,0:T(8,128)S(1)}, u32[]{:S(2)}, u32[]{:S(2)}) collective-permute-start(f32[17,16,128]{2,1,0:T(8,128)S(1)} %get-tuple-element.17), channel_id=1, source_target_pairs={{0,8},{8,16},{16,24},{24,0},{1,9},{9,17},{17,25},{25,1},{2,10},{10... | collective-permute-start | bytes 417800 | tf_op jit(solution)/shard_map/ppermute | solution.py:534
  5.3 7.3 %collective-permute-start.1 = (f32[17,16,128]{2,1,0:T(8,128)S(1)}, f32[17,16,128]{2,1,0:T(8,128)S(1)}, u32[]{:S(2)}, u32[]{:S(2)}) collective-permute-start(f32[17,16,128]{2,1,0:T(8,128)S(1)} %get-tuple-element.18), channel_id=1, source_target_pairs={{8,0},{16,8},{24,16},{0,24},{9,1},{17,9},{25,17},{1,25},{10,2},{18... | collective-permute-start | bytes 417800 | tf_op jit(solution)/shard_map/ppermute | solution.py:534
  13.2 6.0 %collective-permute-start.2 = (f32[424,128]{1,0:T(8,128)S(1)}, f32[424,128]{1,0:T(8,128)S(1)}, u32[]{:S(2)}, u32[]{:S(2)}) collective-permute-start(f32[424,128]{1,0:T(8,128)S(1)} %get-tuple-element.19), channel_id=1, source_target_pairs={{0,1},{1,0},{2,3},{3,2},{4,5},{5,4},{6,7},{7,6},{8,9},{9,8},{10,11... | collective-permute-start | bytes 651272 | tf_op jit(solution)/shard_map/ppermute | solution.py:542
  14.8 7.2 %collective-permute-start.3 = (f32[424,128]{1,0:T(8,128)S(1)}, f32[424,128]{1,0:T(8,128)S(1)}, u32[]{:S(2)}, u32[]{:S(2)}) collective-permute-start(f32[424,128]{1,0:T(8,128)S(1)} %get-tuple-element.20), channel_id=1, source_target_pairs={{0,0},{7,7},{1,2},{2,1},{3,4},{4,3},{5,6},{6,5},{8,8},{15,15},{9,1... | collective-permute-start | bytes 651272 | tf_op jit(solution)/shard_map/ppermute | solution.py:542
  25.6 5.3 %collective-permute-start.4 = (f32[45,8,128]{2,1,0:T(8,128)S(1)}, f32[45,8,128]{2,1,0:T(8,128)S(1)}, u32[]{:S(2)}, u32[]{:S(2)}) collective-permute-start(f32[45,8,128]{2,1,0:T(8,128)S(1)} %get-tuple-element.25), channel_id=1, source_target_pairs={{0,8},{8,16},{16,24},{24,0},{1,9},{9,17},{17,25},{25,1},{2,10},{10... | collective-permute-start | bytes 552968 | tf_op jit(solution)/shard_map/ppermute | solution.py:534
  26.9 4.9 %collective-permute-start.5 = (f32[45,8,128]{2,1,0:T(8,128)S(1)}, f32[45,8,128]{2,1,0:T(8,128)S(1)}, u32[]{:S(2)}, u32[]{:S(2)}) collective-permute-start(f32[45,8,128]{2,1,0:T(8,128)S(1)} %get-tuple-element.26), channel_id=1, source_target_pairs={{8,0},{16,8},{24,16},{0,24},{9,1},{17,9},{25,17},{1,25},{10,2},{18... | collective-permute-start | bytes 552968 | tf_op jit(solution)/shard_map/ppermute | solution.py:534
  31.9 8.0 %collective-permute-start.6 = (f32[712,128]{1,0:T(8,128)S(1)}, f32[712,128]{1,0:T(8,128)S(1)}, u32[]{:S(2)}, u32[]{:S(2)}) collective-permute-start(f32[712,128]{1,0:T(8,128)S(1)} %get-tuple-element.27), channel_id=1, source_target_pairs={{0,1},{1,0},{2,3},{3,2},{4,5},{5,4},{6,7},{7,6},{8,9},{9,8},{10,11... | collective-permute-start | bytes 1093640 | tf_op jit(solution)/shard_map/ppermute | solution.py:542
  31.9 13.1 %collective-permute-start.7 = (f32[712,128]{1,0:T(8,128)S(1)}, f32[712,128]{1,0:T(8,128)S(1)}, u32[]{:S(2)}, u32[]{:S(2)}) collective-permute-start(f32[712,128]{1,0:T(8,128)S(1)} %get-tuple-element.28), channel_id=1, source_target_pairs={{0,0},{7,7},{1,2},{2,1},{3,4},{4,3},{5,6},{6,5},{8,8},{15,15},{9,1... | collective-permute-start | bytes 1093640 | tf_op jit(solution)/shard_map/ppermute | solution.py:542

commit v3 on v2

--- a/solution.py
+++ b/solution.py
@@ -61,48 +61,118 @@
     return lax.rem(lax.axis_index(axis), 2) == 1
 
 
-def pack_x_kernel(forcing_ref, phase_ref, table_ref, low_ref, high_ref):
+def pack_x_kernel(forcing_ref, phase_ref, table_ref, low_ref, high_ref, phases_ref, rows_ref, sems):
     parts, nx = forcing_ref.shape[:2]
-    for c in range(parts):
-        for i in range(HALO):
-            low_ref[c * HALO + i] = forcing_ref[c, i]
-            high_ref[c * HALO + i] = forcing_ref[c, nx - HALO + i]
-    for i in range(VISC_HALO):
-        low_ref[parts * HALO + i] = lookup(table_ref, phase_ref[i])
-        high_ref[parts * HALO + i] = lookup(table_ref, phase_ref[nx - VISC_HALO + i])
-
-
-def pack_y_kernel(forcing_ref, phase_ref, table_ref, left_ref, right_ref, same_ref, cross_ref):
-    parts, nx, ny = forcing_ref.shape[:3]
+    base = parts * HALO
+    sides = ((low_ref, 0, 0), (high_ref, nx - HALO, nx - VISC_HALO))
+    first_copies, copies = [pltpu.make_async_copy(table_ref, rows_ref, sems.at[2, 0])], []
+    for s, (ref, x, visc_x) in enumerate(sides):
+        source = phase_ref.at[pl.ds(visc_x, VISC_HALO)]
+        first_copies.append(pltpu.make_async_copy(source, phases_ref.at[s], sems.at[s, parts]))
+        for c in range(parts):
+            source, target = forcing_ref.at[c, pl.ds(x, HALO)], ref.at[pl.ds(c * HALO, HALO)]
+            copies.append(pltpu.make_async_copy(source, target, sems.at[s, c]))
+    for copy in first_copies + copies:
+        copy.start()
+    for copy in first_copies:
+        copy.wait()
+    for s, (ref, _, _) in enumerate(sides):
+        for i in range(VISC_HALO):
+            ref[base + i] = lookup(rows_ref, phases_ref[s, i])
+    for copy in copies:
+        copy.wait()
+
+
+def stage_kernel(forcing_ref, phase_ref, table_ref, here_ref, visc_ref, phases_ref, rows_ref, sems):
+    first_copies = [
+        pltpu.make_async_copy(table_ref, rows_ref, sems.at[0]),
+        pltpu.make_async_copy(phase_ref, phases_ref, sems.at[1]),
+    ]
+    copy = pltpu.make_async_copy(forcing_ref, here_ref, sems.at[2])
+    for each in first_copies + [copy]:
+        each.start()
+    for each in first_copies:
+        each.wait()
+    for x in range(phase_ref.shape[0]):
+        visc_ref[x] = lookup(rows_ref, phases_ref[x])
+    copy.wait()
+
+
+def row_plan(length, halo, shared=1):
+    plan, row = [], 0
+    for start in range(-halo, length + halo, shared):
+        away = min(max(-x, x - length + 1, 0) for x in range(start, start + shared))
+        plan.append((start, row, halo - away))
+        row += halo - away
+    return plan, row
+
+
+def place(plane, first, inner, halo, own, low, high):
+    count = low.shape[0] if low is not None else 0
+    plane(first + halo, own)
+    if count:
+        plane(first + halo - count, low)
+        plane(first + halo + inner, high)
+    if count < halo:
+        empty = jnp.zeros((halo - count, own.shape[1]), jnp.float32)
+        plane(first, empty)
+        plane(first + halo + inner + count, empty)
+
+
+def writer(ref, *at):
+    def store(row, value):
+        ref[at + (pl.ds(row, value.shape[0]), slice(None))] = value
+
+    return store
+
+
+def message_reader(same_ref, cross_ref):
     odd = is_odd("gy")
 
-    def put(row, low, high):
-        count = low.shape[0]
+    def low_and_high(row, count):
+        if count == 0:
+            return None, None
+        same, cross = same_ref[pl.ds(row, count), :], cross_ref[pl.ds(row, count), :]
+        return jnp.where(odd, same, cross), jnp.where(odd, cross, same)
+
+    return low_and_high
+
+
+def message_writer(same_ref, cross_ref):
+    odd = is_odd("gy")
+
+    def put(row, count, ref, at, ref_high=None, at_high=None):
+        if count == 0:
+            return
+        ref_high, at_high = (ref, at) if ref_high is None else (ref_high, at_high)
+        length = ref_high.shape[-2]
+        low = ref[at + (pl.ds(0, count), slice(None))]
+        high = ref_high[at_high + (pl.ds(length - count, count), slice(None))]
         same_ref[pl.ds(row, count), :] = jnp.where(odd, low, high)
         cross_ref[pl.ds(row, count), :] = jnp.where(odd, high, low)
 
-    row = 0
+    return put
+
+
+def pack_y_kernel(forcing_ref, visc_ref, left_ref, right_ref, same_ref, cross_ref):
+    parts, nx = forcing_ref.shape[:2]
+    put = message_writer(same_ref, cross_ref)
+    plan, total = row_plan(nx, HALO)
     for c in range(parts):
-        for x in range(-HALO, nx + HALO):
+        for x, row, count in plan:
             if x < 0:
-                ref, at = left_ref, (c * HALO + x + HALO,)
+                put(c * total + row, count, left_ref, (c * HALO + x + HALO,))
             elif x < nx:
-                ref, at = forcing_ref, (c, x)
+                put(c * total + row, count, forcing_ref, (c, x))
             else:
-                ref, at = right_ref, (c * HALO + x - nx,)
-            put(row, ref[at + (slice(0, HALO),)], ref[at + (slice(ny - HALO, ny),)])
-            row += HALO
-    for x in range(-VISC_HALO, nx + VISC_HALO):
-        first, last = slice(0, VISC_HALO), slice(ny - VISC_HALO, ny)
+                put(c * total + row, count, right_ref, (c * HALO + x - nx,))
+    for x, row, count in row_plan(nx, VISC_HALO)[0]:
         if x < 0:
-            at = parts * HALO + x + VISC_HALO
-            put(row, left_ref[at, first], left_ref[at, last])
+            put(parts * total + row, count, left_ref, (parts * HALO + x + VISC_HALO,))
         elif x < nx:
-            put(row, lookup(table_ref, phase_ref[x, first]), lookup(table_ref, phase_ref[x, last]))
+            put(parts * total + row, count, visc_ref, (x,))
         else:
-            at = parts * HALO + x - nx
-            put(row, right_ref[at, first], right_ref[at, last])
-        row += VISC_HALO
+            put(parts * total + row, count, right_ref, (parts * HALO + x - nx,))
 
 
 def fine_steps(weight_ref, base_ref, residual_ref, d_refs, constants, width, finish):
@@ -135,57 +205,43 @@
                     new[c, x, pl.ds(ROW0, rows), :] = carried[number] * own + scaled[number] * fresh
 
 
-def clear_rims(ref, rows):
-    planes = ref.shape[1]
-    for c in range(ref.shape[0]):
-        for x in range(planes):
-            ref[c, x, pl.ds(0, ROW0), :] = jnp.zeros((ROW0, ref.shape[3]), jnp.float32)
-            ref[c, x, pl.ds(ROW0 + rows, ROW0), :] = jnp.zeros((ROW0, ref.shape[3]), jnp.float32)
+def masked(inside, has_low, has_high, own, low, high):
+    if inside is not None:
+        own = jnp.where(inside, own, 0.0)
+        has_low, has_high = jnp.logical_and(has_low, inside), jnp.logical_and(has_high, inside)
+    if low is not None:
+        low, high = jnp.where(has_low, low, 0.0), jnp.where(has_high, high, 0.0)
+    return own, low, high
 
 
 def pre_kernel(
     shape_x,
     shape_y,
-    forcing_ref, phase_ref, table_ref, lower_ref, upper_ref, left_ref, right_ref, same_ref, cross_ref,
+    forcing_ref, own_visc_ref, lower_ref, upper_ref, left_ref, right_ref, same_ref, cross_ref,
     weight_ref, diagonal_ref, smoothed_ref, coarse_ref, low_ref, high_ref,
     visc_ref, inverse_ref, residual_ref, base_ref, d0_ref, d1_ref, pair_ref, row_ref,
 ):
     parts, nx, ny, depth = forcing_ref.shape
     width, rows = nx + 2 * HALO, ny + 2 * HALO
     at_x, at_y = lax.axis_index("gx"), lax.axis_index("gy")
-    odd = is_odd("gy")
     has_left, has_right = at_x > 0, at_x < shape_x - 1
     has_low, has_high = at_y > 0, at_y < shape_y - 1
-    visc_base = parts * width * HALO
-
-    def low_rows(row, count):
-        here = pl.ds(row, count)
-        return jnp.where(odd, same_ref[here, :], cross_ref[here, :])
-
-    def high_rows(row, count):
-        here = pl.ds(row, count)
-        return jnp.where(odd, cross_ref[here, :], same_ref[here, :])
-
-    for i in range(nx + 2 * VISC_HALO):
-        x = i - VISC_HALO
+    low_and_high = message_reader(same_ref, cross_ref)
+    fine_plan, fine_total = row_plan(nx, HALO)
+
+    for x, row, count in row_plan(nx, VISC_HALO)[0]:
         if x < 0:
-            own = left_ref[parts * HALO + i]
+            own = left_ref[parts * HALO + x + VISC_HALO]
             inside = has_left
         elif x < nx:
-            own = lookup(table_ref, phase_ref[x])
+            own = own_visc_ref[x]
             inside = None
         else:
             own = right_ref[parts * HALO + x - nx]
             inside = has_right
-        low = low_rows(visc_base + i * VISC_HALO, VISC_HALO)
-        high = high_rows(visc_base + i * VISC_HALO, VISC_HALO)
-        ok_low, ok_high = has_low, has_high
-        if inside is not None:
-            own = jnp.where(inside, own, 0.0)
-            ok_low, ok_high = jnp.logical_and(ok_low, inside), jnp.logical_and(ok_high, inside)
-        visc_ref[i, pl.ds(VISC_HALO, ny), :] = own
-        visc_ref[i, pl.ds(0, VISC_HALO), :] = jnp.where(ok_low, low, 0.0)
-        visc_ref[i, pl.ds(VISC_HALO + ny, VISC_HALO), :] = jnp.where(ok_high, high, 0.0)
+        low, high = low_and_high(parts * fine_total + row, count)
+        own, low, high = masked(inside, has_low, has_high, own, low, high)
+        place(writer(visc_ref, x + VISC_HALO), 0, ny, VISC_HALO, own, low, high)
 
     lane = lanes(rows, depth)
 
@@ -215,23 +271,20 @@
             diagonal_ref[x - HALO] = pair_ref[pl.ds(HALO, ny), :]
 
     for c in range(parts):
-        for i in range(width):
-            x = i - HALO
+        for x, row, count in fine_plan:
+            i = x + HALO
             if x < 0:
                 own = left_ref[c * HALO + i]
             elif x < nx:
                 own = forcing_ref[c, x]
             else:
                 own = right_ref[c * HALO + x - nx]
-            at = (c * width + i) * HALO
-            base_ref[c, i, pl.ds(ROW0 + HALO, ny), :] = own * inverse_ref[i, pl.ds(HALO, ny), :]
-            base_ref[c, i, pl.ds(ROW0, HALO), :] = low_rows(at, HALO) * inverse_ref[i, pl.ds(0, HALO), :]
-            base_ref[c, i, pl.ds(ROW0 + HALO + ny, HALO), :] = (
-                high_rows(at, HALO) * inverse_ref[i, pl.ds(HALO + ny, HALO), :]
-            )
-
-    for ref in (base_ref, d0_ref, d1_ref):
-        clear_rims(ref, rows)
+            low, high = low_and_high(c * fine_total + row, count)
+            own = own * inverse_ref[i, pl.ds(HALO, ny), :]
+            if count:
+                low = low * inverse_ref[i, pl.ds(HALO - count, count), :]
+                high = high * inverse_ref[i, pl.ds(HALO + ny, count), :]
+            place(writer(base_ref, c, i), ROW0, ny, HALO, own, low, high)
 
     def finish(c, x, value):
         smoothed_ref[c, x - HALO] = value
@@ -320,38 +373,32 @@
 def pack_y2_kernel(smoothed_ref, coarse_ref, left_ref, right_ref, same_ref, cross_ref):
     parts, nx, ny = smoothed_ref.shape[:3]
     ncx, half = nx // 2, ny // 2
-    odd = is_odd("gy")
     sides = {"left": left_ref, "right": right_ref}
-
-    def put(row, low, high):
-        count = low.shape[0]
-        same_ref[pl.ds(row, count), :] = jnp.where(odd, low, high)
-        cross_ref[pl.ds(row, count), :] = jnp.where(odd, high, low)
-
-    row = 0
+    put = message_writer(same_ref, cross_ref)
+    base = 0
     for f in range(4):
         shared = 2 if f == 3 else 1
-        for i in range((ncx + 2 * COARSE_HALO) // shared):
+        plan, total = row_plan(ncx, COARSE_HALO, shared)
+        for i, (_, row, count) in enumerate(plan):
             side, at = coarse_spot(f, i, ncx)
             if side == "own":
-                ref, spot = coarse_ref, (f, at)
+                put(base + row, count, coarse_ref, (f, at))
             else:
-                ref, spot = sides[side], (at,)
-            first, last = slice(0, COARSE_HALO), slice(half - COARSE_HALO, half)
-            put(row, ref[spot + (first,)], ref[spot + (last,)])
-            row += COARSE_HALO
+                put(base + row, count, sides[side], (at,))
+        base += total
     tiles = ny // half
     fine_base = 3 * COARSE_HALO + COARSE_HALO // 2
+    plan, total = row_plan(nx, HALO)
     for c in range(parts):
-        for x in range(-HALO, nx + HALO):
+        for x, row, count in plan:
             if 0 <= x < nx:
-                put(row, smoothed_ref[c, x, pl.ds(0, HALO), :], smoothed_ref[c, x, pl.ds(ny - HALO, HALO), :])
+                put(base + row, count, smoothed_ref, (c, x))
             else:
                 ref = left_ref if x < 0 else right_ref
                 i = x + HALO if x < 0 else x - nx
                 at = fine_base + (c * HALO + i) * tiles
-                put(row, ref[at, pl.ds(0, HALO), :], ref[at + tiles - 1, pl.ds(half - HALO, HALO), :])
-            row += HALO
+                put(base + row, count, ref, (at,), ref, (at + tiles - 1,))
+        base += total
 
 
 def post_kernel(
@@ -367,49 +414,33 @@
     cwidth, crows = ncx + 2 * COARSE_HALO, half + 2 * COARSE_HALO
     srows = source_ref.shape[2]
     at_x, at_y = lax.axis_index("gx"), lax.axis_index("gy")
-    odd = is_odd("gy")
     has_left, has_right = at_x > 0, at_x < shape_x - 1
     has_low, has_high = at_y > 0, at_y < shape_y - 1
     sides = {"left": left_ref, "right": right_ref}
+    insides = {"left": has_left, "own": None, "right": has_right}
+    low_and_high = message_reader(same_ref, cross_ref)
     constants = constants_of(lower_ref, upper_ref)
     first_scale, carried, scaled = constants
 
-    def low_rows(row, count):
-        here = pl.ds(row, count)
-        return jnp.where(odd, same_ref[here, :], cross_ref[here, :])
-
-    def high_rows(row, count):
-        here = pl.ds(row, count)
-        return jnp.where(odd, cross_ref[here, :], same_ref[here, :])
-
-    def masked(inside, own, low, high):
-        ok_low, ok_high = has_low, has_high
-        if inside is not None:
-            own = jnp.where(inside, own, 0.0)
-            ok_low, ok_high = jnp.logical_and(ok_low, inside), jnp.logical_and(ok_high, inside)
-        return own, jnp.where(ok_low, low, 0.0), jnp.where(ok_high, high, 0.0)
-
-    insides = {"left": has_left, "own": None, "right": has_right}
-    row = 0
+    base = 0
+    tail = field_ref.shape[2] - ROW0 - crows
     for f in range(4):
         shared = 2 if f == 3 else 1
-        for i in range(cwidth // shared):
+        plan, total = row_plan(ncx, COARSE_HALO, shared)
+        for i, (_, row, count) in enumerate(plan):
             side, at = coarse_spot(f, i, ncx)
             own = coarse_ref[f, at] if side == "own" else sides[side][at]
-            low, high = low_rows(row, COARSE_HALO), high_rows(row, COARSE_HALO)
-            own, low, high = masked(insides[side], own, low, high)
-            field_ref[f, i, pl.ds(ROW0 + COARSE_HALO, half), :] = own
-            field_ref[f, i, pl.ds(ROW0, COARSE_HALO), :] = low
-            field_ref[f, i, pl.ds(ROW0 + COARSE_HALO + half, COARSE_HALO), :] = high
+            low, high = low_and_high(base + row, count)
+            own, low, high = masked(insides[side], has_low, has_high, own, low, high)
+            place(writer(field_ref, f, i), ROW0, half, COARSE_HALO, own, low, high)
             field_ref[f, i, pl.ds(0, ROW0), :] = jnp.zeros((ROW0, depth), jnp.float32)
-            tail = field_ref.shape[2] - ROW0 - crows
             field_ref[f, i, pl.ds(ROW0 + crows, tail), :] = jnp.zeros((tail, depth), jnp.float32)
-            row += COARSE_HALO
+        base += total
     tiles = ny // half
     fine_base = 3 * COARSE_HALO + COARSE_HALO // 2
+    plan, total = row_plan(nx, HALO)
     for c in range(parts):
-        for i in range(width):
-            x = i - HALO
+        for i, (x, row, count) in enumerate(plan):
             if 0 <= x < nx:
                 side = "own"
                 own = smoothed_ref[c, x]
@@ -418,11 +449,10 @@
                 j = i if x < 0 else x - nx
                 at = fine_base + (c * HALO + j) * tiles
                 own = jnp.concatenate([sides[side][at + t] for t in range(tiles)], axis=0)
-            own, low, high = masked(insides[side], own, low_rows(row, HALO), high_rows(row, HALO))
-            residual_ref[c, i, pl.ds(HALO, ny), :] = own
-            residual_ref[c, i, pl.ds(0, HALO), :] = low
-            residual_ref[c, i, pl.ds(HALO + ny, HALO), :] = high
-            row += HALO
+            low, high = low_and_high(base + row, count)
+            own, low, high = masked(insides[side], has_low, has_high, own, low, high)
+            place(writer(residual_ref, c, i), 0, ny, HALO, own, low, high)
+        base += total
 
     mid = pl.ds(ROW0, srows)
     lane = lanes(srows, depth)
@@ -451,9 +481,6 @@
         cweight_ref[3, i] = upper_y[ROW0 : ROW0 + srows] * inverse
         cweight_ref[4, i] = jnp.where(lane < 2, 0.0, below(upper_z, 2) * inverse)
         cweight_ref[5, i] = jnp.where(lane >= depth - 2, 0.0, upper_z * inverse)
-
-    clear_rims(cd0_ref, srows)
-    clear_rims(cd1_ref, srows)
 
     for i in range(cwidth):
         for s in range(2):
@@ -507,9 +534,6 @@
             beside = beside + weights[4] * below(own) + weights[5] * above(own)
             base_ref[c, i, fine, :] = residual_ref[c, i] - own + beside
 
-    for ref in (base_ref, d0_ref, d1_ref):
-        clear_rims(ref, rows)
-
     def finish(c, x, value):
         out_ref[c, x - HALO] = value * diagonal_ref[x - HALO]
 
@@ -522,7 +546,7 @@
         out_shape=[jax.ShapeDtypeStruct(shape, jnp.float32) for shape in outs],
         in_specs=[pl.BlockSpec(memory_space=space) for space in specs],
         out_specs=[pl.BlockSpec(memory_space=pltpu.VMEM) for _ in outs],
-        scratch_shapes=[pltpu.VMEM(shape, jnp.float32) for shape in scratch],
+        scratch_shapes=[pltpu.VMEM(shape, jnp.float32) if isinstance(shape, tuple) else shape for shape in scratch],
         compiler_params=pltpu.CompilerParams(vmem_limit_bytes=VMEM_LIMIT),
     )
 
@@ -540,6 +564,10 @@
     others = [(0, 0), (devices - 1, devices - 1)]
     others = others + [(i, ((i + 1) ^ 1) - 1) for i in range(1, devices - 1)]
     return lax.ppermute(same, "gy", pairs), lax.ppermute(cross, "gy", others)
+
+
+def in_hbm(value):
+    return pltpu.with_memory_space_constraint(value, pltpu.HBM)
 
 
 def up_to(value, unit):
@@ -556,14 +584,20 @@
     srows = up_to(crows, 8)
 
     slab = (parts * HALO + VISC_HALO, ny, depth)
-    low, high = call(pack_x_kernel, [slab, slab], [], [vmem, vmem, smem])(forcing, phase_index, visc_table)
+    semaphores = pltpu.SemaphoreType.DMA
+    table_rows = pltpu.SMEM(visc_table.shape, jnp.float32)
+    scratch = [pltpu.VMEM((2, VISC_HALO, ny, depth), jnp.int32), table_rows, semaphores((3, parts + 1))]
+    low, high = call(pack_x_kernel, [slab, slab], scratch, [pltpu.HBM] * 3)(
+        in_hbm(forcing), in_hbm(phase_index), in_hbm(visc_table)
+    )
     left, right = ring_x(low, high)
-
-    count = up_to(parts * width * HALO + (nx + 2 * VISC_HALO) * VISC_HALO, 8)
-    slab = (count, depth)
-    same, cross = call(pack_y_kernel, [slab, slab], [], [vmem, vmem, smem, vmem, vmem])(
-        forcing, phase_index, visc_table, left, right
+    scratch = [pltpu.VMEM((nx, ny, depth), jnp.int32), table_rows, semaphores((3,))]
+    forcing, viscosity = call(stage_kernel, [forcing.shape, (nx, ny, depth)], scratch, [pltpu.HBM] * 3)(
+        in_hbm(forcing), in_hbm(phase_index), in_hbm(visc_table)
     )
+
+    slab = (up_to(parts * row_plan(nx, HALO)[1] + row_plan(nx, VISC_HALO)[1], 8), depth)
+    same, cross = call(pack_y_kernel, [slab, slab], [], [vmem] * 4)(forcing, viscosity, left, right)
     same, cross = swap_y(same, cross)
 
     tiles = 3 * COARSE_HALO + COARSE_HALO // 2 + parts * HALO * (ny // half)
@@ -582,12 +616,12 @@
             (rows, depth),
             (6, up_to(ny + 2, 8), depth),
         ],
-        [vmem, vmem, smem, smem, smem, vmem, vmem, vmem, vmem],
-    )(forcing, phase_index, visc_table, lower_bound, upper_bound, left, right, same, cross)
+        [vmem, vmem, smem, smem, vmem, vmem, vmem, vmem],
+    )(forcing, viscosity, lower_bound, upper_bound, left, right, same, cross)
     left, right = ring_x(low, high)
 
-    count = up_to((3 * cwidth + cwidth // 2) * COARSE_HALO + parts * width * HALO, 8)
-    slab = (count, depth)
+    count = 3 * row_plan(ncx, COARSE_HALO)[1] + row_plan(ncx, COARSE_HALO, 2)[1] + parts * row_plan(nx, HALO)[1]
+    slab = (up_to(count, 8), depth)
     same, cross = call(pack_y2_kernel, [slab, slab], [], [vmem] * 4)(smoothed, coarse, left, right)
     same, cross = swap_y(same, cross)
 

time: 50.9 us -> 45.1 us (0.89)
  waiting for transfers between devices: 17.9 us -> 15.1 us
  local copies, waits for them, and re-layouts: 2.55 us -> 0 us
  Pallas kernels: 10.7 us -> 10.1 us
    unnamed x6 -> x0, local copies, waits for them, and re-layouts: 2.55 us -> none
    ppermute x4, waiting for transfers between devices: 7.91 us -> 6.25 us  [swap_y(): return (lax.ppermute(same, 'gy', pairs), lax.ppermute(cross, 'gy', others))]
    ppermute x4, waiting for transfers between devices: 10 us -> 8.9 us  [ring_x(): return (lax.ppermute(high, 'gx', up), lax.ppermute(low, 'gx', down))]
    pallas_call x1, Pallas kernels: 3.58 us -> 2.65 us  [local(): call(functools.partial(pre_kernel, shape_x, shape_y), [(6, width, rows, d...]
    pallas_call x2 -> x3, Pallas kernels: 1.26 us -> 2.14 us  [the longest x1 1.09 us: local(): call(stage_kernel, [forcing.shape, (nx, ny, depth)], scratch, [pltpu.HBM]...]
  transfers between devices with their start and end apart: 8 -> 8, of which waited for: 6 -> 6; matrix products, arithmetic and copies ran while one was open for 0% -> 0% of each run, Pallas kernels for 0% -> 2%
where the time goes in v3:
time: 45.1 us; the launch traced here: 44.9 us
  starting transfers between devices  18.2 us (40%)
  waiting for transfers between devices  15.1 us (33%)
  Pallas kernels  10.1 us (22%)
  between operations  1.37 us (3%)
    ppermute x4, starting transfers between devices, swap_y(): return (lax.ppermute(same, 'gy', pairs), lax.ppermute(cross, 'gy', others))  12.7 us
    ppermute x4, waiting for transfers between devices, ring_x(): return (lax.ppermute(high, 'gx', up), lax.ppermute(low, 'gx', down))  8.9 us
    ppermute x4, waiting for transfers between devices, swap_y(): return (lax.ppermute(same, 'gy', pairs), lax.ppermute(cross, 'gy', others))  6.25 us
    ppermute x4, starting transfers between devices, ring_x(): return (lax.ppermute(high, 'gx', up), lax.ppermute(low, 'gx', down))  5.53 us
    pallas_call x1, Pallas kernels, local(): call(functools.partial(post_kernel, shape_x, shape_y), [(parts, nx, ny, d...  5.23 us
    pallas_call x1, Pallas kernels, local(): call(functools.partial(pre_kernel, shape_x, shape_y), [(6, width, rows, d...  2.65 us
    pallas_call x1, Pallas kernels, local(): call(stage_kernel, [forcing.shape, (nx, ny, depth)], scratch, [pltpu.HBM]...  1.09 us
    pallas_call x1, Pallas kernels, local(): call(pack_x_kernel, [slab, slab], scratch, [pltpu.HBM] * 3)  0.98 us
  transfers between devices with their start and end apart: 8, of which 6 were waited for; matrix products, arithmetic and copies ran while one was open for 0% of the time, Pallas kernels for 2%

profile of v3, /device:TPU:1, one launch (start us, length us, event | category | flops | bytes accessed | tf_op | source)
XLA Modules:
  0.0 44.9 jit_solution(6489435468121354293)
XLA Ops:
  0.0 1.0 %shard_map.56 = (f32[17,16,128]{2,1,0:T(8,128)S(1)}, f32[17,16,128]{2,1,0:T(8,128)S(1)}) custom-call(f32[3,16,16,128]{3,2,1,0:T(8,128)} %forcing_ref.3, s32[16,16,128]{2,1,0:T(8,128)} %phase_ref.3, f32[8]{0:T(128)} %table_ref.3), custom_call_target="tpu_custom_call" | custom-call | tf_op jit(solution)/shard_map/pallas_call | solution.py:590
  1.0 2.1 %collective-permute-start = (f32[17,16,128]{2,1,0:T(8,128)S(1)}, f32[17,16,128]{2,1,0:T(8,128)S(1)}, u32[]{:S(2)}, u32[]{:S(2)}) collective-permute-start(f32[17,16,128]{2,1,0:T(8,128)S(1)} %get-tuple-element.21), channel_id=1, source_target_pairs={{0,8},{8,16},{16,24},{24,0},{1,9},{9,17},{17,25},{25,1},{2,10},{10... | collective-permute-start | bytes 417800 | tf_op jit(solution)/shard_map/ppermute | solution.py:558
  3.1 1.0 %collective-permute-start.1 = (f32[17,16,128]{2,1,0:T(8,128)S(1)}, f32[17,16,128]{2,1,0:T(8,128)S(1)}, u32[]{:S(2)}, u32[]{:S(2)}) collective-permute-start(f32[17,16,128]{2,1,0:T(8,128)S(1)} %get-tuple-element.22), channel_id=1, source_target_pairs={{8,0},{16,8},{24,16},{0,24},{9,1},{17,9},{25,17},{1,25},{10,2},{18... | collective-permute-start | bytes 417800 | tf_op jit(solution)/shard_map/ppermute | solution.py:558
  4.1 1.1 %shard_map.55 = (f32[3,16,16,128]{3,2,1,0:T(8,128)S(1)}, f32[16,16,128]{2,1,0:T(8,128)S(1)}) custom-call(f32[3,16,16,128]{3,2,1,0:T(8,128)} %forcing_ref.3, s32[16,16,128]{2,1,0:T(8,128)} %phase_ref.3, f32[8]{0:T(128)} %table_ref.3), custom_call_target="tpu_custom_call" | custom-call | tf_op jit(solution)/shard_map/pallas_call | solution.py:595
  5.2 2.2 %collective-permute-done.left_ref = f32[17,16,128]{2,1,0:T(8,128)S(1)} collective-permute-done((f32[17,16,128]{2,1,0:T(8,128)S(1)}, f32[17,16,128]{2,1,0:T(8,128)S(1)}, u32[]{:S(2)}, u32[]{:S(2)}) %collective-permute-start) | collective-permute-done | bytes 139296 | tf_op jit(solution)/shard_map/ppermute | solution.py:558
  7.4 2.9 %collective-permute-done.1.right_ref = f32[17,16,128]{2,1,0:T(8,128)S(1)} collective-permute-done((f32[17,16,128]{2,1,0:T(8,128)S(1)}, f32[17,16,128]{2,1,0:T(8,128)S(1)}, u32[]{:S(2)}, u32[]{:S(2)}) %collective-permute-start.1) | collective-permute-done | bytes 139296 | tf_op jit(solution)/shard_map/ppermute | solution.py:558
  10.4 0.1 shard_map.57
  10.4 1.6 %collective-permute-start.2 = (f32[328,128]{1,0:T(8,128)S(1)}, f32[328,128]{1,0:T(8,128)S(1)}, u32[]{:S(2)}, u32[]{:S(2)}) collective-permute-start(f32[328,128]{1,0:T(8,128)S(1)} %get-tuple-element.23), channel_id=1, source_target_pairs={{0,1},{1,0},{2,3},{3,2},{4,5},{5,4},{6,7},{7,6},{8,9},{9,8},{10,11... | collective-permute-start | bytes 503816 | tf_op jit(solution)/shard_map/ppermute | solution.py:566
  12.0 3.1 %collective-permute-start.3 = (f32[328,128]{1,0:T(8,128)S(1)}, f32[328,128]{1,0:T(8,128)S(1)}, u32[]{:S(2)}, u32[]{:S(2)}) collective-permute-start(f32[328,128]{1,0:T(8,128)S(1)} %get-tuple-element.24), channel_id=1, source_target_pairs={{0,0},{7,7},{1,2},{2,1},{3,4},{4,3},{5,6},{6,5},{8,8},{15,15},{9,1... | collective-permute-start | bytes 503816 | tf_op jit(solution)/shard_map/ppermute | solution.py:566
  16.4 0.0 collective-permute-done.2.same_ref
  16.5 2.3 %collective-permute-done.3.cross_ref = f32[328,128]{1,0:T(8,128)S(1)} collective-permute-done((f32[328,128]{1,0:T(8,128)S(1)}, f32[328,128]{1,0:T(8,128)S(1)}, u32[]{:S(2)}, u32[]{:S(2)}) %collective-permute-start.3) | collective-permute-done | bytes 167968 | tf_op jit(solution)/shard_map/ppermute | solution.py:566
  18.7 2.7 %shard_map.58 = (f32[6,24,24,128]{3,2,1,0:T(8,128)S(1)}, f32[16,16,128]{2,1,0:T(8,128)S(1)}, f32[3,16,16,128]{3,2,1,0:T(8,128)S(1)}, f32[4,8,8,128]{3,2,1,0:T(8,...) custom-call(f32[3,16,16,128]{3,2,1,0:T(8,128)S(1)} %get-tuple-element.19.forcing_ref, ...), custom_call_target="tpu_custom_call" | custom-call | tf_op jit(solution)/shard_map/pallas_call | solution.py:606
  21.4 1.3 %collective-permute-start.4 = (f32[45,8,128]{2,1,0:T(8,128)S(1)}, f32[45,8,128]{2,1,0:T(8,128)S(1)}, u32[]{:S(2)}, u32[]{:S(2)}) collective-permute-start(f32[45,8,128]{2,1,0:T(8,128)S(1)} %get-tuple-element.29), channel_id=1, source_target_pairs={{0,8},{8,16},{16,24},{24,0},{1,9},{9,17},{17,25},{25,1},{2,10},{10... | collective-permute-start | bytes 552968 | tf_op jit(solution)/shard_map/ppermute | solution.py:558
  22.6 1.2 %collective-permute-start.5 = (f32[45,8,128]{2,1,0:T(8,128)S(1)}, f32[45,8,128]{2,1,0:T(8,128)S(1)}, u32[]{:S(2)}, u32[]{:S(2)}) collective-permute-start(f32[45,8,128]{2,1,0:T(8,128)S(1)} %get-tuple-element.30), channel_id=1, source_target_pairs={{8,0},{16,8},{24,16},{0,24},{9,1},{17,9},{25,17},{1,25},{10,2},{18... | collective-permute-start | bytes 552968 | tf_op jit(solution)/shard_map/ppermute | solution.py:558
  23.8 2.9 %collective-permute-done.4.left_ref = f32[45,8,128]{2,1,0:T(8,128)S(1)} collective-permute-done((f32[45,8,128]{2,1,0:T(8,128)S(1)}, f32[45,8,128]{2,1,0:T(8,128)S(1)}, u32[]{:S(2)}, u32[]{:S(2)}) %collective-permute-start.4) | collective-permute-done | bytes 184352 | tf_op jit(solution)/shard_map/ppermute | solution.py:558
  26.7 0.8 %collective-permute-done.5.right_ref = f32[45,8,128]{2,1,0:T(8,128)S(1)} collective-permute-done((f32[45,8,128]{2,1,0:T(8,128)S(1)}, f32[45,8,128]{2,1,0:T(8,128)S(1)}, u32[]{:S(2)}, u32[]{:S(2)}) %collective-permute-start.5) | collective-permute-done | bytes 184352 | tf_op jit(solution)/shard_map/ppermute | solution.py:558
  27.5 0.1 shard_map.59
  27.6 0.1 collective-permute-start.6
  27.7 7.9 %collective-permute-start.7 = (f32[504,128]{1,0:T(8,128)S(1)}, f32[504,128]{1,0:T(8,128)S(1)}, u32[]{:S(2)}, u32[]{:S(2)}) collective-permute-start(f32[504,128]{1,0:T(8,128)S(1)} %get-tuple-element.32), channel_id=1, source_target_pairs={{0,0},{7,7},{1,2},{2,1},{3,4},{4,3},{5,6},{6,5},{8,8},{15,15},{9,1... | collective-permute-start | bytes 774152 | tf_op jit(solution)/shard_map/ppermute | solution.py:566
  35.6 0.0 collective-permute-done.6.same_ref
  35.7 4.0 %collective-permute-done.7.cross_ref = f32[504,128]{1,0:T(8,128)S(1)} collective-permute-done((f32[504,128]{1,0:T(8,128)S(1)}, f32[504,128]{1,0:T(8,128)S(1)}, u32[]{:S(2)}, u32[]{:S(2)}) %collective-permute-start.7) | collective-permute-done | bytes 258080 | tf_op jit(solution)/shard_map/ppermute | solution.py:566
  39.6 5.2 %shard_map.60 = f32[3,16,16,128]{3,2,1,0:T(8,128)} custom-call(f32[6,24,24,128]{3,2,1,0:T(8,128)S(1)} %get-tuple-element.25.weight_ref, f32[16,16,128]{2,1,0:T(8,128)S(1)} %get-tuple-element.26.diagonal_ref, f32[3,16,16,128]{3,2,1,0:T(8,128)S(1)} %get-tuple-element.27.smoothed_ref, f32[4,8,8,128]{3,2,1,0:T(8,128)S(1)} %get-tuple-element.28.coarse_ref, ...), custom_call_target="tpu_custom_call" | custom-call | tf_op jit(solution)/shard_map/pallas_call | solution.py:629
Async XLA Ops:
  1.0 6.4 %collective-permute-start = (f32[17,16,128]{2,1,0:T(8,128)S(1)}, f32[17,16,128]{2,1,0:T(8,128)S(1)}, u32[]{:S(2)}, u32[]{:S(2)}) collective-permute-start(f32[17,16,128]{2,1,0:T(8,128)S(1)} %get-tuple-element.21), channel_id=1, source_target_pairs={{0,8},{8,16},{16,24},{24,0},{1,9},{9,17},{17,25},{25,1},{2,10},{10... | collective-permute-start | bytes 417800 | tf_op jit(solution)/shard_map/ppermute | solution.py:558
  3.1 7.3 %collective-permute-start.1 = (f32[17,16,128]{2,1,0:T(8,128)S(1)}, f32[17,16,128]{2,1,0:T(8,128)S(1)}, u32[]{:S(2)}, u32[]{:S(2)}) collective-permute-start(f32[17,16,128]{2,1,0:T(8,128)S(1)} %get-tuple-element.22), channel_id=1, source_target_pairs={{8,0},{16,8},{24,16},{0,24},{9,1},{17,9},{25,17},{1,25},{10,2},{18... | collective-permute-start | bytes 417800 | tf_op jit(solution)/shard_map/ppermute | solution.py:558
  10.4 6.0 %collective-permute-start.2 = (f32[328,128]{1,0:T(8,128)S(1)}, f32[328,128]{1,0:T(8,128)S(1)}, u32[]{:S(2)}, u32[]{:S(2)}) collective-permute-start(f32[328,128]{1,0:T(8,128)S(1)} %get-tuple-element.23), channel_id=1, source_target_pairs={{0,1},{1,0},{2,3},{3,2},{4,5},{5,4},{6,7},{7,6},{8,9},{9,8},{10,11... | collective-permute-start | bytes 503816 | tf_op jit(solution)/shard_map/ppermute | solution.py:566
  12.0 6.7 %collective-permute-start.3 = (f32[328,128]{1,0:T(8,128)S(1)}, f32[328,128]{1,0:T(8,128)S(1)}, u32[]{:S(2)}, u32[]{:S(2)}) collective-permute-start(f32[328,128]{1,0:T(8,128)S(1)} %get-tuple-element.24), channel_id=1, source_target_pairs={{0,0},{7,7},{1,2},{2,1},{3,4},{4,3},{5,6},{6,5},{8,8},{15,15},{9,1... | collective-permute-start | bytes 503816 | tf_op jit(solution)/shard_map/ppermute | solution.py:566
  21.4 5.3 %collective-permute-start.4 = (f32[45,8,128]{2,1,0:T(8,128)S(1)}, f32[45,8,128]{2,1,0:T(8,128)S(1)}, u32[]{:S(2)}, u32[]{:S(2)}) collective-permute-start(f32[45,8,128]{2,1,0:T(8,128)S(1)} %get-tuple-element.29), channel_id=1, source_target_pairs={{0,8},{8,16},{16,24},{24,0},{1,9},{9,17},{17,25},{25,1},{2,10},{10... | collective-permute-start | bytes 552968 | tf_op jit(solution)/shard_map/ppermute | solution.py:558
  22.6 4.9 %collective-permute-start.5 = (f32[45,8,128]{2,1,0:T(8,128)S(1)}, f32[45,8,128]{2,1,0:T(8,128)S(1)}, u32[]{:S(2)}, u32[]{:S(2)}) collective-permute-start(f32[45,8,128]{2,1,0:T(8,128)S(1)} %get-tuple-element.30), channel_id=1, source_target_pairs={{8,0},{16,8},{24,16},{0,24},{9,1},{17,9},{25,17},{1,25},{10,2},{18... | collective-permute-start | bytes 552968 | tf_op jit(solution)/shard_map/ppermute | solution.py:558
  27.6 8.0 %collective-permute-start.6 = (f32[504,128]{1,0:T(8,128)S(1)}, f32[504,128]{1,0:T(8,128)S(1)}, u32[]{:S(2)}, u32[]{:S(2)}) collective-permute-start(f32[504,128]{1,0:T(8,128)S(1)} %get-tuple-element.31), channel_id=1, source_target_pairs={{0,1},{1,0},{2,3},{3,2},{4,5},{5,4},{6,7},{7,6},{8,9},{9,8},{10,11... | collective-permute-start | bytes 774152 | tf_op jit(solution)/shard_map/ppermute | solution.py:566
  27.7 11.9 %collective-permute-start.7 = (f32[504,128]{1,0:T(8,128)S(1)}, f32[504,128]{1,0:T(8,128)S(1)}, u32[]{:S(2)}, u32[]{:S(2)}) collective-permute-start(f32[504,128]{1,0:T(8,128)S(1)} %get-tuple-element.32), channel_id=1, source_target_pairs={{0,0},{7,7},{1,2},{2,1},{3,4},{4,3},{5,6},{6,5},{8,8},{15,15},{9,1... | collective-permute-start | bytes 774152 | tf_op jit(solution)/shard_map/ppermute | solution.py:566

commit v4 on v3

--- a/solution.py
+++ b/solution.py
@@ -218,7 +218,7 @@
     shape_x,
     shape_y,
     forcing_ref, own_visc_ref, lower_ref, upper_ref, left_ref, right_ref, same_ref, cross_ref,
-    weight_ref, diagonal_ref, smoothed_ref, coarse_ref, low_ref, high_ref,
+    weight_ref, diagonal_ref, smoothed_ref, coarse_ref, low_ref, high_ref, fine_low_ref, fine_high_ref,
     visc_ref, inverse_ref, residual_ref, base_ref, d0_ref, d1_ref, pair_ref, row_ref,
 ):
     parts, nx, ny, depth = forcing_ref.shape
@@ -350,13 +350,10 @@
             low_ref[at] = coarse_ref[f, i]
             high_ref[at] = coarse_ref[f, ncx // shared - count + i]
             at += 1
-    tiles = ny // half
     for c in range(parts):
         for i in range(HALO):
-            for t in range(tiles):
-                low_ref[at] = smoothed_ref[c, i, pl.ds(t * half, half), :]
-                high_ref[at] = smoothed_ref[c, nx - HALO + i, pl.ds(t * half, half), :]
-                at += 1
+            fine_low_ref[c * HALO + i] = smoothed_ref[c, i]
+            fine_high_ref[c * HALO + i] = smoothed_ref[c, nx - HALO + i]
 
 
 def coarse_spot(f, i, ncx):
@@ -370,15 +367,13 @@
     return "right", base + i - count - own
 
 
-def pack_y2_kernel(smoothed_ref, coarse_ref, left_ref, right_ref, same_ref, cross_ref):
-    parts, nx, ny = smoothed_ref.shape[:3]
-    ncx, half = nx // 2, ny // 2
+def pack_coarse_kernel(coarse_ref, left_ref, right_ref, same_ref, cross_ref):
+    ncx = coarse_ref.shape[1]
     sides = {"left": left_ref, "right": right_ref}
     put = message_writer(same_ref, cross_ref)
     base = 0
     for f in range(4):
-        shared = 2 if f == 3 else 1
-        plan, total = row_plan(ncx, COARSE_HALO, shared)
+        plan, total = row_plan(ncx, COARSE_HALO, 2 if f == 3 else 1)
         for i, (_, row, count) in enumerate(plan):
             side, at = coarse_spot(f, i, ncx)
             if side == "own":
@@ -386,31 +381,32 @@
             else:
                 put(base + row, count, sides[side], (at,))
         base += total
-    tiles = ny // half
-    fine_base = 3 * COARSE_HALO + COARSE_HALO // 2
+
+
+def pack_fine_kernel(smoothed_ref, left_ref, right_ref, after_ref, same_ref, cross_ref):
+    parts, nx = smoothed_ref.shape[:2]
+    put = message_writer(same_ref, cross_ref)
     plan, total = row_plan(nx, HALO)
     for c in range(parts):
         for x, row, count in plan:
-            if 0 <= x < nx:
-                put(base + row, count, smoothed_ref, (c, x))
+            if x < 0:
+                put(c * total + row, count, left_ref, (c * HALO + x + HALO,))
+            elif x < nx:
+                put(c * total + row, count, smoothed_ref, (c, x))
             else:
-                ref = left_ref if x < 0 else right_ref
-                i = x + HALO if x < 0 else x - nx
-                at = fine_base + (c * HALO + i) * tiles
-                put(base + row, count, ref, (at,), ref, (at + tiles - 1,))
-        base += total
-
-
-def post_kernel(
+                put(c * total + row, count, right_ref, (c * HALO + x - nx,))
+
+
+def coarse_kernel(
     shape_x,
     shape_y,
-    weight_ref, diagonal_ref, smoothed_ref, coarse_ref, lower_ref, upper_ref, left_ref, right_ref, same_ref, cross_ref,
-    out_ref,
-    field_ref, cweight_ref, source_ref, cd0_ref, cd1_ref, correction_ref, prolonged_ref, residual_ref, base_ref, d0_ref, d1_ref,
+    weight_ref, coarse_ref, lower_ref, upper_ref, left_ref, right_ref, same_ref, cross_ref,
+    change_ref,
+    field_ref, cweight_ref, source_ref, cd0_ref, cd1_ref, correction_ref, prolonged_ref,
 ):
-    parts, nx, ny, depth = smoothed_ref.shape
-    width, rows = nx + 2 * HALO, ny + 2 * HALO
-    ncx, half = nx // 2, ny // 2
+    parts = change_ref.shape[0]
+    width, rows = weight_ref.shape[1:3]
+    ncx, half, depth = coarse_ref.shape[1:]
     cwidth, crows = ncx + 2 * COARSE_HALO, half + 2 * COARSE_HALO
     srows = source_ref.shape[2]
     at_x, at_y = lax.axis_index("gx"), lax.axis_index("gy")
@@ -436,24 +432,6 @@
             field_ref[f, i, pl.ds(0, ROW0), :] = jnp.zeros((ROW0, depth), jnp.float32)
             field_ref[f, i, pl.ds(ROW0 + crows, tail), :] = jnp.zeros((tail, depth), jnp.float32)
         base += total
-    tiles = ny // half
-    fine_base = 3 * COARSE_HALO + COARSE_HALO // 2
-    plan, total = row_plan(nx, HALO)
-    for c in range(parts):
-        for i, (x, row, count) in enumerate(plan):
-            if 0 <= x < nx:
-                side = "own"
-                own = smoothed_ref[c, x]
-            else:
-                side = "left" if x < 0 else "right"
-                j = i if x < 0 else x - nx
-                at = fine_base + (c * HALO + j) * tiles
-                own = jnp.concatenate([sides[side][at + t] for t in range(tiles)], axis=0)
-            low, high = low_and_high(base + row, count)
-            own, low, high = masked(insides[side], has_low, has_high, own, low, high)
-            place(writer(residual_ref, c, i), 0, ny, HALO, own, low, high)
-        base += total
-
     mid = pl.ds(ROW0, srows)
     lane = lanes(srows, depth)
     even = lane % 2 == 0
@@ -532,11 +510,44 @@
             beside = beside + weights[2] * prolonged_ref[c, at, pl.ds(ROW0 - 1, rows), :]
             beside = beside + weights[3] * prolonged_ref[c, at, pl.ds(ROW0 + 1, rows), :]
             beside = beside + weights[4] * below(own) + weights[5] * above(own)
-            base_ref[c, i, fine, :] = residual_ref[c, i] - own + beside
+            change_ref[c, i] = beside - own
+
+
+def post_kernel(
+    shape_x,
+    shape_y,
+    weight_ref, diagonal_ref, smoothed_ref, change_ref, lower_ref, upper_ref, left_ref, right_ref, same_ref, cross_ref,
+    out_ref,
+    residual_ref, base_ref, d0_ref, d1_ref,
+):
+    parts, nx, ny = smoothed_ref.shape[:3]
+    width = nx + 2 * HALO
+    at_x, at_y = lax.axis_index("gx"), lax.axis_index("gy")
+    has_left, has_right = at_x > 0, at_x < shape_x - 1
+    has_low, has_high = at_y > 0, at_y < shape_y - 1
+    low_and_high = message_reader(same_ref, cross_ref)
+    plan, total = row_plan(nx, HALO)
+    for c in range(parts):
+        for i, (x, row, count) in enumerate(plan):
+            inside = None
+            if x < 0:
+                own, inside = left_ref[c * HALO + i], has_left
+            elif x < nx:
+                own = smoothed_ref[c, x]
+            else:
+                own, inside = right_ref[c * HALO + x - nx], has_right
+            low, high = low_and_high(c * total + row, count)
+            own, low, high = masked(inside, has_low, has_high, own, low, high)
+            own = own + change_ref[c, i, pl.ds(HALO, ny), :]
+            if count:
+                low = low + change_ref[c, i, pl.ds(HALO - count, count), :]
+                high = high + change_ref[c, i, pl.ds(HALO + ny, count), :]
+            place(writer(base_ref, c, i), ROW0, ny, HALO, own, low, high)
 
     def finish(c, x, value):
         out_ref[c, x - HALO] = value * diagonal_ref[x - HALO]
 
+    constants = constants_of(lower_ref, upper_ref)
     fine_steps(weight_ref, base_ref, residual_ref, (d0_ref, d1_ref), constants, width, finish)
 
 
@@ -600,12 +611,13 @@
     same, cross = call(pack_y_kernel, [slab, slab], [], [vmem] * 4)(forcing, viscosity, left, right)
     same, cross = swap_y(same, cross)
 
-    tiles = 3 * COARSE_HALO + COARSE_HALO // 2 + parts * HALO * (ny // half)
-    slab = (tiles, half, depth)
+    slab = (3 * COARSE_HALO + COARSE_HALO // 2, half, depth)
+    fine_slab = (parts * HALO, ny, depth)
     fine_d = (parts, width, rows + 2 * ROW0, depth)
-    weight, diagonal, smoothed, coarse, low, high = call(
+    weight, diagonal, smoothed, coarse, low, high, fine_low, fine_high = call(
         functools.partial(pre_kernel, shape_x, shape_y),
-        [(6, width, rows, depth), (nx, ny, depth), (parts, nx, ny, depth), (4, ncx, half, depth), slab, slab],
+        [(6, width, rows, depth), (nx, ny, depth), (parts, nx, ny, depth), (4, ncx, half, depth)]
+        + [slab, slab, fine_slab, fine_slab],
         [
             (nx + 2 * VISC_HALO, up_to(ny + 2 * VISC_HALO, 8), depth),
             (width, rows, depth),
@@ -619,16 +631,22 @@
         [vmem, vmem, smem, smem, vmem, vmem, vmem, vmem],
     )(forcing, viscosity, lower_bound, upper_bound, left, right, same, cross)
     left, right = ring_x(low, high)
-
-    count = 3 * row_plan(ncx, COARSE_HALO)[1] + row_plan(ncx, COARSE_HALO, 2)[1] + parts * row_plan(nx, HALO)[1]
+    fine_left, fine_right = ring_x(fine_low, fine_high)
+
+    count = 3 * row_plan(ncx, COARSE_HALO)[1] + row_plan(ncx, COARSE_HALO, 2)[1]
     slab = (up_to(count, 8), depth)
-    same, cross = call(pack_y2_kernel, [slab, slab], [], [vmem] * 4)(smoothed, coarse, left, right)
-    same, cross = swap_y(same, cross)
+    packed, cross = call(pack_coarse_kernel, [slab, slab], [], [vmem] * 3)(coarse, left, right)
+    same, cross = swap_y(packed, cross)
+    slab = (up_to(parts * row_plan(nx, HALO)[1], 8), depth)
+    fine_same, fine_cross = call(pack_fine_kernel, [slab, slab], [], [vmem] * 4)(
+        smoothed, fine_left, fine_right, packed
+    )
+    fine_same, fine_cross = swap_y(fine_same, fine_cross)
 
     coarse_d = (2, cwidth, srows + 2 * ROW0, depth)
-    (out,) = call(
-        functools.partial(post_kernel, shape_x, shape_y),
-        [(parts, nx, ny, depth)],
+    (change,) = call(
+        functools.partial(coarse_kernel, shape_x, shape_y),
+        [(parts, width, rows, depth)],
         [
             (4, cwidth, up_to(ROW0 + crows + 1, 8), depth),
             (6, cwidth, srows, depth),
@@ -637,13 +655,16 @@
             coarse_d,
             (2, cwidth, srows, depth),
             (parts, ncx + 2 * COARSE_REACH, rows + 2 * ROW0, depth),
-            (parts, width, rows, depth),
-            fine_d,
-            fine_d,
-            fine_d,
         ],
+        [vmem, vmem, smem, smem, vmem, vmem, vmem, vmem],
+    )(weight, coarse, lower_bound, upper_bound, left, right, same, cross)
+
+    (out,) = call(
+        functools.partial(post_kernel, shape_x, shape_y),
+        [(parts, nx, ny, depth)],
+        [(parts, width, rows, depth), fine_d, fine_d, fine_d],
         [vmem, vmem, vmem, vmem, smem, smem, vmem, vmem, vmem, vmem],
-    )(weight, diagonal, smoothed, coarse, lower_bound, upper_bound, left, right, same, cross)
+    )(weight, diagonal, smoothed, change, lower_bound, upper_bound, fine_left, fine_right, fine_same, fine_cross)
     return out
 
 

time: 45.1 us -> 41.3 us (0.916)
  waiting for transfers between devices: 15.1 us -> 7.76 us
  starting transfers between devices: 18.2 us -> 21.5 us
    ppermute x4 -> x6, waiting for transfers between devices: 6.25 us -> 2.27 us  [swap_y(): return (lax.ppermute(same, 'gy', pairs), lax.ppermute(cross, 'gy', others))]
    ppermute x4 -> x6, waiting for transfers between devices: 8.9 us -> 5.49 us  [ring_x(): return (lax.ppermute(high, 'gx', up), lax.ppermute(low, 'gx', down))]
    pallas_call x1 -> x3, Pallas kernels: 0.1 us -> 3.03 us  [the longest x1 2.93 us: local(): call(functools.partial(coarse_kernel, shape_x, shape_y), [(parts, width,...]
    pallas_call x1, Pallas kernels: 5.23 us -> 2.45 us  [local(): call(functools.partial(post_kernel, shape_x, shape_y), [(parts, nx, ny, d...]
    ppermute x4 -> x6, starting transfers between devices: 5.53 us -> 7.9 us  [ring_x(): return (lax.ppermute(high, 'gx', up), lax.ppermute(low, 'gx', down))]
    ppermute x4 -> x6, starting transfers between devices: 12.7 us -> 13.7 us  [swap_y(): return (lax.ppermute(same, 'gy', pairs), lax.ppermute(cross, 'gy', others))]
  transfers between devices with their start and end apart: 8 -> 12, of which waited for: 6 -> 4; matrix products, arithmetic and copies ran while one was open for 0% -> 0% of each run, Pallas kernels for 2% -> 10%
where the time goes in v4:
time: 41.3 us; the launch traced here: 41 us
  starting transfers between devices  21.5 us (52%)
  Pallas kernels  10.3 us (25%)
  waiting for transfers between devices  7.76 us (19%)
  between operations  1.44 us (3%)
    ppermute x6, starting transfers between devices, swap_y(): return (lax.ppermute(same, 'gy', pairs), lax.ppermute(cross, 'gy', others))  13.7 us
    ppermute x6, starting transfers between devices, ring_x(): return (lax.ppermute(high, 'gx', up), lax.ppermute(low, 'gx', down))  7.9 us
    ppermute x6, waiting for transfers between devices, ring_x(): return (lax.ppermute(high, 'gx', up), lax.ppermute(low, 'gx', down))  5.49 us
    pallas_call x1, Pallas kernels, local(): call(functools.partial(coarse_kernel, shape_x, shape_y), [(parts, width,...  2.93 us
    pallas_call x1, Pallas kernels, local(): call(functools.partial(pre_kernel, shape_x, shape_y), [(6, width, rows, d...  2.65 us
    pallas_call x1, Pallas kernels, local(): call(functools.partial(post_kernel, shape_x, shape_y), [(parts, nx, ny, d...  2.45 us
    ppermute x6, waiting for transfers between devices, swap_y(): return (lax.ppermute(same, 'gy', pairs), lax.ppermute(cross, 'gy', others))  2.27 us
    pallas_call x1, Pallas kernels, local(): call(stage_kernel, [forcing.shape, (nx, ny, depth)], scratch, [pltpu.HBM]...  1.09 us
  transfers between devices with their start and end apart: 12, of which 4 were waited for; matrix products, arithmetic and copies ran while one was open for 0% of the time, Pallas kernels for 10%

profile of v4, /device:TPU:1, one launch (start us, length us, event | category | flops | bytes accessed | tf_op | source)
XLA Modules:
  0.0 41.0 jit_solution(124400101214454144)
XLA Ops:
  0.0 1.0 %shard_map.56 = (f32[17,16,128]{2,1,0:T(8,128)S(1)}, f32[17,16,128]{2,1,0:T(8,128)S(1)}) custom-call(f32[3,16,16,128]{3,2,1,0:T(8,128)} %forcing_ref.3, s32[16,16,128]{2,1,0:T(8,128)} %phase_ref.3, f32[8]{0:T(128)} %table_ref.3), custom_call_target="tpu_custom_call" | custom-call | tf_op jit(solution)/shard_map/pallas_call | solution.py:601
  1.0 2.1 %collective-permute-start = (f32[17,16,128]{2,1,0:T(8,128)S(1)}, f32[17,16,128]{2,1,0:T(8,128)S(1)}, u32[]{:S(2)}, u32[]{:S(2)}) collective-permute-start(f32[17,16,128]{2,1,0:T(8,128)S(1)} %get-tuple-element.25), channel_id=1, source_target_pairs={{0,8},{8,16},{16,24},{24,0},{1,9},{9,17},{17,25},{25,1},{2,10},{10... | collective-permute-start | bytes 417800 | tf_op jit(solution)/shard_map/ppermute | solution.py:569
  3.1 1.0 %collective-permute-start.1 = (f32[17,16,128]{2,1,0:T(8,128)S(1)}, f32[17,16,128]{2,1,0:T(8,128)S(1)}, u32[]{:S(2)}, u32[]{:S(2)}) collective-permute-start(f32[17,16,128]{2,1,0:T(8,128)S(1)} %get-tuple-element.26), channel_id=1, source_target_pairs={{8,0},{16,8},{24,16},{0,24},{9,1},{17,9},{25,17},{1,25},{10,2},{18... | collective-permute-start | bytes 417800 | tf_op jit(solution)/shard_map/ppermute | solution.py:569
  4.1 1.1 %shard_map.55 = (f32[3,16,16,128]{3,2,1,0:T(8,128)S(1)}, f32[16,16,128]{2,1,0:T(8,128)S(1)}) custom-call(f32[3,16,16,128]{3,2,1,0:T(8,128)} %forcing_ref.3, s32[16,16,128]{2,1,0:T(8,128)} %phase_ref.3, f32[8]{0:T(128)} %table_ref.3), custom_call_target="tpu_custom_call" | custom-call | tf_op jit(solution)/shard_map/pallas_call | solution.py:606
  5.2 2.2 %collective-permute-done.left_ref = f32[17,16,128]{2,1,0:T(8,128)S(1)} collective-permute-done((f32[17,16,128]{2,1,0:T(8,128)S(1)}, f32[17,16,128]{2,1,0:T(8,128)S(1)}, u32[]{:S(2)}, u32[]{:S(2)}) %collective-permute-start) | collective-permute-done | bytes 139296 | tf_op jit(solution)/shard_map/ppermute | solution.py:569
  7.4 2.9 %collective-permute-done.1.right_ref = f32[17,16,128]{2,1,0:T(8,128)S(1)} collective-permute-done((f32[17,16,128]{2,1,0:T(8,128)S(1)}, f32[17,16,128]{2,1,0:T(8,128)S(1)}, u32[]{:S(2)}, u32[]{:S(2)}) %collective-permute-start.1) | collective-permute-done | bytes 139296 | tf_op jit(solution)/shard_map/ppermute | solution.py:569
  10.4 0.1 shard_map.57
  10.4 1.6 %collective-permute-start.2 = (f32[328,128]{1,0:T(8,128)S(1)}, f32[328,128]{1,0:T(8,128)S(1)}, u32[]{:S(2)}, u32[]{:S(2)}) collective-permute-start(f32[328,128]{1,0:T(8,128)S(1)} %get-tuple-element.27), channel_id=1, source_target_pairs={{0,1},{1,0},{2,3},{3,2},{4,5},{5,4},{6,7},{7,6},{8,9},{9,8},{10,11... | collective-permute-start | bytes 503816 | tf_op jit(solution)/shard_map/ppermute | solution.py:577
  12.0 3.1 %collective-permute-start.3 = (f32[328,128]{1,0:T(8,128)S(1)}, f32[328,128]{1,0:T(8,128)S(1)}, u32[]{:S(2)}, u32[]{:S(2)}) collective-permute-start(f32[328,128]{1,0:T(8,128)S(1)} %get-tuple-element.28), channel_id=1, source_target_pairs={{0,0},{7,7},{1,2},{2,1},{3,4},{4,3},{5,6},{6,5},{8,8},{15,15},{9,1... | collective-permute-start | bytes 503816 | tf_op jit(solution)/shard_map/ppermute | solution.py:577
  16.4 0.0 collective-permute-done.2.same_ref
  16.5 2.3 %collective-permute-done.3.cross_ref = f32[328,128]{1,0:T(8,128)S(1)} collective-permute-done((f32[328,128]{1,0:T(8,128)S(1)}, f32[328,128]{1,0:T(8,128)S(1)}, u32[]{:S(2)}, u32[]{:S(2)}) %collective-permute-start.3) | collective-permute-done | bytes 167968 | tf_op jit(solution)/shard_map/ppermute | solution.py:577
  18.7 2.6 %shard_map.58 = (f32[6,24,24,128]{3,2,1,0:T(8,128)S(1)}, f32[16,16,128]{2,1,0:T(8,128)S(1)}, f32[3,16,16,128]{3,2,1,0:T(8,128)S(1)}, f32[4,8,8,128]{3,2,1,0:T(8,...) custom-call(f32[3,16,16,128]{3,2,1,0:T(8,128)S(1)} %get-tuple-elemen, ...), custom_call_target="tpu_custom_call" | custom-call | tf_op jit(solution)/shard_map/pallas_call | solution.py:617
  21.4 1.3 %collective-permute-start.4 = (f32[21,8,128]{2,1,0:T(8,128)S(1)}, f32[21,8,128]{2,1,0:T(8,128)S(1)}, u32[]{:S(2)}, u32[]{:S(2)}) collective-permute-start(f32[21,8,128]{2,1,0:T(8,128)S(1)} %get-tuple-element.33), channel_id=1, source_target_pairs={{0,8},{8,16},{16,24},{24,0},{1,9},{9,17},{17,25},{25,1},{2,10},{10... | collective-permute-start | bytes 258056 | tf_op jit(solution)/shard_map/ppermute | solution.py:569
  22.6 1.2 %collective-permute-start.5 = (f32[21,8,128]{2,1,0:T(8,128)S(1)}, f32[21,8,128]{2,1,0:T(8,128)S(1)}, u32[]{:S(2)}, u32[]{:S(2)}) collective-permute-start(f32[21,8,128]{2,1,0:T(8,128)S(1)} %get-tuple-element.34), channel_id=1, source_target_pairs={{8,0},{16,8},{24,16},{0,24},{9,1},{17,9},{25,17},{1,25},{10,2},{18... | collective-permute-start | bytes 258056 | tf_op jit(solution)/shard_map/ppermute | solution.py:569
  23.8 0.3 collective-permute-start.8
  24.1 2.1 %collective-permute-start.9 = (f32[12,16,128]{2,1,0:T(8,128)S(1)}, f32[12,16,128]{2,1,0:T(8,128)S(1)}, u32[]{:S(2)}, u32[]{:S(2)}) collective-permute-start(f32[12,16,128]{2,1,0:T(8,128)S(1)} %get-tuple-element.38), channel_id=1, source_target_pairs={{8,0},{16,8},{24,16},{0,24},{9,1},{17,9},{25,17},{1,25},{10,2},{18... | collective-permute-start | bytes 294920 | tf_op jit(solution)/shard_map/ppermute | solution.py:569
  26.1 0.3 collective-permute-done.4.left_ref
  26.5 0.0 collective-permute-done.5.right_ref
  26.5 0.1 collective-permute-start.6
  26.6 5.2 %collective-permute-start.7 = (f32[280,128]{1,0:T(8,128)S(1)}, f32[280,128]{1,0:T(8,128)S(1)}, u32[]{:S(2)}, u32[]{:S(2)}) collective-permute-start(f32[280,128]{1,0:T(8,128)S(1)} %get-tuple-element.36), channel_id=1, source_target_pairs={{0,0},{7,7},{1,2},{2,1},{3,4},{4,3},{5,6},{6,5},{8,8},{15,15},{9,1... | collective-permute-start | bytes 430088 | tf_op jit(solution)/shard_map/ppermute | solution.py:577
  31.8 0.0 collective-permute-done.8.left_ref
  31.8 0.0 collective-permute-done.9.right_ref
  31.8 0.1 shard_map.61
  31.9 0.1 collective-permute-start.10
  31.9 3.6 %collective-permute-start.11 = (f32[232,128]{1,0:T(8,128)S(1)}, f32[232,128]{1,0:T(8,128)S(1)}, u32[]{:S(2)}, u32[]{:S(2)}) collective-permute-start(f32[232,128]{1,0:T(8,128)S(1)} %get-tuple-element.40), channel_id=1, source_target_pairs={{0,0},{7,7},{1,2},{2,1},{3,4},{4,3},{5,6},{6,5},{8,8},{15,15},{9,1... | collective-permute-start | bytes 356360 | tf_op jit(solution)/shard_map/ppermute | solution.py:577
  35.6 0.0 collective-permute-done.6.same_ref
  35.6 0.0 collective-permute-done.7.cross_ref
  35.6 2.9 %shard_map.60.change_ref = f32[3,24,24,128]{3,2,1,0:T(8,128)S(1)} custom-call(f32[6,24,24,128]{3,2,1,0:T(8,128)S(1)} %get-tuple-element.29.weight_ref, f32[4,8,8,128]{3,2,1,0:T(8,128)S(1)} %get-tuple-element.32.coarse_ref, f32[1]{0:T(128)S(6)} %copy.6.lower_ref, f32[1]{0:T(128)S(6)} %copy.7.upper_ref, f32[21,8,128]{2,1,0:T(8,128)S(1)} %collective-permute-done.4.left_ref, ...), custom_call_target="tpu_custom_call" | custom-call | tf_op jit(solution)/shard_map/pallas_call | solution.py:647
  38.5 0.0 collective-permute-done.10.same_ref
  38.6 0.0 collective-permute-done.11.cross_ref
  38.6 2.4 %shard_map.62 = f32[3,16,16,128]{3,2,1,0:T(8,128)} custom-call(f32[6,24,24,128]{3,2,1,0:T(8,128)S(1)} %get-tuple-element.29.weight_ref, f32[16,16,128]{2,1,0:T(8,128)S(1)} %get-tuple-element.30.diagonal_ref, f32[3,16,16,128]{3,2,1,0:T(8,128)S(1)} %get-tuple-element.31.smoothed_ref, f32[3,24,24,128]{3,2,1,0:T(8,128)S(1)} %shard_map.60.change_ref, ...), custom_call_target="tpu_custom_call" | custom-call | tf_op jit(solution)/shard_map/pallas_call | solution.py:662
  (1 shorter events, 0.0 us)
Async XLA Ops:
  1.0 6.4 %collective-permute-start = (f32[17,16,128]{2,1,0:T(8,128)S(1)}, f32[17,16,128]{2,1,0:T(8,128)S(1)}, u32[]{:S(2)}, u32[]{:S(2)}) collective-permute-start(f32[17,16,128]{2,1,0:T(8,128)S(1)} %get-tuple-element.25), channel_id=1, source_target_pairs={{0,8},{8,16},{16,24},{24,0},{1,9},{9,17},{17,25},{25,1},{2,10},{10... | collective-permute-start | bytes 417800 | tf_op jit(solution)/shard_map/ppermute | solution.py:569
  3.1 7.3 %collective-permute-start.1 = (f32[17,16,128]{2,1,0:T(8,128)S(1)}, f32[17,16,128]{2,1,0:T(8,128)S(1)}, u32[]{:S(2)}, u32[]{:S(2)}) collective-permute-start(f32[17,16,128]{2,1,0:T(8,128)S(1)} %get-tuple-element.26), channel_id=1, source_target_pairs={{8,0},{16,8},{24,16},{0,24},{9,1},{17,9},{25,17},{1,25},{10,2},{18... | collective-permute-start | bytes 417800 | tf_op jit(solution)/shard_map/ppermute | solution.py:569
  10.4 6.0 %collective-permute-start.2 = (f32[328,128]{1,0:T(8,128)S(1)}, f32[328,128]{1,0:T(8,128)S(1)}, u32[]{:S(2)}, u32[]{:S(2)}) collective-permute-start(f32[328,128]{1,0:T(8,128)S(1)} %get-tuple-element.27), channel_id=1, source_target_pairs={{0,1},{1,0},{2,3},{3,2},{4,5},{5,4},{6,7},{7,6},{8,9},{9,8},{10,11... | collective-permute-start | bytes 503816 | tf_op jit(solution)/shard_map/ppermute | solution.py:577
  12.0 6.7 %collective-permute-start.3 = (f32[328,128]{1,0:T(8,128)S(1)}, f32[328,128]{1,0:T(8,128)S(1)}, u32[]{:S(2)}, u32[]{:S(2)}) collective-permute-start(f32[328,128]{1,0:T(8,128)S(1)} %get-tuple-element.28), channel_id=1, source_target_pairs={{0,0},{7,7},{1,2},{2,1},{3,4},{4,3},{5,6},{6,5},{8,8},{15,15},{9,1... | collective-permute-start | bytes 503816 | tf_op jit(solution)/shard_map/ppermute | solution.py:577
  21.4 5.1 %collective-permute-start.4 = (f32[21,8,128]{2,1,0:T(8,128)S(1)}, f32[21,8,128]{2,1,0:T(8,128)S(1)}, u32[]{:S(2)}, u32[]{:S(2)}) collective-permute-start(f32[21,8,128]{2,1,0:T(8,128)S(1)} %get-tuple-element.33), channel_id=1, source_target_pairs={{0,8},{8,16},{16,24},{24,0},{1,9},{9,17},{17,25},{25,1},{2,10},{10... | collective-permute-start | bytes 258056 | tf_op jit(solution)/shard_map/ppermute | solution.py:569
  22.6 3.9 %collective-permute-start.5 = (f32[21,8,128]{2,1,0:T(8,128)S(1)}, f32[21,8,128]{2,1,0:T(8,128)S(1)}, u32[]{:S(2)}, u32[]{:S(2)}) collective-permute-start(f32[21,8,128]{2,1,0:T(8,128)S(1)} %get-tuple-element.34), channel_id=1, source_target_pairs={{8,0},{16,8},{24,16},{0,24},{9,1},{17,9},{25,17},{1,25},{10,2},{18... | collective-permute-start | bytes 258056 | tf_op jit(solution)/shard_map/ppermute | solution.py:569
  23.8 8.0 %collective-permute-start.8 = (f32[12,16,128]{2,1,0:T(8,128)S(1)}, f32[12,16,128]{2,1,0:T(8,128)S(1)}, u32[]{:S(2)}, u32[]{:S(2)}) collective-permute-start(f32[12,16,128]{2,1,0:T(8,128)S(1)} %get-tuple-element.37), channel_id=1, source_target_pairs={{0,8},{8,16},{16,24},{24,0},{1,9},{9,17},{17,25},{25,1},{2,10},{10... | collective-permute-start | bytes 294920 | tf_op jit(solution)/shard_map/ppermute | solution.py:569
  24.1 7.7 %collective-permute-start.9 = (f32[12,16,128]{2,1,0:T(8,128)S(1)}, f32[12,16,128]{2,1,0:T(8,128)S(1)}, u32[]{:S(2)}, u32[]{:S(2)}) collective-permute-start(f32[12,16,128]{2,1,0:T(8,128)S(1)} %get-tuple-element.38), channel_id=1, source_target_pairs={{8,0},{16,8},{24,16},{0,24},{9,1},{17,9},{25,17},{1,25},{10,2},{18... | collective-permute-start | bytes 294920 | tf_op jit(solution)/shard_map/ppermute | solution.py:569
  26.5 9.1 %collective-permute-start.6 = (f32[280,128]{1,0:T(8,128)S(1)}, f32[280,128]{1,0:T(8,128)S(1)}, u32[]{:S(2)}, u32[]{:S(2)}) collective-permute-start(f32[280,128]{1,0:T(8,128)S(1)} %get-tuple-element.35.after_ref), channel_id=1, source_target_pairs={{0,1},{1,0},{2,3},{3,2},{4,5},{5,4},{6,7},{7,6},{8,9},{9,8},{10,11... | collective-permute-start | bytes 430088 | tf_op jit(solution)/shard_map/ppermute | solution.py:577
  26.6 9.0 %collective-permute-start.7 = (f32[280,128]{1,0:T(8,128)S(1)}, f32[280,128]{1,0:T(8,128)S(1)}, u32[]{:S(2)}, u32[]{:S(2)}) collective-permute-start(f32[280,128]{1,0:T(8,128)S(1)} %get-tuple-element.36), channel_id=1, source_target_pairs={{0,0},{7,7},{1,2},{2,1},{3,4},{4,3},{5,6},{6,5},{8,8},{15,15},{9,1... | collective-permute-start | bytes 430088 | tf_op jit(solution)/shard_map/ppermute | solution.py:577
  31.9 6.7 %collective-permute-start.10 = (f32[232,128]{1,0:T(8,128)S(1)}, f32[232,128]{1,0:T(8,128)S(1)}, u32[]{:S(2)}, u32[]{:S(2)}) collective-permute-start(f32[232,128]{1,0:T(8,128)S(1)} %get-tuple-element.39), channel_id=1, source_target_pairs={{0,1},{1,0},{2,3},{3,2},{4,5},{5,4},{6,7},{7,6},{8,9},{9,8},{10,11... | collective-permute-start | bytes 356360 | tf_op jit(solution)/shard_map/ppermute | solution.py:577
  31.9 6.6 %collective-permute-start.11 = (f32[232,128]{1,0:T(8,128)S(1)}, f32[232,128]{1,0:T(8,128)S(1)}, u32[]{:S(2)}, u32[]{:S(2)}) collective-permute-start(f32[232,128]{1,0:T(8,128)S(1)} %get-tuple-element.40), channel_id=1, source_target_pairs={{0,0},{7,7},{1,2},{2,1},{3,4},{4,3},{5,6},{6,5},{8,8},{15,15},{9,1... | collective-permute-start | bytes 356360 | tf_op jit(solution)/shard_map/ppermute | solution.py:577

commit v5 on v4

--- a/solution.py
+++ b/solution.py
@@ -9,6 +9,7 @@
 
 CHEB = 4
 COARSE_STEPS = 4
+OUT_PIECES = 4
 HALO = CHEB
 VISC_HALO = HALO + 1
 COARSE_REACH = (HALO + 2) // 2
@@ -126,7 +127,7 @@
     return store
 
 
-def message_reader(same_ref, cross_ref):
+def message_reader(cross_ref, same_ref):
     odd = is_odd("gy")
 
     def low_and_high(row, count):
@@ -138,7 +139,7 @@
     return low_and_high
 
 
-def message_writer(same_ref, cross_ref):
+def message_writer(cross_ref, same_ref):
     odd = is_odd("gy")
 
     def put(row, count, ref, at, ref_high=None, at_high=None):
@@ -154,9 +155,9 @@
     return put
 
 
-def pack_y_kernel(forcing_ref, visc_ref, left_ref, right_ref, same_ref, cross_ref):
+def pack_y_kernel(forcing_ref, visc_ref, left_ref, right_ref, cross_ref, same_ref):
     parts, nx = forcing_ref.shape[:2]
-    put = message_writer(same_ref, cross_ref)
+    put = message_writer(cross_ref, same_ref)
     plan, total = row_plan(nx, HALO)
     for c in range(parts):
         for x, row, count in plan:
@@ -217,7 +218,7 @@
 def pre_kernel(
     shape_x,
     shape_y,
-    forcing_ref, own_visc_ref, lower_ref, upper_ref, left_ref, right_ref, same_ref, cross_ref,
+    forcing_ref, own_visc_ref, lower_ref, upper_ref, left_ref, right_ref, cross_ref, same_ref,
     weight_ref, diagonal_ref, smoothed_ref, coarse_ref, low_ref, high_ref, fine_low_ref, fine_high_ref,
     visc_ref, inverse_ref, residual_ref, base_ref, d0_ref, d1_ref, pair_ref, row_ref,
 ):
@@ -226,7 +227,7 @@
     at_x, at_y = lax.axis_index("gx"), lax.axis_index("gy")
     has_left, has_right = at_x > 0, at_x < shape_x - 1
     has_low, has_high = at_y > 0, at_y < shape_y - 1
-    low_and_high = message_reader(same_ref, cross_ref)
+    low_and_high = message_reader(cross_ref, same_ref)
     fine_plan, fine_total = row_plan(nx, HALO)
 
     for x, row, count in row_plan(nx, VISC_HALO)[0]:
@@ -367,10 +368,10 @@
     return "right", base + i - count - own
 
 
-def pack_coarse_kernel(coarse_ref, left_ref, right_ref, same_ref, cross_ref):
+def pack_coarse_kernel(coarse_ref, left_ref, right_ref, cross_ref, same_ref):
     ncx = coarse_ref.shape[1]
     sides = {"left": left_ref, "right": right_ref}
-    put = message_writer(same_ref, cross_ref)
+    put = message_writer(cross_ref, same_ref)
     base = 0
     for f in range(4):
         plan, total = row_plan(ncx, COARSE_HALO, 2 if f == 3 else 1)
@@ -383,9 +384,9 @@
         base += total
 
 
-def pack_fine_kernel(smoothed_ref, left_ref, right_ref, after_ref, same_ref, cross_ref):
+def pack_fine_kernel(smoothed_ref, left_ref, right_ref, after_ref, cross_ref, same_ref):
     parts, nx = smoothed_ref.shape[:2]
-    put = message_writer(same_ref, cross_ref)
+    put = message_writer(cross_ref, same_ref)
     plan, total = row_plan(nx, HALO)
     for c in range(parts):
         for x, row, count in plan:
@@ -400,7 +401,7 @@
 def coarse_kernel(
     shape_x,
     shape_y,
-    weight_ref, coarse_ref, lower_ref, upper_ref, left_ref, right_ref, same_ref, cross_ref,
+    weight_ref, coarse_ref, lower_ref, upper_ref, left_ref, right_ref, cross_ref, same_ref,
     change_ref,
     field_ref, cweight_ref, source_ref, cd0_ref, cd1_ref, correction_ref, prolonged_ref,
 ):
@@ -414,7 +415,7 @@
     has_low, has_high = at_y > 0, at_y < shape_y - 1
     sides = {"left": left_ref, "right": right_ref}
     insides = {"left": has_left, "own": None, "right": has_right}
-    low_and_high = message_reader(same_ref, cross_ref)
+    low_and_high = message_reader(cross_ref, same_ref)
     constants = constants_of(lower_ref, upper_ref)
     first_scale, carried, scaled = constants
 
@@ -442,29 +443,27 @@
     def second_of(value):
         return jnp.where(even, above(value), value)
 
-    even_low = lanes(field_ref.shape[2], depth) % 2 == 0
+    before_x = None
     for i in range(cwidth):
-        packed = field_ref[3, i // 2, mid, :]
-        inverse = first_of(packed) if i % 2 == 0 else second_of(packed)
-        upper_x = second_of(field_ref[1, i, mid, :])
-        faces_y = field_ref[2, i]
-        upper_y = jnp.where(even_low, faces_y, below(faces_y))
-        upper_z = second_of(field_ref[2, i, mid, :])
-        source_ref[0, i] = field_ref[0, i, mid, :]
-        source_ref[1, i] = first_of(field_ref[1, i, mid, :])
-        if i > 0:
-            cweight_ref[0, i] = second_of(field_ref[1, i - 1, mid, :]) * inverse
-        cweight_ref[1, i] = upper_x * inverse
-        cweight_ref[2, i] = upper_y[ROW0 - 1 : ROW0 - 1 + srows] * inverse
-        cweight_ref[3, i] = upper_y[ROW0 : ROW0 + srows] * inverse
-        cweight_ref[4, i] = jnp.where(lane < 2, 0.0, below(upper_z, 2) * inverse)
-        cweight_ref[5, i] = jnp.where(lane >= depth - 2, 0.0, upper_z * inverse)
-
-    for i in range(cwidth):
-        for s in range(2):
-            value = first_scale * source_ref[s, i]
-            cd0_ref[s, i, mid, :] = value
-            correction_ref[s, i] = value
+        pair, faces_x = field_ref[0, i, mid, :], field_ref[1, i, mid, :]
+        single, upper_x = first_of(faces_x), second_of(faces_x)
+        source_ref[0, i] = pair
+        source_ref[1, i] = single
+        cd0_ref[0, i, mid, :] = first_scale * pair
+        cd0_ref[1, i, mid, :] = first_scale * single
+        if 0 < i < cwidth - 1:
+            packed = field_ref[3, i // 2, mid, :]
+            inverse = first_of(packed) if i % 2 == 0 else second_of(packed)
+            faces_y = field_ref[2, i, mid, :]
+            upper_z = second_of(faces_y)
+            cweight_ref[0, i] = before_x * inverse
+            cweight_ref[1, i] = upper_x * inverse
+            cweight_ref[2, i] = first_of(field_ref[2, i, pl.ds(ROW0 - 1, srows), :]) * inverse
+            cweight_ref[3, i] = first_of(faces_y) * inverse
+            cweight_ref[4, i] = jnp.where(lane < 2, 0.0, below(upper_z, 2) * inverse)
+            cweight_ref[5, i] = jnp.where(lane >= depth - 2, 0.0, upper_z * inverse)
+        before_x = upper_x
+
     for number in range(COARSE_STEPS - 1):
         old, new = ((cd0_ref, cd1_ref), (cd1_ref, cd0_ref))[number % 2]
         last = number + 2 == COARSE_STEPS
@@ -481,7 +480,7 @@
                 if not last:
                     source_ref[s, i] = fresh
                     new[s, i, mid, :] = direction
-                correction_ref[s, i] = correction_ref[s, i] + direction
+                correction_ref[s, i] = (own if number == 0 else correction_ref[s, i]) + direction
 
     edge = COARSE_HALO - COARSE_REACH
     pwidth, prows = ncx + 2 * COARSE_REACH, half + 2 * COARSE_REACH
@@ -516,16 +515,16 @@
 def post_kernel(
     shape_x,
     shape_y,
-    weight_ref, diagonal_ref, smoothed_ref, change_ref, lower_ref, upper_ref, left_ref, right_ref, same_ref, cross_ref,
+    weight_ref, diagonal_ref, smoothed_ref, change_ref, lower_ref, upper_ref, left_ref, right_ref, cross_ref, same_ref,
     out_ref,
-    residual_ref, base_ref, d0_ref, d1_ref,
+    done_ref, sems, residual_ref, base_ref, d0_ref, d1_ref,
 ):
     parts, nx, ny = smoothed_ref.shape[:3]
     width = nx + 2 * HALO
     at_x, at_y = lax.axis_index("gx"), lax.axis_index("gy")
     has_left, has_right = at_x > 0, at_x < shape_x - 1
     has_low, has_high = at_y > 0, at_y < shape_y - 1
-    low_and_high = message_reader(same_ref, cross_ref)
+    low_and_high = message_reader(cross_ref, same_ref)
     plan, total = row_plan(nx, HALO)
     for c in range(parts):
         for i, (x, row, count) in enumerate(plan):
@@ -544,19 +543,29 @@
                 high = high + change_ref[c, i, pl.ds(HALO + ny, count), :]
             place(writer(base_ref, c, i), ROW0, ny, HALO, own, low, high)
 
+    piece = nx // OUT_PIECES
+    copies = []
+
     def finish(c, x, value):
-        out_ref[c, x - HALO] = value * diagonal_ref[x - HALO]
+        at = x - HALO
+        done_ref[c, at] = value * diagonal_ref[at]
+        if c == parts - 1 and at % piece == piece - 1:
+            here = pl.ds(at + 1 - piece, piece)
+            copies.append(pltpu.make_async_copy(done_ref.at[:, here], out_ref.at[:, here], sems.at[len(copies)]))
+            copies[-1].start()
 
     constants = constants_of(lower_ref, upper_ref)
     fine_steps(weight_ref, base_ref, residual_ref, (d0_ref, d1_ref), constants, width, finish)
-
-
-def call(kernel, outs, scratch, specs):
+    for copy in copies:
+        copy.wait()
+
+
+def call(kernel, outs, scratch, specs, out_space=pltpu.VMEM):
     return pl.pallas_call(
         kernel,
         out_shape=[jax.ShapeDtypeStruct(shape, jnp.float32) for shape in outs],
         in_specs=[pl.BlockSpec(memory_space=space) for space in specs],
-        out_specs=[pl.BlockSpec(memory_space=pltpu.VMEM) for _ in outs],
+        out_specs=[pl.BlockSpec(memory_space=out_space) for _ in outs],
         scratch_shapes=[pltpu.VMEM(shape, jnp.float32) if isinstance(shape, tuple) else shape for shape in scratch],
         compiler_params=pltpu.CompilerParams(vmem_limit_bytes=VMEM_LIMIT),
     )
@@ -569,12 +578,12 @@
     return lax.ppermute(high, "gx", up), lax.ppermute(low, "gx", down)
 
 
-def swap_y(same, cross):
+def swap_y(cross, same):
     devices = lax.axis_size("gy")
     pairs = [(i, i ^ 1) for i in range(devices)]
     others = [(0, 0), (devices - 1, devices - 1)]
     others = others + [(i, ((i + 1) ^ 1) - 1) for i in range(1, devices - 1)]
-    return lax.ppermute(same, "gy", pairs), lax.ppermute(cross, "gy", others)
+    return lax.ppermute(cross, "gy", others), lax.ppermute(same, "gy", pairs)
 
 
 def in_hbm(value):
@@ -608,8 +617,8 @@
     )
 
     slab = (up_to(parts * row_plan(nx, HALO)[1] + row_plan(nx, VISC_HALO)[1], 8), depth)
-    same, cross = call(pack_y_kernel, [slab, slab], [], [vmem] * 4)(forcing, viscosity, left, right)
-    same, cross = swap_y(same, cross)
+    cross, same = call(pack_y_kernel, [slab, slab], [], [vmem] * 4)(forcing, viscosity, left, right)
+    cross, same = swap_y(cross, same)
 
     slab = (3 * COARSE_HALO + COARSE_HALO // 2, half, depth)
     fine_slab = (parts * HALO, ny, depth)
@@ -629,19 +638,19 @@
             (6, up_to(ny + 2, 8), depth),
         ],
         [vmem, vmem, smem, smem, vmem, vmem, vmem, vmem],
-    )(forcing, viscosity, lower_bound, upper_bound, left, right, same, cross)
+    )(forcing, viscosity, lower_bound, upper_bound, left, right, cross, same)
     left, right = ring_x(low, high)
     fine_left, fine_right = ring_x(fine_low, fine_high)
 
     count = 3 * row_plan(ncx, COARSE_HALO)[1] + row_plan(ncx, COARSE_HALO, 2)[1]
     slab = (up_to(count, 8), depth)
-    packed, cross = call(pack_coarse_kernel, [slab, slab], [], [vmem] * 3)(coarse, left, right)
-    same, cross = swap_y(packed, cross)
+    packed, same = call(pack_coarse_kernel, [slab, slab], [], [vmem] * 3)(coarse, left, right)
+    cross, same = swap_y(packed, same)
     slab = (up_to(parts * row_plan(nx, HALO)[1], 8), depth)
-    fine_same, fine_cross = call(pack_fine_kernel, [slab, slab], [], [vmem] * 4)(
+    fine_cross, fine_same = call(pack_fine_kernel, [slab, slab], [], [vmem] * 4)(
         smoothed, fine_left, fine_right, packed
     )
-    fine_same, fine_cross = swap_y(fine_same, fine_cross)
+    fine_cross, fine_same = swap_y(fine_cross, fine_same)
 
     coarse_d = (2, cwidth, srows + 2 * ROW0, depth)
     (change,) = call(
@@ -657,14 +666,15 @@
             (parts, ncx + 2 * COARSE_REACH, rows + 2 * ROW0, depth),
         ],
         [vmem, vmem, smem, smem, vmem, vmem, vmem, vmem],
-    )(weight, coarse, lower_bound, upper_bound, left, right, same, cross)
+    )(weight, coarse, lower_bound, upper_bound, left, right, cross, same)
 
     (out,) = call(
         functools.partial(post_kernel, shape_x, shape_y),
         [(parts, nx, ny, depth)],
-        [(parts, width, rows, depth), fine_d, fine_d, fine_d],
+        [(parts, nx, ny, depth), pltpu.SemaphoreType.DMA((OUT_PIECES,)), (parts, width, rows, depth), fine_d, fine_d, fine_d],
         [vmem, vmem, vmem, vmem, smem, smem, vmem, vmem, vmem, vmem],
-    )(weight, diagonal, smoothed, change, lower_bound, upper_bound, fine_left, fine_right, fine_same, fine_cross)
+        pltpu.HBM,
+    )(weight, diagonal, smoothed, change, lower_bound, upper_bound, fine_left, fine_right, fine_cross, fine_same)
     return out
 
 

time: 41.3 us -> 41.1 us (level)
    ppermute x6, waiting for transfers between devices: 5.49 us -> 6.1 us  [ring_x(): return (lax.ppermute(high, 'gx', up), lax.ppermute(low, 'gx', down))]
    ppermute x6, waiting for transfers between devices: 2.27 us -> 1.67 us  [swap_y(): return (lax.ppermute(cross, 'gy', others), lax.ppermute(same, 'gy', pairs))]
  transfers between devices with their start and end apart: 12 -> 12, of which waited for: 4 -> 5; matrix products, arithmetic and copies ran while one was open for 0% -> 0% of each run, Pallas kernels for 10% -> 10%
where the time goes in v5:
time: 41.1 us; the launch traced here: 40.5 us
  starting transfers between devices  21.3 us (52%)
  Pallas kernels  9.97 us (24%)
  waiting for transfers between devices  7.77 us (19%)
  between operations  1.44 us (4%)
    ppermute x6, starting transfers between devices, swap_y(): return (lax.ppermute(cross, 'gy', others), lax.ppermute(same, 'gy', pairs))  13.4 us
    ppermute x6, starting transfers between devices, ring_x(): return (lax.ppermute(high, 'gx', up), lax.ppermute(low, 'gx', down))  7.9 us
    ppermute x6, waiting for transfers between devices, ring_x(): return (lax.ppermute(high, 'gx', up), lax.ppermute(low, 'gx', down))  6.1 us
    pallas_call x1, Pallas kernels, local(): call(functools.partial(coarse_kernel, shape_x, shape_y), [(parts, width,...  2.71 us
    pallas_call x1, Pallas kernels, local(): call(functools.partial(pre_kernel, shape_x, shape_y), [(6, width, rows, d...  2.65 us
    pallas_call x1, Pallas kernels, local(): call(functools.partial(post_kernel, shape_x, shape_y), [(parts, nx, ny, d...  2.38 us
    ppermute x6, waiting for transfers between devices, swap_y(): return (lax.ppermute(cross, 'gy', others), lax.ppermute(same, 'gy', pairs))  1.67 us
    pallas_call x1, Pallas kernels, local(): call(stage_kernel, [forcing.shape, (nx, ny, depth)], scratch, [pltpu.HBM]...  1.09 us
  transfers between devices with their start and end apart: 12, of which 5 were waited for; matrix products, arithmetic and copies ran while one was open for 0% of the time, Pallas kernels for 10%

profile of v5, /device:TPU:1, one launch (start us, length us, event | category | flops | bytes accessed | tf_op | source)
XLA Modules:
  0.0 40.5 jit_solution(13827608415718989380)
XLA Ops:
  0.0 1.0 %shard_map.56 = (f32[17,16,128]{2,1,0:T(8,128)S(1)}, f32[17,16,128]{2,1,0:T(8,128)S(1)}) custom-call(f32[3,16,16,128]{3,2,1,0:T(8,128)} %forcing_ref.3, s32[16,16,128]{2,1,0:T(8,128)} %phase_ref.3, f32[8]{0:T(128)} %table_ref.3), custom_call_target="tpu_custom_call" | custom-call | tf_op jit(solution)/shard_map/pallas_call | solution.py:610
  1.0 2.1 %collective-permute-start = (f32[17,16,128]{2,1,0:T(8,128)S(1)}, f32[17,16,128]{2,1,0:T(8,128)S(1)}, u32[]{:S(2)}, u32[]{:S(2)}) collective-permute-start(f32[17,16,128]{2,1,0:T(8,128)S(1)} %get-tuple-element.25), channel_id=1, source_target_pairs={{0,8},{8,16},{16,24},{24,0},{1,9},{9,17},{17,25},{25,1},{2,10},{10... | collective-permute-start | bytes 417800 | tf_op jit(solution)/shard_map/ppermute | solution.py:578
  3.1 1.0 %collective-permute-start.1 = (f32[17,16,128]{2,1,0:T(8,128)S(1)}, f32[17,16,128]{2,1,0:T(8,128)S(1)}, u32[]{:S(2)}, u32[]{:S(2)}) collective-permute-start(f32[17,16,128]{2,1,0:T(8,128)S(1)} %get-tuple-element.26), channel_id=1, source_target_pairs={{8,0},{16,8},{24,16},{0,24},{9,1},{17,9},{25,17},{1,25},{10,2},{18... | collective-permute-start | bytes 417800 | tf_op jit(solution)/shard_map/ppermute | solution.py:578
  4.1 1.1 %shard_map.55 = (f32[3,16,16,128]{3,2,1,0:T(8,128)S(1)}, f32[16,16,128]{2,1,0:T(8,128)S(1)}) custom-call(f32[3,16,16,128]{3,2,1,0:T(8,128)} %forcing_ref.3, s32[16,16,128]{2,1,0:T(8,128)} %phase_ref.3, f32[8]{0:T(128)} %table_ref.3), custom_call_target="tpu_custom_call" | custom-call | tf_op jit(solution)/shard_map/pallas_call | solution.py:615
  5.2 2.2 %collective-permute-done.left_ref = f32[17,16,128]{2,1,0:T(8,128)S(1)} collective-permute-done((f32[17,16,128]{2,1,0:T(8,128)S(1)}, f32[17,16,128]{2,1,0:T(8,128)S(1)}, u32[]{:S(2)}, u32[]{:S(2)}) %collective-permute-start) | collective-permute-done | bytes 139296 | tf_op jit(solution)/shard_map/ppermute | solution.py:578
  7.4 2.9 %collective-permute-done.1.right_ref = f32[17,16,128]{2,1,0:T(8,128)S(1)} collective-permute-done((f32[17,16,128]{2,1,0:T(8,128)S(1)}, f32[17,16,128]{2,1,0:T(8,128)S(1)}, u32[]{:S(2)}, u32[]{:S(2)}) %collective-permute-start.1) | collective-permute-done | bytes 139296 | tf_op jit(solution)/shard_map/ppermute | solution.py:578
  10.4 0.1 shard_map.57
  10.4 4.6 %collective-permute-start.2 = (f32[328,128]{1,0:T(8,128)S(1)}, f32[328,128]{1,0:T(8,128)S(1)}, u32[]{:S(2)}, u32[]{:S(2)}) collective-permute-start(f32[328,128]{1,0:T(8,128)S(1)} %get-tuple-element.27), channel_id=1, source_target_pairs={{0,0},{7,7},{1,2},{2,1},{3,4},{4,3},{5,6},{6,5},{8,8},{15,15},{9,1... | collective-permute-start | bytes 503816 | tf_op jit(solution)/shard_map/ppermute | solution.py:586
  15.1 0.1 collective-permute-start.3
  16.4 1.7 %collective-permute-done.2.cross_ref = f32[328,128]{1,0:T(8,128)S(1)} collective-permute-done((f32[328,128]{1,0:T(8,128)S(1)}, f32[328,128]{1,0:T(8,128)S(1)}, u32[]{:S(2)}, u32[]{:S(2)}) %collective-permute-start.2) | collective-permute-done | bytes 167968 | tf_op jit(solution)/shard_map/ppermute | solution.py:586
  18.1 0.0 collective-permute-done.3.same_ref
  18.1 2.6 %shard_map.58 = (f32[6,24,24,128]{3,2,1,0:T(8,128)S(1)}, f32[16,16,128]{2,1,0:T(8,128)S(1)}, f32[3,16,16,128]{3,2,1,0:T(8,128)S(1)}, f32[4,8,8,128]{3,2,1,0:T(8,...) custom-call(f32[3,16,16,128]{3,2,1,0:T(8,128)S(1)} %get-tuple-elemen, ...), custom_call_target="tpu_custom_call" | custom-call | tf_op jit(solution)/shard_map/pallas_call | solution.py:626
  20.8 1.3 %collective-permute-start.4 = (f32[21,8,128]{2,1,0:T(8,128)S(1)}, f32[21,8,128]{2,1,0:T(8,128)S(1)}, u32[]{:S(2)}, u32[]{:S(2)}) collective-permute-start(f32[21,8,128]{2,1,0:T(8,128)S(1)} %get-tuple-element.33), channel_id=1, source_target_pairs={{0,8},{8,16},{16,24},{24,0},{1,9},{9,17},{17,25},{25,1},{2,10},{10... | collective-permute-start | bytes 258056 | tf_op jit(solution)/shard_map/ppermute | solution.py:578
  22.0 1.2 %collective-permute-start.5 = (f32[21,8,128]{2,1,0:T(8,128)S(1)}, f32[21,8,128]{2,1,0:T(8,128)S(1)}, u32[]{:S(2)}, u32[]{:S(2)}) collective-permute-start(f32[21,8,128]{2,1,0:T(8,128)S(1)} %get-tuple-element.34), channel_id=1, source_target_pairs={{8,0},{16,8},{24,16},{0,24},{9,1},{17,9},{25,17},{1,25},{10,2},{18... | collective-permute-start | bytes 258056 | tf_op jit(solution)/shard_map/ppermute | solution.py:578
  23.2 0.3 collective-permute-start.8
  23.5 2.1 %collective-permute-start.9 = (f32[12,16,128]{2,1,0:T(8,128)S(1)}, f32[12,16,128]{2,1,0:T(8,128)S(1)}, u32[]{:S(2)}, u32[]{:S(2)}) collective-permute-start(f32[12,16,128]{2,1,0:T(8,128)S(1)} %get-tuple-element.38), channel_id=1, source_target_pairs={{8,0},{16,8},{24,16},{0,24},{9,1},{17,9},{25,17},{1,25},{10,2},{18... | collective-permute-start | bytes 294920 | tf_op jit(solution)/shard_map/ppermute | solution.py:578
  25.5 0.4 collective-permute-done.4.left_ref
  25.9 0.6 %collective-permute-done.5.right_ref = f32[21,8,128]{2,1,0:T(8,128)S(1)} collective-permute-done((f32[21,8,128]{2,1,0:T(8,128)S(1)}, f32[21,8,128]{2,1,0:T(8,128)S(1)}, u32[]{:S(2)}, u32[]{:S(2)}) %collective-permute-start.5) | collective-permute-done | bytes 86048 | tf_op jit(solution)/shard_map/ppermute | solution.py:578
  26.5 5.0 %collective-permute-start.6 = (f32[280,128]{1,0:T(8,128)S(1)}, f32[280,128]{1,0:T(8,128)S(1)}, u32[]{:S(2)}, u32[]{:S(2)}) collective-permute-start(f32[280,128]{1,0:T(8,128)S(1)} %get-tuple-element.35.after_ref), channel_id=1, source_target_pairs={{0,0},{7,7},{1,2},{2,1},{3,4},{4,3},{5,6},{6,5},{8,8},{15,15},{9,1... | collective-permute-start | bytes 430088 | tf_op jit(solution)/shard_map/ppermute | solution.py:586
  31.5 0.1 collective-permute-start.7
  31.6 0.0 collective-permute-done.8.left_ref
  31.6 0.0 collective-permute-done.9.right_ref
  31.6 0.1 shard_map.61
  31.7 3.6 %collective-permute-start.10 = (f32[232,128]{1,0:T(8,128)S(1)}, f32[232,128]{1,0:T(8,128)S(1)}, u32[]{:S(2)}, u32[]{:S(2)}) collective-permute-start(f32[232,128]{1,0:T(8,128)S(1)} %get-tuple-element.39), channel_id=1, source_target_pairs={{0,0},{7,7},{1,2},{2,1},{3,4},{4,3},{5,6},{6,5},{8,8},{15,15},{9,1... | collective-permute-start | bytes 356360 | tf_op jit(solution)/shard_map/ppermute | solution.py:586
  35.2 0.1 collective-permute-start.11
  35.3 0.0 collective-permute-done.6.cross_ref
  35.3 0.0 collective-permute-done.7.same_ref
  35.3 2.7 %shard_map.60.change_ref = f32[3,24,24,128]{3,2,1,0:T(8,128)S(1)} custom-call(f32[6,24,24,128]{3,2,1,0:T(8,128)S(1)} %get-tuple-element.29.weight_ref, f32[4,8,8,128]{3,2,1,0:T(8,128)S(1)} %get-tuple-element.32.coarse_ref, f32[1]{0:T(128)S(6)} %copy.6.lower_ref, f32[1]{0:T(128)S(6)} %copy.7.upper_ref, f32[21,8,128]{2,1,0:T(8,128)S(1)} %collective-permute-done.4.left_ref, ...), custom_call_target="tpu_custom_call" | custom-call | tf_op jit(solution)/shard_map/pallas_call | solution.py:656
  38.1 0.0 collective-permute-done.10.cross_ref
  38.1 0.0 collective-permute-done.11.same_ref
  38.1 2.4 %shard_map.62 = f32[3,16,16,128]{3,2,1,0:T(8,128)} custom-call(f32[6,24,24,128]{3,2,1,0:T(8,128)S(1)} %get-tuple-element.29.weight_ref, f32[16,16,128]{2,1,0:T(8,128)S(1)} %get-tuple-element.30.diagonal_ref, f32[3,16,16,128]{3,2,1,0:T(8,128)S(1)} %get-tuple-element.31.smoothed_ref, f32[3,24,24,128]{3,2,1,0:T(8,128)S(1)} %shard_map.60.change_ref, ...), custom_call_target="tpu_custom_call" | custom-call | tf_op jit(solution)/shard_map/pallas_call | solution.py:671
  (1 shorter events, 0.0 us)
Async XLA Ops:
  1.0 6.4 %collective-permute-start = (f32[17,16,128]{2,1,0:T(8,128)S(1)}, f32[17,16,128]{2,1,0:T(8,128)S(1)}, u32[]{:S(2)}, u32[]{:S(2)}) collective-permute-start(f32[17,16,128]{2,1,0:T(8,128)S(1)} %get-tuple-element.25), channel_id=1, source_target_pairs={{0,8},{8,16},{16,24},{24,0},{1,9},{9,17},{17,25},{25,1},{2,10},{10... | collective-permute-start | bytes 417800 | tf_op jit(solution)/shard_map/ppermute | solution.py:578
  3.1 7.3 %collective-permute-start.1 = (f32[17,16,128]{2,1,0:T(8,128)S(1)}, f32[17,16,128]{2,1,0:T(8,128)S(1)}, u32[]{:S(2)}, u32[]{:S(2)}) collective-permute-start(f32[17,16,128]{2,1,0:T(8,128)S(1)} %get-tuple-element.26), channel_id=1, source_target_pairs={{8,0},{16,8},{24,16},{0,24},{9,1},{17,9},{25,17},{1,25},{10,2},{18... | collective-permute-start | bytes 417800 | tf_op jit(solution)/shard_map/ppermute | solution.py:578
  10.4 7.7 %collective-permute-start.2 = (f32[328,128]{1,0:T(8,128)S(1)}, f32[328,128]{1,0:T(8,128)S(1)}, u32[]{:S(2)}, u32[]{:S(2)}) collective-permute-start(f32[328,128]{1,0:T(8,128)S(1)} %get-tuple-element.27), channel_id=1, source_target_pairs={{0,0},{7,7},{1,2},{2,1},{3,4},{4,3},{5,6},{6,5},{8,8},{15,15},{9,1... | collective-permute-start | bytes 503816 | tf_op jit(solution)/shard_map/ppermute | solution.py:586
  15.1 3.0 %collective-permute-start.3 = (f32[328,128]{1,0:T(8,128)S(1)}, f32[328,128]{1,0:T(8,128)S(1)}, u32[]{:S(2)}, u32[]{:S(2)}) collective-permute-start(f32[328,128]{1,0:T(8,128)S(1)} %get-tuple-element.28), channel_id=1, source_target_pairs={{0,1},{1,0},{2,3},{3,2},{4,5},{5,4},{6,7},{7,6},{8,9},{9,8},{10,11... | collective-permute-start | bytes 503816 | tf_op jit(solution)/shard_map/ppermute | solution.py:586
  20.8 5.2 %collective-permute-start.4 = (f32[21,8,128]{2,1,0:T(8,128)S(1)}, f32[21,8,128]{2,1,0:T(8,128)S(1)}, u32[]{:S(2)}, u32[]{:S(2)}) collective-permute-start(f32[21,8,128]{2,1,0:T(8,128)S(1)} %get-tuple-element.33), channel_id=1, source_target_pairs={{0,8},{8,16},{16,24},{24,0},{1,9},{9,17},{17,25},{25,1},{2,10},{10... | collective-permute-start | bytes 258056 | tf_op jit(solution)/shard_map/ppermute | solution.py:578
  22.0 4.5 %collective-permute-start.5 = (f32[21,8,128]{2,1,0:T(8,128)S(1)}, f32[21,8,128]{2,1,0:T(8,128)S(1)}, u32[]{:S(2)}, u32[]{:S(2)}) collective-permute-start(f32[21,8,128]{2,1,0:T(8,128)S(1)} %get-tuple-element.34), channel_id=1, source_target_pairs={{8,0},{16,8},{24,16},{0,24},{9,1},{17,9},{25,17},{1,25},{10,2},{18... | collective-permute-start | bytes 258056 | tf_op jit(solution)/shard_map/ppermute | solution.py:578
  23.2 8.4 %collective-permute-start.8 = (f32[12,16,128]{2,1,0:T(8,128)S(1)}, f32[12,16,128]{2,1,0:T(8,128)S(1)}, u32[]{:S(2)}, u32[]{:S(2)}) collective-permute-start(f32[12,16,128]{2,1,0:T(8,128)S(1)} %get-tuple-element.37), channel_id=1, source_target_pairs={{0,8},{8,16},{16,24},{24,0},{1,9},{9,17},{17,25},{25,1},{2,10},{10... | collective-permute-start | bytes 294920 | tf_op jit(solution)/shard_map/ppermute | solution.py:578
  23.5 8.1 %collective-permute-start.9 = (f32[12,16,128]{2,1,0:T(8,128)S(1)}, f32[12,16,128]{2,1,0:T(8,128)S(1)}, u32[]{:S(2)}, u32[]{:S(2)}) collective-permute-start(f32[12,16,128]{2,1,0:T(8,128)S(1)} %get-tuple-element.38), channel_id=1, source_target_pairs={{8,0},{16,8},{24,16},{0,24},{9,1},{17,9},{25,17},{1,25},{10,2},{18... | collective-permute-start | bytes 294920 | tf_op jit(solution)/shard_map/ppermute | solution.py:578
  26.5 8.8 %collective-permute-start.6 = (f32[280,128]{1,0:T(8,128)S(1)}, f32[280,128]{1,0:T(8,128)S(1)}, u32[]{:S(2)}, u32[]{:S(2)}) collective-permute-start(f32[280,128]{1,0:T(8,128)S(1)} %get-tuple-element.35.after_ref), channel_id=1, source_target_pairs={{0,0},{7,7},{1,2},{2,1},{3,4},{4,3},{5,6},{6,5},{8,8},{15,15},{9,1... | collective-permute-start | bytes 430088 | tf_op jit(solution)/shard_map/ppermute | solution.py:586
  31.5 3.8 %collective-permute-start.7 = (f32[280,128]{1,0:T(8,128)S(1)}, f32[280,128]{1,0:T(8,128)S(1)}, u32[]{:S(2)}, u32[]{:S(2)}) collective-permute-start(f32[280,128]{1,0:T(8,128)S(1)} %get-tuple-element.36), channel_id=1, source_target_pairs={{0,1},{1,0},{2,3},{3,2},{4,5},{5,4},{6,7},{7,6},{8,9},{9,8},{10,11... | collective-permute-start | bytes 430088 | tf_op jit(solution)/shard_map/ppermute | solution.py:586
  31.7 6.4 %collective-permute-start.10 = (f32[232,128]{1,0:T(8,128)S(1)}, f32[232,128]{1,0:T(8,128)S(1)}, u32[]{:S(2)}, u32[]{:S(2)}) collective-permute-start(f32[232,128]{1,0:T(8,128)S(1)} %get-tuple-element.39), channel_id=1, source_target_pairs={{0,0},{7,7},{1,2},{2,1},{3,4},{4,3},{5,6},{6,5},{8,8},{15,15},{9,1... | collective-permute-start | bytes 356360 | tf_op jit(solution)/shard_map/ppermute | solution.py:586
  35.2 2.8 %collective-permute-start.11 = (f32[232,128]{1,0:T(8,128)S(1)}, f32[232,128]{1,0:T(8,128)S(1)}, u32[]{:S(2)}, u32[]{:S(2)}) collective-permute-start(f32[232,128]{1,0:T(8,128)S(1)} %get-tuple-element.40), channel_id=1, source_target_pairs={{0,1},{1,0},{2,3},{3,2},{4,5},{5,4},{6,7},{7,6},{8,9},{9,8},{10,11... | collective-permute-start | bytes 356360 | tf_op jit(solution)/shard_map/ppermute | solution.py:586

commit v6 on v5

--- a/solution.py
+++ b/solution.py
@@ -467,20 +467,24 @@
     for number in range(COARSE_STEPS - 1):
         old, new = ((cd0_ref, cd1_ref), (cd1_ref, cd0_ref))[number % 2]
         last = number + 2 == COARSE_STEPS
+        skip = 0 if number == 0 else 2
+        count = srows if number == 0 else crows - 2 * skip
+        inner, here = pl.ds(skip, count), pl.ds(ROW0 + skip, count)
         for i in range(number + 1, cwidth - 1 - number):
-            weights = [cweight_ref[f, i] for f in range(6)]
+            weights = [cweight_ref[f, i, inner, :] for f in range(6)]
             for s in range(2):
-                own = old[s, i, mid, :]
-                beside = weights[0] * old[s, i - 1, mid, :] + weights[1] * old[s, i + 1, mid, :]
-                beside = beside + weights[2] * old[s, i, pl.ds(ROW0 - 1, srows), :]
-                beside = beside + weights[3] * old[s, i, pl.ds(ROW0 + 1, srows), :]
+                own = old[s, i, here, :]
+                beside = weights[0] * old[s, i - 1, here, :] + weights[1] * old[s, i + 1, here, :]
+                beside = beside + weights[2] * old[s, i, pl.ds(ROW0 + skip - 1, count), :]
+                beside = beside + weights[3] * old[s, i, pl.ds(ROW0 + skip + 1, count), :]
                 beside = beside + weights[4] * below(own, 2) + weights[5] * above(own, 2)
-                fresh = source_ref[s, i] - own + beside
+                fresh = source_ref[s, i, inner, :] - own + beside
                 direction = carried[number] * own + scaled[number] * fresh
                 if not last:
-                    source_ref[s, i] = fresh
-                    new[s, i, mid, :] = direction
-                correction_ref[s, i] = (own if number == 0 else correction_ref[s, i]) + direction
+                    source_ref[s, i, inner, :] = fresh
+                    new[s, i, here, :] = direction
+                before = own if number == 0 else correction_ref[s, i, inner, :]
+                correction_ref[s, i, inner, :] = before + direction
 
     edge = COARSE_HALO - COARSE_REACH
     pwidth, prows = ncx + 2 * COARSE_REACH, half + 2 * COARSE_REACH

time: 41.1 us -> 41 us (level)
  transfers between devices with their start and end apart: 12 -> 12, of which waited for: 5 -> 5; matrix products, arithmetic and copies ran while one was open for 0% -> 0% of each run, Pallas kernels for 10% -> 9%
where the time goes in v6:
time: 41 us; the launch traced here: 40.3 us
  starting transfers between devices  21.3 us (52%)
  Pallas kernels  9.85 us (24%)
  waiting for transfers between devices  7.77 us (19%)
  between operations  1.44 us (4%)
    ppermute x6, starting transfers between devices, swap_y(): return (lax.ppermute(cross, 'gy', others), lax.ppermute(same, 'gy', pairs))  13.4 us
    ppermute x6, starting transfers between devices, ring_x(): return (lax.ppermute(high, 'gx', up), lax.ppermute(low, 'gx', down))  7.9 us
    ppermute x6, waiting for transfers between devices, ring_x(): return (lax.ppermute(high, 'gx', up), lax.ppermute(low, 'gx', down))  6.1 us
    pallas_call x1, Pallas kernels, local(): call(functools.partial(pre_kernel, shape_x, shape_y), [(6, width, rows, d...  2.65 us
    pallas_call x1, Pallas kernels, local(): call(functools.partial(coarse_kernel, shape_x, shape_y), [(parts, width,...  2.59 us
    pallas_call x1, Pallas kernels, local(): call(functools.partial(post_kernel, shape_x, shape_y), [(parts, nx, ny, d...  2.38 us
    ppermute x6, waiting for transfers between devices, swap_y(): return (lax.ppermute(cross, 'gy', others), lax.ppermute(same, 'gy', pairs))  1.67 us
    pallas_call x1, Pallas kernels, local(): call(stage_kernel, [forcing.shape, (nx, ny, depth)], scratch, [pltpu.HBM]...  1.09 us
  transfers between devices with their start and end apart: 12, of which 5 were waited for; matrix products, arithmetic and copies ran while one was open for 0% of the time, Pallas kernels for 9%

profile of v6, /device:TPU:1, one launch (start us, length us, event | category | flops | bytes accessed | tf_op | source)
XLA Modules:
  0.0 40.3 jit_solution(18203589051934664995)
XLA Ops:
  0.0 1.0 %shard_map.56 = (f32[17,16,128]{2,1,0:T(8,128)S(1)}, f32[17,16,128]{2,1,0:T(8,128)S(1)}) custom-call(f32[3,16,16,128]{3,2,1,0:T(8,128)} %forcing_ref.3, s32[16,16,128]{2,1,0:T(8,128)} %phase_ref.3, f32[8]{0:T(128)} %table_ref.3), custom_call_target="tpu_custom_call" | custom-call | tf_op jit(solution)/shard_map/pallas_call | solution.py:614
  1.0 2.1 %collective-permute-start = (f32[17,16,128]{2,1,0:T(8,128)S(1)}, f32[17,16,128]{2,1,0:T(8,128)S(1)}, u32[]{:S(2)}, u32[]{:S(2)}) collective-permute-start(f32[17,16,128]{2,1,0:T(8,128)S(1)} %get-tuple-element.25), channel_id=1, source_target_pairs={{0,8},{8,16},{16,24},{24,0},{1,9},{9,17},{17,25},{25,1},{2,10},{10... | collective-permute-start | bytes 417800 | tf_op jit(solution)/shard_map/ppermute | solution.py:582
  3.1 1.0 %collective-permute-start.1 = (f32[17,16,128]{2,1,0:T(8,128)S(1)}, f32[17,16,128]{2,1,0:T(8,128)S(1)}, u32[]{:S(2)}, u32[]{:S(2)}) collective-permute-start(f32[17,16,128]{2,1,0:T(8,128)S(1)} %get-tuple-element.26), channel_id=1, source_target_pairs={{8,0},{16,8},{24,16},{0,24},{9,1},{17,9},{25,17},{1,25},{10,2},{18... | collective-permute-start | bytes 417800 | tf_op jit(solution)/shard_map/ppermute | solution.py:582
  4.1 1.1 %shard_map.55 = (f32[3,16,16,128]{3,2,1,0:T(8,128)S(1)}, f32[16,16,128]{2,1,0:T(8,128)S(1)}) custom-call(f32[3,16,16,128]{3,2,1,0:T(8,128)} %forcing_ref.3, s32[16,16,128]{2,1,0:T(8,128)} %phase_ref.3, f32[8]{0:T(128)} %table_ref.3), custom_call_target="tpu_custom_call" | custom-call | tf_op jit(solution)/shard_map/pallas_call | solution.py:619
  5.2 2.2 %collective-permute-done.left_ref = f32[17,16,128]{2,1,0:T(8,128)S(1)} collective-permute-done((f32[17,16,128]{2,1,0:T(8,128)S(1)}, f32[17,16,128]{2,1,0:T(8,128)S(1)}, u32[]{:S(2)}, u32[]{:S(2)}) %collective-permute-start) | collective-permute-done | bytes 139296 | tf_op jit(solution)/shard_map/ppermute | solution.py:582
  7.4 2.9 %collective-permute-done.1.right_ref = f32[17,16,128]{2,1,0:T(8,128)S(1)} collective-permute-done((f32[17,16,128]{2,1,0:T(8,128)S(1)}, f32[17,16,128]{2,1,0:T(8,128)S(1)}, u32[]{:S(2)}, u32[]{:S(2)}) %collective-permute-start.1) | collective-permute-done | bytes 139296 | tf_op jit(solution)/shard_map/ppermute | solution.py:582
  10.4 0.1 shard_map.57
  10.4 4.6 %collective-permute-start.2 = (f32[328,128]{1,0:T(8,128)S(1)}, f32[328,128]{1,0:T(8,128)S(1)}, u32[]{:S(2)}, u32[]{:S(2)}) collective-permute-start(f32[328,128]{1,0:T(8,128)S(1)} %get-tuple-element.27), channel_id=1, source_target_pairs={{0,0},{7,7},{1,2},{2,1},{3,4},{4,3},{5,6},{6,5},{8,8},{15,15},{9,1... | collective-permute-start | bytes 503816 | tf_op jit(solution)/shard_map/ppermute | solution.py:590
  15.1 0.1 collective-permute-start.3
  16.4 1.7 %collective-permute-done.2.cross_ref = f32[328,128]{1,0:T(8,128)S(1)} collective-permute-done((f32[328,128]{1,0:T(8,128)S(1)}, f32[328,128]{1,0:T(8,128)S(1)}, u32[]{:S(2)}, u32[]{:S(2)}) %collective-permute-start.2) | collective-permute-done | bytes 167968 | tf_op jit(solution)/shard_map/ppermute | solution.py:590
  18.1 0.0 collective-permute-done.3.same_ref
  18.1 2.6 %shard_map.58 = (f32[6,24,24,128]{3,2,1,0:T(8,128)S(1)}, f32[16,16,128]{2,1,0:T(8,128)S(1)}, f32[3,16,16,128]{3,2,1,0:T(8,128)S(1)}, f32[4,8,8,128]{3,2,1,0:T(8,...) custom-call(f32[3,16,16,128]{3,2,1,0:T(8,128)S(1)} %get-tuple-elemen, ...), custom_call_target="tpu_custom_call" | custom-call | tf_op jit(solution)/shard_map/pallas_call | solution.py:630
  20.8 1.3 %collective-permute-start.4 = (f32[21,8,128]{2,1,0:T(8,128)S(1)}, f32[21,8,128]{2,1,0:T(8,128)S(1)}, u32[]{:S(2)}, u32[]{:S(2)}) collective-permute-start(f32[21,8,128]{2,1,0:T(8,128)S(1)} %get-tuple-element.33), channel_id=1, source_target_pairs={{0,8},{8,16},{16,24},{24,0},{1,9},{9,17},{17,25},{25,1},{2,10},{10... | collective-permute-start | bytes 258056 | tf_op jit(solution)/shard_map/ppermute | solution.py:582
  22.0 1.2 %collective-permute-start.5 = (f32[21,8,128]{2,1,0:T(8,128)S(1)}, f32[21,8,128]{2,1,0:T(8,128)S(1)}, u32[]{:S(2)}, u32[]{:S(2)}) collective-permute-start(f32[21,8,128]{2,1,0:T(8,128)S(1)} %get-tuple-element.34), channel_id=1, source_target_pairs={{8,0},{16,8},{24,16},{0,24},{9,1},{17,9},{25,17},{1,25},{10,2},{18... | collective-permute-start | bytes 258056 | tf_op jit(solution)/shard_map/ppermute | solution.py:582
  23.2 0.3 collective-permute-start.8
  23.5 2.1 %collective-permute-start.9 = (f32[12,16,128]{2,1,0:T(8,128)S(1)}, f32[12,16,128]{2,1,0:T(8,128)S(1)}, u32[]{:S(2)}, u32[]{:S(2)}) collective-permute-start(f32[12,16,128]{2,1,0:T(8,128)S(1)} %get-tuple-element.38), channel_id=1, source_target_pairs={{8,0},{16,8},{24,16},{0,24},{9,1},{17,9},{25,17},{1,25},{10,2},{18... | collective-permute-start | bytes 294920 | tf_op jit(solution)/shard_map/ppermute | solution.py:582
  25.5 0.4 collective-permute-done.4.left_ref
  25.9 0.6 %collective-permute-done.5.right_ref = f32[21,8,128]{2,1,0:T(8,128)S(1)} collective-permute-done((f32[21,8,128]{2,1,0:T(8,128)S(1)}, f32[21,8,128]{2,1,0:T(8,128)S(1)}, u32[]{:S(2)}, u32[]{:S(2)}) %collective-permute-start.5) | collective-permute-done | bytes 86048 | tf_op jit(solution)/shard_map/ppermute | solution.py:582
  26.5 5.0 %collective-permute-start.6 = (f32[280,128]{1,0:T(8,128)S(1)}, f32[280,128]{1,0:T(8,128)S(1)}, u32[]{:S(2)}, u32[]{:S(2)}) collective-permute-start(f32[280,128]{1,0:T(8,128)S(1)} %get-tuple-element.35.after_ref), channel_id=1, source_target_pairs={{0,0},{7,7},{1,2},{2,1},{3,4},{4,3},{5,6},{6,5},{8,8},{15,15},{9,1... | collective-permute-start | bytes 430088 | tf_op jit(solution)/shard_map/ppermute | solution.py:590
  31.5 0.1 collective-permute-start.7
  31.6 0.0 collective-permute-done.8.left_ref
  31.6 0.0 collective-permute-done.9.right_ref
  31.6 0.1 shard_map.61
  31.7 3.6 %collective-permute-start.10 = (f32[232,128]{1,0:T(8,128)S(1)}, f32[232,128]{1,0:T(8,128)S(1)}, u32[]{:S(2)}, u32[]{:S(2)}) collective-permute-start(f32[232,128]{1,0:T(8,128)S(1)} %get-tuple-element.39), channel_id=1, source_target_pairs={{0,0},{7,7},{1,2},{2,1},{3,4},{4,3},{5,6},{6,5},{8,8},{15,15},{9,1... | collective-permute-start | bytes 356360 | tf_op jit(solution)/shard_map/ppermute | solution.py:590
  35.2 0.1 collective-permute-start.11
  35.3 0.0 collective-permute-done.6.cross_ref
  35.3 0.0 collective-permute-done.7.same_ref
  35.3 2.6 %shard_map.60.change_ref = f32[3,24,24,128]{3,2,1,0:T(8,128)S(1)} custom-call(f32[6,24,24,128]{3,2,1,0:T(8,128)S(1)} %get-tuple-element.29.weight_ref, f32[4,8,8,128]{3,2,1,0:T(8,128)S(1)} %get-tuple-element.32.coarse_ref, f32[1]{0:T(128)S(6)} %copy.6.lower_ref, f32[1]{0:T(128)S(6)} %copy.7.upper_ref, f32[21,8,128]{2,1,0:T(8,128)S(1)} %collective-permute-done.4.left_ref, ...), custom_call_target="tpu_custom_call" | custom-call | tf_op jit(solution)/shard_map/pallas_call | solution.py:660
  37.9 0.0 collective-permute-done.10.cross_ref
  37.9 0.0 collective-permute-done.11.same_ref
  38.0 2.4 %shard_map.62 = f32[3,16,16,128]{3,2,1,0:T(8,128)} custom-call(f32[6,24,24,128]{3,2,1,0:T(8,128)S(1)} %get-tuple-element.29.weight_ref, f32[16,16,128]{2,1,0:T(8,128)S(1)} %get-tuple-element.30.diagonal_ref, f32[3,16,16,128]{3,2,1,0:T(8,128)S(1)} %get-tuple-element.31.smoothed_ref, f32[3,24,24,128]{3,2,1,0:T(8,128)S(1)} %shard_map.60.change_ref, ...), custom_call_target="tpu_custom_call" | custom-call | tf_op jit(solution)/shard_map/pallas_call | solution.py:675
  (1 shorter events, 0.0 us)
Async XLA Ops:
  1.0 6.4 %collective-permute-start = (f32[17,16,128]{2,1,0:T(8,128)S(1)}, f32[17,16,128]{2,1,0:T(8,128)S(1)}, u32[]{:S(2)}, u32[]{:S(2)}) collective-permute-start(f32[17,16,128]{2,1,0:T(8,128)S(1)} %get-tuple-element.25), channel_id=1, source_target_pairs={{0,8},{8,16},{16,24},{24,0},{1,9},{9,17},{17,25},{25,1},{2,10},{10... | collective-permute-start | bytes 417800 | tf_op jit(solution)/shard_map/ppermute | solution.py:582
  3.1 7.3 %collective-permute-start.1 = (f32[17,16,128]{2,1,0:T(8,128)S(1)}, f32[17,16,128]{2,1,0:T(8,128)S(1)}, u32[]{:S(2)}, u32[]{:S(2)}) collective-permute-start(f32[17,16,128]{2,1,0:T(8,128)S(1)} %get-tuple-element.26), channel_id=1, source_target_pairs={{8,0},{16,8},{24,16},{0,24},{9,1},{17,9},{25,17},{1,25},{10,2},{18... | collective-permute-start | bytes 417800 | tf_op jit(solution)/shard_map/ppermute | solution.py:582
  10.4 7.7 %collective-permute-start.2 = (f32[328,128]{1,0:T(8,128)S(1)}, f32[328,128]{1,0:T(8,128)S(1)}, u32[]{:S(2)}, u32[]{:S(2)}) collective-permute-start(f32[328,128]{1,0:T(8,128)S(1)} %get-tuple-element.27), channel_id=1, source_target_pairs={{0,0},{7,7},{1,2},{2,1},{3,4},{4,3},{5,6},{6,5},{8,8},{15,15},{9,1... | collective-permute-start | bytes 503816 | tf_op jit(solution)/shard_map/ppermute | solution.py:590
  15.1 3.0 %collective-permute-start.3 = (f32[328,128]{1,0:T(8,128)S(1)}, f32[328,128]{1,0:T(8,128)S(1)}, u32[]{:S(2)}, u32[]{:S(2)}) collective-permute-start(f32[328,128]{1,0:T(8,128)S(1)} %get-tuple-element.28), channel_id=1, source_target_pairs={{0,1},{1,0},{2,3},{3,2},{4,5},{5,4},{6,7},{7,6},{8,9},{9,8},{10,11... | collective-permute-start | bytes 503816 | tf_op jit(solution)/shard_map/ppermute | solution.py:590
  20.8 5.2 %collective-permute-start.4 = (f32[21,8,128]{2,1,0:T(8,128)S(1)}, f32[21,8,128]{2,1,0:T(8,128)S(1)}, u32[]{:S(2)}, u32[]{:S(2)}) collective-permute-start(f32[21,8,128]{2,1,0:T(8,128)S(1)} %get-tuple-element.33), channel_id=1, source_target_pairs={{0,8},{8,16},{16,24},{24,0},{1,9},{9,17},{17,25},{25,1},{2,10},{10... | collective-permute-start | bytes 258056 | tf_op jit(solution)/shard_map/ppermute | solution.py:582
  22.0 4.5 %collective-permute-start.5 = (f32[21,8,128]{2,1,0:T(8,128)S(1)}, f32[21,8,128]{2,1,0:T(8,128)S(1)}, u32[]{:S(2)}, u32[]{:S(2)}) collective-permute-start(f32[21,8,128]{2,1,0:T(8,128)S(1)} %get-tuple-element.34), channel_id=1, source_target_pairs={{8,0},{16,8},{24,16},{0,24},{9,1},{17,9},{25,17},{1,25},{10,2},{18... | collective-permute-start | bytes 258056 | tf_op jit(solution)/shard_map/ppermute | solution.py:582
  23.2 8.4 %collective-permute-start.8 = (f32[12,16,128]{2,1,0:T(8,128)S(1)}, f32[12,16,128]{2,1,0:T(8,128)S(1)}, u32[]{:S(2)}, u32[]{:S(2)}) collective-permute-start(f32[12,16,128]{2,1,0:T(8,128)S(1)} %get-tuple-element.37), channel_id=1, source_target_pairs={{0,8},{8,16},{16,24},{24,0},{1,9},{9,17},{17,25},{25,1},{2,10},{10... | collective-permute-start | bytes 294920 | tf_op jit(solution)/shard_map/ppermute | solution.py:582
  23.5 8.1 %collective-permute-start.9 = (f32[12,16,128]{2,1,0:T(8,128)S(1)}, f32[12,16,128]{2,1,0:T(8,128)S(1)}, u32[]{:S(2)}, u32[]{:S(2)}) collective-permute-start(f32[12,16,128]{2,1,0:T(8,128)S(1)} %get-tuple-element.38), channel_id=1, source_target_pairs={{8,0},{16,8},{24,16},{0,24},{9,1},{17,9},{25,17},{1,25},{10,2},{18... | collective-permute-start | bytes 294920 | tf_op jit(solution)/shard_map/ppermute | solution.py:582
  26.5 8.8 %collective-permute-start.6 = (f32[280,128]{1,0:T(8,128)S(1)}, f32[280,128]{1,0:T(8,128)S(1)}, u32[]{:S(2)}, u32[]{:S(2)}) collective-permute-start(f32[280,128]{1,0:T(8,128)S(1)} %get-tuple-element.35.after_ref), channel_id=1, source_target_pairs={{0,0},{7,7},{1,2},{2,1},{3,4},{4,3},{5,6},{6,5},{8,8},{15,15},{9,1... | collective-permute-start | bytes 430088 | tf_op jit(solution)/shard_map/ppermute | solution.py:590
  31.5 3.8 %collective-permute-start.7 = (f32[280,128]{1,0:T(8,128)S(1)}, f32[280,128]{1,0:T(8,128)S(1)}, u32[]{:S(2)}, u32[]{:S(2)}) collective-permute-start(f32[280,128]{1,0:T(8,128)S(1)} %get-tuple-element.36), channel_id=1, source_target_pairs={{0,1},{1,0},{2,3},{3,2},{4,5},{5,4},{6,7},{7,6},{8,9},{9,8},{10,11... | collective-permute-start | bytes 430088 | tf_op jit(solution)/shard_map/ppermute | solution.py:590
  31.7 6.3 %collective-permute-start.10 = (f32[232,128]{1,0:T(8,128)S(1)}, f32[232,128]{1,0:T(8,128)S(1)}, u32[]{:S(2)}, u32[]{:S(2)}) collective-permute-start(f32[232,128]{1,0:T(8,128)S(1)} %get-tuple-element.39), channel_id=1, source_target_pairs={{0,0},{7,7},{1,2},{2,1},{3,4},{4,3},{5,6},{6,5},{8,8},{15,15},{9,1... | collective-permute-start | bytes 356360 | tf_op jit(solution)/shard_map/ppermute | solution.py:590
  35.2 2.7 %collective-permute-start.11 = (f32[232,128]{1,0:T(8,128)S(1)}, f32[232,128]{1,0:T(8,128)S(1)}, u32[]{:S(2)}, u32[]{:S(2)}) collective-permute-start(f32[232,128]{1,0:T(8,128)S(1)} %get-tuple-element.40), channel_id=1, source_target_pairs={{0,1},{1,0},{2,3},{3,2},{4,5},{5,4},{6,7},{7,6},{8,9},{9,8},{10,11... | collective-permute-start | bytes 356360 | tf_op jit(solution)/shard_map/ppermute | solution.py:590

commit v7 on v6

--- a/solution.py
+++ b/solution.py
@@ -183,9 +183,10 @@
         old = base_ref if number == 0 else d_refs[number % 2]
         new = d_refs[(number + 1) % 2]
         last = number + 1 == CHEB
-        skip, count = (HALO, rows - 2 * HALO) if last else (0, rows)
-        inner = pl.ds(skip, count)
         for x in range(number + 1, width - 1 - number):
+            outermost = x in (number + 1, width - 2 - number)
+            skip, count = (HALO, rows - 2 * HALO) if last or outermost else (0, rows)
+            inner = pl.ds(skip, count)
             weights = [weight_ref[f, x, inner, :] for f in range(6)]
             for c in range(parts):
                 own = old[c, x, pl.ds(ROW0 + skip, count), :]
@@ -202,8 +203,8 @@
                 if last:
                     finish(c, x, fresh)
                 else:
-                    residual_ref[c, x] = fresh
-                    new[c, x, pl.ds(ROW0, rows), :] = carried[number] * own + scaled[number] * fresh
+                    residual_ref[c, x, inner, :] = fresh
+                    new[c, x, pl.ds(ROW0 + skip, count), :] = carried[number] * own + scaled[number] * fresh
 
 
 def masked(inside, has_low, has_high, own, low, high):

time: 41 us -> 40.9 us (level)
  no operation moved by 1% of the time
where the time goes in v7:
time: 40.9 us; the launch traced here: 40.2 us
  starting transfers between devices  21.3 us (52%)
  Pallas kernels  9.76 us (24%)
  waiting for transfers between devices  7.77 us (19%)
  between operations  1.44 us (4%)
    ppermute x6, starting transfers between devices, swap_y(): return (lax.ppermute(cross, 'gy', others), lax.ppermute(same, 'gy', pairs))  13.4 us
    ppermute x6, starting transfers between devices, ring_x(): return (lax.ppermute(high, 'gx', up), lax.ppermute(low, 'gx', down))  7.9 us
    ppermute x6, waiting for transfers between devices, ring_x(): return (lax.ppermute(high, 'gx', up), lax.ppermute(low, 'gx', down))  6.1 us
    pallas_call x1, Pallas kernels, local(): call(functools.partial(coarse_kernel, shape_x, shape_y), [(parts, width,...  2.59 us
    pallas_call x1, Pallas kernels, local(): call(functools.partial(pre_kernel, shape_x, shape_y), [(6, width, rows, d...  2.57 us
    pallas_call x1, Pallas kernels, local(): call(functools.partial(post_kernel, shape_x, shape_y), [(parts, nx, ny, d...  2.36 us
    ppermute x6, waiting for transfers between devices, swap_y(): return (lax.ppermute(cross, 'gy', others), lax.ppermute(same, 'gy', pairs))  1.67 us
    pallas_call x1, Pallas kernels, local(): call(stage_kernel, [forcing.shape, (nx, ny, depth)], scratch, [pltpu.HBM]...  1.09 us
  transfers between devices with their start and end apart: 12, of which 5 were waited for; matrix products, arithmetic and copies ran while one was open for 0% of the time, Pallas kernels for 9%

profile of v7, /device:TPU:1, one launch (start us, length us, event | category | flops | bytes accessed | tf_op | source)
XLA Modules:
  0.0 40.2 jit_solution(11373025647717287661)
XLA Ops:
  0.0 1.0 %shard_map.56 = (f32[17,16,128]{2,1,0:T(8,128)S(1)}, f32[17,16,128]{2,1,0:T(8,128)S(1)}) custom-call(f32[3,16,16,128]{3,2,1,0:T(8,128)} %forcing_ref.3, s32[16,16,128]{2,1,0:T(8,128)} %phase_ref.3, f32[8]{0:T(128)} %table_ref.3), custom_call_target="tpu_custom_call" | custom-call | tf_op jit(solution)/shard_map/pallas_call | solution.py:615
  1.0 2.1 %collective-permute-start = (f32[17,16,128]{2,1,0:T(8,128)S(1)}, f32[17,16,128]{2,1,0:T(8,128)S(1)}, u32[]{:S(2)}, u32[]{:S(2)}) collective-permute-start(f32[17,16,128]{2,1,0:T(8,128)S(1)} %get-tuple-element.25), channel_id=1, source_target_pairs={{0,8},{8,16},{16,24},{24,0},{1,9},{9,17},{17,25},{25,1},{2,10},{10... | collective-permute-start | bytes 417800 | tf_op jit(solution)/shard_map/ppermute | solution.py:583
  3.1 1.0 %collective-permute-start.1 = (f32[17,16,128]{2,1,0:T(8,128)S(1)}, f32[17,16,128]{2,1,0:T(8,128)S(1)}, u32[]{:S(2)}, u32[]{:S(2)}) collective-permute-start(f32[17,16,128]{2,1,0:T(8,128)S(1)} %get-tuple-element.26), channel_id=1, source_target_pairs={{8,0},{16,8},{24,16},{0,24},{9,1},{17,9},{25,17},{1,25},{10,2},{18... | collective-permute-start | bytes 417800 | tf_op jit(solution)/shard_map/ppermute | solution.py:583
  4.1 1.1 %shard_map.55 = (f32[3,16,16,128]{3,2,1,0:T(8,128)S(1)}, f32[16,16,128]{2,1,0:T(8,128)S(1)}) custom-call(f32[3,16,16,128]{3,2,1,0:T(8,128)} %forcing_ref.3, s32[16,16,128]{2,1,0:T(8,128)} %phase_ref.3, f32[8]{0:T(128)} %table_ref.3), custom_call_target="tpu_custom_call" | custom-call | tf_op jit(solution)/shard_map/pallas_call | solution.py:620
  5.2 2.2 %collective-permute-done.left_ref = f32[17,16,128]{2,1,0:T(8,128)S(1)} collective-permute-done((f32[17,16,128]{2,1,0:T(8,128)S(1)}, f32[17,16,128]{2,1,0:T(8,128)S(1)}, u32[]{:S(2)}, u32[]{:S(2)}) %collective-permute-start) | collective-permute-done | bytes 139296 | tf_op jit(solution)/shard_map/ppermute | solution.py:583
  7.4 2.9 %collective-permute-done.1.right_ref = f32[17,16,128]{2,1,0:T(8,128)S(1)} collective-permute-done((f32[17,16,128]{2,1,0:T(8,128)S(1)}, f32[17,16,128]{2,1,0:T(8,128)S(1)}, u32[]{:S(2)}, u32[]{:S(2)}) %collective-permute-start.1) | collective-permute-done | bytes 139296 | tf_op jit(solution)/shard_map/ppermute | solution.py:583
  10.4 0.1 shard_map.57
  10.4 4.6 %collective-permute-start.2 = (f32[328,128]{1,0:T(8,128)S(1)}, f32[328,128]{1,0:T(8,128)S(1)}, u32[]{:S(2)}, u32[]{:S(2)}) collective-permute-start(f32[328,128]{1,0:T(8,128)S(1)} %get-tuple-element.27), channel_id=1, source_target_pairs={{0,0},{7,7},{1,2},{2,1},{3,4},{4,3},{5,6},{6,5},{8,8},{15,15},{9,1... | collective-permute-start | bytes 503816 | tf_op jit(solution)/shard_map/ppermute | solution.py:591
  15.1 0.1 collective-permute-start.3
  16.4 1.7 %collective-permute-done.2.cross_ref = f32[328,128]{1,0:T(8,128)S(1)} collective-permute-done((f32[328,128]{1,0:T(8,128)S(1)}, f32[328,128]{1,0:T(8,128)S(1)}, u32[]{:S(2)}, u32[]{:S(2)}) %collective-permute-start.2) | collective-permute-done | bytes 167968 | tf_op jit(solution)/shard_map/ppermute | solution.py:591
  18.1 0.0 collective-permute-done.3.same_ref
  18.1 2.6 %shard_map.58 = (f32[6,24,24,128]{3,2,1,0:T(8,128)S(1)}, f32[16,16,128]{2,1,0:T(8,128)S(1)}, f32[3,16,16,128]{3,2,1,0:T(8,128)S(1)}, f32[4,8,8,128]{3,2,1,0:T(8,...) custom-call(f32[3,16,16,128]{3,2,1,0:T(8,128)S(1)} %get-tuple-elemen, ...), custom_call_target="tpu_custom_call" | custom-call | tf_op jit(solution)/shard_map/pallas_call | solution.py:631
  20.7 1.3 %collective-permute-start.4 = (f32[21,8,128]{2,1,0:T(8,128)S(1)}, f32[21,8,128]{2,1,0:T(8,128)S(1)}, u32[]{:S(2)}, u32[]{:S(2)}) collective-permute-start(f32[21,8,128]{2,1,0:T(8,128)S(1)} %get-tuple-element.33), channel_id=1, source_target_pairs={{0,8},{8,16},{16,24},{24,0},{1,9},{9,17},{17,25},{25,1},{2,10},{10... | collective-permute-start | bytes 258056 | tf_op jit(solution)/shard_map/ppermute | solution.py:583
  21.9 1.2 %collective-permute-start.5 = (f32[21,8,128]{2,1,0:T(8,128)S(1)}, f32[21,8,128]{2,1,0:T(8,128)S(1)}, u32[]{:S(2)}, u32[]{:S(2)}) collective-permute-start(f32[21,8,128]{2,1,0:T(8,128)S(1)} %get-tuple-element.34), channel_id=1, source_target_pairs={{8,0},{16,8},{24,16},{0,24},{9,1},{17,9},{25,17},{1,25},{10,2},{18... | collective-permute-start | bytes 258056 | tf_op jit(solution)/shard_map/ppermute | solution.py:583
  23.1 0.3 collective-permute-start.8
  23.4 2.1 %collective-permute-start.9 = (f32[12,16,128]{2,1,0:T(8,128)S(1)}, f32[12,16,128]{2,1,0:T(8,128)S(1)}, u32[]{:S(2)}, u32[]{:S(2)}) collective-permute-start(f32[12,16,128]{2,1,0:T(8,128)S(1)} %get-tuple-element.38), channel_id=1, source_target_pairs={{8,0},{16,8},{24,16},{0,24},{9,1},{17,9},{25,17},{1,25},{10,2},{18... | collective-permute-start | bytes 294920 | tf_op jit(solution)/shard_map/ppermute | solution.py:583
  25.5 0.4 collective-permute-done.4.left_ref
  25.8 0.6 %collective-permute-done.5.right_ref = f32[21,8,128]{2,1,0:T(8,128)S(1)} collective-permute-done((f32[21,8,128]{2,1,0:T(8,128)S(1)}, f32[21,8,128]{2,1,0:T(8,128)S(1)}, u32[]{:S(2)}, u32[]{:S(2)}) %collective-permute-start.5) | collective-permute-done | bytes 86048 | tf_op jit(solution)/shard_map/ppermute | solution.py:583
  26.5 5.0 %collective-permute-start.6 = (f32[280,128]{1,0:T(8,128)S(1)}, f32[280,128]{1,0:T(8,128)S(1)}, u32[]{:S(2)}, u32[]{:S(2)}) collective-permute-start(f32[280,128]{1,0:T(8,128)S(1)} %get-tuple-element.35.after_ref), channel_id=1, source_target_pairs={{0,0},{7,7},{1,2},{2,1},{3,4},{4,3},{5,6},{6,5},{8,8},{15,15},{9,1... | collective-permute-start | bytes 430088 | tf_op jit(solution)/shard_map/ppermute | solution.py:591
  31.4 0.1 collective-permute-start.7
  31.5 0.0 collective-permute-done.8.left_ref
  31.5 0.0 collective-permute-done.9.right_ref
  31.5 0.1 shard_map.61
  31.6 3.6 %collective-permute-start.10 = (f32[232,128]{1,0:T(8,128)S(1)}, f32[232,128]{1,0:T(8,128)S(1)}, u32[]{:S(2)}, u32[]{:S(2)}) collective-permute-start(f32[232,128]{1,0:T(8,128)S(1)} %get-tuple-element.39), channel_id=1, source_target_pairs={{0,0},{7,7},{1,2},{2,1},{3,4},{4,3},{5,6},{6,5},{8,8},{15,15},{9,1... | collective-permute-start | bytes 356360 | tf_op jit(solution)/shard_map/ppermute | solution.py:591
  35.2 0.1 collective-permute-start.11
  35.2 0.0 collective-permute-done.6.cross_ref
  35.3 0.0 collective-permute-done.7.same_ref
  35.3 2.6 %shard_map.60.change_ref = f32[3,24,24,128]{3,2,1,0:T(8,128)S(1)} custom-call(f32[6,24,24,128]{3,2,1,0:T(8,128)S(1)} %get-tuple-element.29.weight_ref, f32[4,8,8,128]{3,2,1,0:T(8,128)S(1)} %get-tuple-element.32.coarse_ref, f32[1]{0:T(128)S(6)} %copy.6.lower_ref, f32[1]{0:T(128)S(6)} %copy.7.upper_ref, f32[21,8,128]{2,1,0:T(8,128)S(1)} %collective-permute-done.4.left_ref, ...), custom_call_target="tpu_custom_call" | custom-call | tf_op jit(solution)/shard_map/pallas_call | solution.py:661
  37.9 0.0 collective-permute-done.10.cross_ref
  37.9 0.0 collective-permute-done.11.same_ref
  37.9 2.4 %shard_map.62 = f32[3,16,16,128]{3,2,1,0:T(8,128)} custom-call(f32[6,24,24,128]{3,2,1,0:T(8,128)S(1)} %get-tuple-element.29.weight_ref, f32[16,16,128]{2,1,0:T(8,128)S(1)} %get-tuple-element.30.diagonal_ref, f32[3,16,16,128]{3,2,1,0:T(8,128)S(1)} %get-tuple-element.31.smoothed_ref, f32[3,24,24,128]{3,2,1,0:T(8,128)S(1)} %shard_map.60.change_ref, ...), custom_call_target="tpu_custom_call" | custom-call | tf_op jit(solution)/shard_map/pallas_call | solution.py:676
  (1 shorter events, 0.0 us)
Async XLA Ops:
  1.0 6.4 %collective-permute-start = (f32[17,16,128]{2,1,0:T(8,128)S(1)}, f32[17,16,128]{2,1,0:T(8,128)S(1)}, u32[]{:S(2)}, u32[]{:S(2)}) collective-permute-start(f32[17,16,128]{2,1,0:T(8,128)S(1)} %get-tuple-element.25), channel_id=1, source_target_pairs={{0,8},{8,16},{16,24},{24,0},{1,9},{9,17},{17,25},{25,1},{2,10},{10... | collective-permute-start | bytes 417800 | tf_op jit(solution)/shard_map/ppermute | solution.py:583
  3.1 7.3 %collective-permute-start.1 = (f32[17,16,128]{2,1,0:T(8,128)S(1)}, f32[17,16,128]{2,1,0:T(8,128)S(1)}, u32[]{:S(2)}, u32[]{:S(2)}) collective-permute-start(f32[17,16,128]{2,1,0:T(8,128)S(1)} %get-tuple-element.26), channel_id=1, source_target_pairs={{8,0},{16,8},{24,16},{0,24},{9,1},{17,9},{25,17},{1,25},{10,2},{18... | collective-permute-start | bytes 417800 | tf_op jit(solution)/shard_map/ppermute | solution.py:583
  10.4 7.7 %collective-permute-start.2 = (f32[328,128]{1,0:T(8,128)S(1)}, f32[328,128]{1,0:T(8,128)S(1)}, u32[]{:S(2)}, u32[]{:S(2)}) collective-permute-start(f32[328,128]{1,0:T(8,128)S(1)} %get-tuple-element.27), channel_id=1, source_target_pairs={{0,0},{7,7},{1,2},{2,1},{3,4},{4,3},{5,6},{6,5},{8,8},{15,15},{9,1... | collective-permute-start | bytes 503816 | tf_op jit(solution)/shard_map/ppermute | solution.py:591
  15.1 3.0 %collective-permute-start.3 = (f32[328,128]{1,0:T(8,128)S(1)}, f32[328,128]{1,0:T(8,128)S(1)}, u32[]{:S(2)}, u32[]{:S(2)}) collective-permute-start(f32[328,128]{1,0:T(8,128)S(1)} %get-tuple-element.28), channel_id=1, source_target_pairs={{0,1},{1,0},{2,3},{3,2},{4,5},{5,4},{6,7},{7,6},{8,9},{9,8},{10,11... | collective-permute-start | bytes 503816 | tf_op jit(solution)/shard_map/ppermute | solution.py:591
  20.7 5.2 %collective-permute-start.4 = (f32[21,8,128]{2,1,0:T(8,128)S(1)}, f32[21,8,128]{2,1,0:T(8,128)S(1)}, u32[]{:S(2)}, u32[]{:S(2)}) collective-permute-start(f32[21,8,128]{2,1,0:T(8,128)S(1)} %get-tuple-element.33), channel_id=1, source_target_pairs={{0,8},{8,16},{16,24},{24,0},{1,9},{9,17},{17,25},{25,1},{2,10},{10... | collective-permute-start | bytes 258056 | tf_op jit(solution)/shard_map/ppermute | solution.py:583
  21.9 4.5 %collective-permute-start.5 = (f32[21,8,128]{2,1,0:T(8,128)S(1)}, f32[21,8,128]{2,1,0:T(8,128)S(1)}, u32[]{:S(2)}, u32[]{:S(2)}) collective-permute-start(f32[21,8,128]{2,1,0:T(8,128)S(1)} %get-tuple-element.34), channel_id=1, source_target_pairs={{8,0},{16,8},{24,16},{0,24},{9,1},{17,9},{25,17},{1,25},{10,2},{18... | collective-permute-start | bytes 258056 | tf_op jit(solution)/shard_map/ppermute | solution.py:583
  23.1 8.4 %collective-permute-start.8 = (f32[12,16,128]{2,1,0:T(8,128)S(1)}, f32[12,16,128]{2,1,0:T(8,128)S(1)}, u32[]{:S(2)}, u32[]{:S(2)}) collective-permute-start(f32[12,16,128]{2,1,0:T(8,128)S(1)} %get-tuple-element.37), channel_id=1, source_target_pairs={{0,8},{8,16},{16,24},{24,0},{1,9},{9,17},{17,25},{25,1},{2,10},{10... | collective-permute-start | bytes 294920 | tf_op jit(solution)/shard_map/ppermute | solution.py:583
  23.4 8.1 %collective-permute-start.9 = (f32[12,16,128]{2,1,0:T(8,128)S(1)}, f32[12,16,128]{2,1,0:T(8,128)S(1)}, u32[]{:S(2)}, u32[]{:S(2)}) collective-permute-start(f32[12,16,128]{2,1,0:T(8,128)S(1)} %get-tuple-element.38), channel_id=1, source_target_pairs={{8,0},{16,8},{24,16},{0,24},{9,1},{17,9},{25,17},{1,25},{10,2},{18... | collective-permute-start | bytes 294920 | tf_op jit(solution)/shard_map/ppermute | solution.py:583
  26.5 8.8 %collective-permute-start.6 = (f32[280,128]{1,0:T(8,128)S(1)}, f32[280,128]{1,0:T(8,128)S(1)}, u32[]{:S(2)}, u32[]{:S(2)}) collective-permute-start(f32[280,128]{1,0:T(8,128)S(1)} %get-tuple-element.35.after_ref), channel_id=1, source_target_pairs={{0,0},{7,7},{1,2},{2,1},{3,4},{4,3},{5,6},{6,5},{8,8},{15,15},{9,1... | collective-permute-start | bytes 430088 | tf_op jit(solution)/shard_map/ppermute | solution.py:591
  31.4 3.8 %collective-permute-start.7 = (f32[280,128]{1,0:T(8,128)S(1)}, f32[280,128]{1,0:T(8,128)S(1)}, u32[]{:S(2)}, u32[]{:S(2)}) collective-permute-start(f32[280,128]{1,0:T(8,128)S(1)} %get-tuple-element.36), channel_id=1, source_target_pairs={{0,1},{1,0},{2,3},{3,2},{4,5},{5,4},{6,7},{7,6},{8,9},{9,8},{10,11... | collective-permute-start | bytes 430088 | tf_op jit(solution)/shard_map/ppermute | solution.py:591
  31.6 6.3 %collective-permute-start.10 = (f32[232,128]{1,0:T(8,128)S(1)}, f32[232,128]{1,0:T(8,128)S(1)}, u32[]{:S(2)}, u32[]{:S(2)}) collective-permute-start(f32[232,128]{1,0:T(8,128)S(1)} %get-tuple-element.39), channel_id=1, source_target_pairs={{0,0},{7,7},{1,2},{2,1},{3,4},{4,3},{5,6},{6,5},{8,8},{15,15},{9,1... | collective-permute-start | bytes 356360 | tf_op jit(solution)/shard_map/ppermute | solution.py:591
  35.2 2.7 %collective-permute-start.11 = (f32[232,128]{1,0:T(8,128)S(1)}, f32[232,128]{1,0:T(8,128)S(1)}, u32[]{:S(2)}, u32[]{:S(2)}) collective-permute-start(f32[232,128]{1,0:T(8,128)S(1)} %get-tuple-element.40), channel_id=1, source_target_pairs={{0,1},{1,0},{2,3},{3,2},{4,5},{5,4},{6,7},{7,6},{8,9},{9,8},{10,11... | collective-permute-start | bytes 356360 | tf_op jit(solution)/shard_map/ppermute | solution.py:591

commit v8 on v7

--- a/solution.py
+++ b/solution.py
@@ -468,10 +468,11 @@
     for number in range(COARSE_STEPS - 1):
         old, new = ((cd0_ref, cd1_ref), (cd1_ref, cd0_ref))[number % 2]
         last = number + 2 == COARSE_STEPS
-        skip = 0 if number == 0 else 2
-        count = srows if number == 0 else crows - 2 * skip
-        inner, here = pl.ds(skip, count), pl.ds(ROW0 + skip, count)
         for i in range(number + 1, cwidth - 1 - number):
+            outermost = i in (number + 1, cwidth - 2 - number)
+            skip = COARSE_HALO if outermost else 0 if number == 0 else 2
+            count = srows if skip == 0 else crows - 2 * skip
+            inner, here = pl.ds(skip, count), pl.ds(ROW0 + skip, count)
             weights = [cweight_ref[f, i, inner, :] for f in range(6)]
             for s in range(2):
                 own = old[s, i, here, :]

time: 40.9 us -> 40.9 us (level)
  no operation moved by 1% of the time
where the time goes in v8:
time: 40.9 us; the launch traced here: 40.2 us
  starting transfers between devices  21.3 us (52%)
  Pallas kernels  9.74 us (24%)
  waiting for transfers between devices  7.77 us (19%)
  between operations  1.44 us (4%)
    ppermute x6, starting transfers between devices, swap_y(): return (lax.ppermute(cross, 'gy', others), lax.ppermute(same, 'gy', pairs))  13.4 us
    ppermute x6, starting transfers between devices, ring_x(): return (lax.ppermute(high, 'gx', up), lax.ppermute(low, 'gx', down))  7.9 us
    ppermute x6, waiting for transfers between devices, ring_x(): return (lax.ppermute(high, 'gx', up), lax.ppermute(low, 'gx', down))  6.1 us
    pallas_call x1, Pallas kernels, local(): call(functools.partial(pre_kernel, shape_x, shape_y), [(6, width, rows, d...  2.57 us
    pallas_call x1, Pallas kernels, local(): call(functools.partial(coarse_kernel, shape_x, shape_y), [(parts, width,...  2.57 us
    pallas_call x1, Pallas kernels, local(): call(functools.partial(post_kernel, shape_x, shape_y), [(parts, nx, ny, d...  2.36 us
    ppermute x6, waiting for transfers between devices, swap_y(): return (lax.ppermute(cross, 'gy', others), lax.ppermute(same, 'gy', pairs))  1.67 us
    pallas_call x1, Pallas kernels, local(): call(stage_kernel, [forcing.shape, (nx, ny, depth)], scratch, [pltpu.HBM]...  1.09 us
  transfers between devices with their start and end apart: 12, of which 5 were waited for; matrix products, arithmetic and copies ran while one was open for 0% of the time, Pallas kernels for 9%

profile of v8, /device:TPU:1, one launch (start us, length us, event | category | flops | bytes accessed | tf_op | source)
XLA Modules:
  0.0 40.2 jit_solution(7826530118741919811)
XLA Ops:
  0.0 1.0 %shard_map.56 = (f32[17,16,128]{2,1,0:T(8,128)S(1)}, f32[17,16,128]{2,1,0:T(8,128)S(1)}) custom-call(f32[3,16,16,128]{3,2,1,0:T(8,128)} %forcing_ref.3, s32[16,16,128]{2,1,0:T(8,128)} %phase_ref.3, f32[8]{0:T(128)} %table_ref.3), custom_call_target="tpu_custom_call" | custom-call | tf_op jit(solution)/shard_map/pallas_call | solution.py:616
  1.0 2.1 %collective-permute-start = (f32[17,16,128]{2,1,0:T(8,128)S(1)}, f32[17,16,128]{2,1,0:T(8,128)S(1)}, u32[]{:S(2)}, u32[]{:S(2)}) collective-permute-start(f32[17,16,128]{2,1,0:T(8,128)S(1)} %get-tuple-element.25), channel_id=1, source_target_pairs={{0,8},{8,16},{16,24},{24,0},{1,9},{9,17},{17,25},{25,1},{2,10},{10... | collective-permute-start | bytes 417800 | tf_op jit(solution)/shard_map/ppermute | solution.py:584
  3.1 1.0 %collective-permute-start.1 = (f32[17,16,128]{2,1,0:T(8,128)S(1)}, f32[17,16,128]{2,1,0:T(8,128)S(1)}, u32[]{:S(2)}, u32[]{:S(2)}) collective-permute-start(f32[17,16,128]{2,1,0:T(8,128)S(1)} %get-tuple-element.26), channel_id=1, source_target_pairs={{8,0},{16,8},{24,16},{0,24},{9,1},{17,9},{25,17},{1,25},{10,2},{18... | collective-permute-start | bytes 417800 | tf_op jit(solution)/shard_map/ppermute | solution.py:584
  4.1 1.1 %shard_map.55 = (f32[3,16,16,128]{3,2,1,0:T(8,128)S(1)}, f32[16,16,128]{2,1,0:T(8,128)S(1)}) custom-call(f32[3,16,16,128]{3,2,1,0:T(8,128)} %forcing_ref.3, s32[16,16,128]{2,1,0:T(8,128)} %phase_ref.3, f32[8]{0:T(128)} %table_ref.3), custom_call_target="tpu_custom_call" | custom-call | tf_op jit(solution)/shard_map/pallas_call | solution.py:621
  5.2 2.2 %collective-permute-done.left_ref = f32[17,16,128]{2,1,0:T(8,128)S(1)} collective-permute-done((f32[17,16,128]{2,1,0:T(8,128)S(1)}, f32[17,16,128]{2,1,0:T(8,128)S(1)}, u32[]{:S(2)}, u32[]{:S(2)}) %collective-permute-start) | collective-permute-done | bytes 139296 | tf_op jit(solution)/shard_map/ppermute | solution.py:584
  7.4 2.9 %collective-permute-done.1.right_ref = f32[17,16,128]{2,1,0:T(8,128)S(1)} collective-permute-done((f32[17,16,128]{2,1,0:T(8,128)S(1)}, f32[17,16,128]{2,1,0:T(8,128)S(1)}, u32[]{:S(2)}, u32[]{:S(2)}) %collective-permute-start.1) | collective-permute-done | bytes 139296 | tf_op jit(solution)/shard_map/ppermute | solution.py:584
  10.4 0.1 shard_map.57
  10.4 4.6 %collective-permute-start.2 = (f32[328,128]{1,0:T(8,128)S(1)}, f32[328,128]{1,0:T(8,128)S(1)}, u32[]{:S(2)}, u32[]{:S(2)}) collective-permute-start(f32[328,128]{1,0:T(8,128)S(1)} %get-tuple-element.27), channel_id=1, source_target_pairs={{0,0},{7,7},{1,2},{2,1},{3,4},{4,3},{5,6},{6,5},{8,8},{15,15},{9,1... | collective-permute-start | bytes 503816 | tf_op jit(solution)/shard_map/ppermute | solution.py:592
  15.1 0.1 collective-permute-start.3
  16.4 1.7 %collective-permute-done.2.cross_ref = f32[328,128]{1,0:T(8,128)S(1)} collective-permute-done((f32[328,128]{1,0:T(8,128)S(1)}, f32[328,128]{1,0:T(8,128)S(1)}, u32[]{:S(2)}, u32[]{:S(2)}) %collective-permute-start.2) | collective-permute-done | bytes 167968 | tf_op jit(solution)/shard_map/ppermute | solution.py:592
  18.1 0.0 collective-permute-done.3.same_ref
  18.1 2.6 %shard_map.58 = (f32[6,24,24,128]{3,2,1,0:T(8,128)S(1)}, f32[16,16,128]{2,1,0:T(8,128)S(1)}, f32[3,16,16,128]{3,2,1,0:T(8,128)S(1)}, f32[4,8,8,128]{3,2,1,0:T(8,...) custom-call(f32[3,16,16,128]{3,2,1,0:T(8,128)S(1)} %get-tuple-elemen, ...), custom_call_target="tpu_custom_call" | custom-call | tf_op jit(solution)/shard_map/pallas_call | solution.py:632
  20.7 1.3 %collective-permute-start.4 = (f32[21,8,128]{2,1,0:T(8,128)S(1)}, f32[21,8,128]{2,1,0:T(8,128)S(1)}, u32[]{:S(2)}, u32[]{:S(2)}) collective-permute-start(f32[21,8,128]{2,1,0:T(8,128)S(1)} %get-tuple-element.33), channel_id=1, source_target_pairs={{0,8},{8,16},{16,24},{24,0},{1,9},{9,17},{17,25},{25,1},{2,10},{10... | collective-permute-start | bytes 258056 | tf_op jit(solution)/shard_map/ppermute | solution.py:584
  21.9 1.2 %collective-permute-start.5 = (f32[21,8,128]{2,1,0:T(8,128)S(1)}, f32[21,8,128]{2,1,0:T(8,128)S(1)}, u32[]{:S(2)}, u32[]{:S(2)}) collective-permute-start(f32[21,8,128]{2,1,0:T(8,128)S(1)} %get-tuple-element.34), channel_id=1, source_target_pairs={{8,0},{16,8},{24,16},{0,24},{9,1},{17,9},{25,17},{1,25},{10,2},{18... | collective-permute-start | bytes 258056 | tf_op jit(solution)/shard_map/ppermute | solution.py:584
  23.1 0.3 collective-permute-start.8
  23.4 2.1 %collective-permute-start.9 = (f32[12,16,128]{2,1,0:T(8,128)S(1)}, f32[12,16,128]{2,1,0:T(8,128)S(1)}, u32[]{:S(2)}, u32[]{:S(2)}) collective-permute-start(f32[12,16,128]{2,1,0:T(8,128)S(1)} %get-tuple-element.38), channel_id=1, source_target_pairs={{8,0},{16,8},{24,16},{0,24},{9,1},{17,9},{25,17},{1,25},{10,2},{18... | collective-permute-start | bytes 294920 | tf_op jit(solution)/shard_map/ppermute | solution.py:584
  25.5 0.4 collective-permute-done.4.left_ref
  25.8 0.6 %collective-permute-done.5.right_ref = f32[21,8,128]{2,1,0:T(8,128)S(1)} collective-permute-done((f32[21,8,128]{2,1,0:T(8,128)S(1)}, f32[21,8,128]{2,1,0:T(8,128)S(1)}, u32[]{:S(2)}, u32[]{:S(2)}) %collective-permute-start.5) | collective-permute-done | bytes 86048 | tf_op jit(solution)/shard_map/ppermute | solution.py:584
  26.5 5.0 %collective-permute-start.6 = (f32[280,128]{1,0:T(8,128)S(1)}, f32[280,128]{1,0:T(8,128)S(1)}, u32[]{:S(2)}, u32[]{:S(2)}) collective-permute-start(f32[280,128]{1,0:T(8,128)S(1)} %get-tuple-element.35.after_ref), channel_id=1, source_target_pairs={{0,0},{7,7},{1,2},{2,1},{3,4},{4,3},{5,6},{6,5},{8,8},{15,15},{9,1... | collective-permute-start | bytes 430088 | tf_op jit(solution)/shard_map/ppermute | solution.py:592
  31.4 0.1 collective-permute-start.7
  31.5 0.0 collective-permute-done.8.left_ref
  31.5 0.0 collective-permute-done.9.right_ref
  31.5 0.1 shard_map.61
  31.6 3.6 %collective-permute-start.10 = (f32[232,128]{1,0:T(8,128)S(1)}, f32[232,128]{1,0:T(8,128)S(1)}, u32[]{:S(2)}, u32[]{:S(2)}) collective-permute-start(f32[232,128]{1,0:T(8,128)S(1)} %get-tuple-element.39), channel_id=1, source_target_pairs={{0,0},{7,7},{1,2},{2,1},{3,4},{4,3},{5,6},{6,5},{8,8},{15,15},{9,1... | collective-permute-start | bytes 356360 | tf_op jit(solution)/shard_map/ppermute | solution.py:592
  35.2 0.1 collective-permute-start.11
  35.2 0.0 collective-permute-done.6.cross_ref
  35.3 0.0 collective-permute-done.7.same_ref
  35.3 2.6 %shard_map.60.change_ref = f32[3,24,24,128]{3,2,1,0:T(8,128)S(1)} custom-call(f32[6,24,24,128]{3,2,1,0:T(8,128)S(1)} %get-tuple-element.29.weight_ref, f32[4,8,8,128]{3,2,1,0:T(8,128)S(1)} %get-tuple-element.32.coarse_ref, f32[1]{0:T(128)S(6)} %copy.6.lower_ref, f32[1]{0:T(128)S(6)} %copy.7.upper_ref, f32[21,8,128]{2,1,0:T(8,128)S(1)} %collective-permute-done.4.left_ref, ...), custom_call_target="tpu_custom_call" | custom-call | tf_op jit(solution)/shard_map/pallas_call | solution.py:662
  37.8 0.0 collective-permute-done.10.cross_ref
  37.9 0.0 collective-permute-done.11.same_ref
  37.9 2.4 %shard_map.62 = f32[3,16,16,128]{3,2,1,0:T(8,128)} custom-call(f32[6,24,24,128]{3,2,1,0:T(8,128)S(1)} %get-tuple-element.29.weight_ref, f32[16,16,128]{2,1,0:T(8,128)S(1)} %get-tuple-element.30.diagonal_ref, f32[3,16,16,128]{3,2,1,0:T(8,128)S(1)} %get-tuple-element.31.smoothed_ref, f32[3,24,24,128]{3,2,1,0:T(8,128)S(1)} %shard_map.60.change_ref, ...), custom_call_target="tpu_custom_call" | custom-call | tf_op jit(solution)/shard_map/pallas_call | solution.py:677
  (1 shorter events, 0.0 us)
Async XLA Ops:
  1.0 6.4 %collective-permute-start = (f32[17,16,128]{2,1,0:T(8,128)S(1)}, f32[17,16,128]{2,1,0:T(8,128)S(1)}, u32[]{:S(2)}, u32[]{:S(2)}) collective-permute-start(f32[17,16,128]{2,1,0:T(8,128)S(1)} %get-tuple-element.25), channel_id=1, source_target_pairs={{0,8},{8,16},{16,24},{24,0},{1,9},{9,17},{17,25},{25,1},{2,10},{10... | collective-permute-start | bytes 417800 | tf_op jit(solution)/shard_map/ppermute | solution.py:584
  3.1 7.3 %collective-permute-start.1 = (f32[17,16,128]{2,1,0:T(8,128)S(1)}, f32[17,16,128]{2,1,0:T(8,128)S(1)}, u32[]{:S(2)}, u32[]{:S(2)}) collective-permute-start(f32[17,16,128]{2,1,0:T(8,128)S(1)} %get-tuple-element.26), channel_id=1, source_target_pairs={{8,0},{16,8},{24,16},{0,24},{9,1},{17,9},{25,17},{1,25},{10,2},{18... | collective-permute-start | bytes 417800 | tf_op jit(solution)/shard_map/ppermute | solution.py:584
  10.4 7.7 %collective-permute-start.2 = (f32[328,128]{1,0:T(8,128)S(1)}, f32[328,128]{1,0:T(8,128)S(1)}, u32[]{:S(2)}, u32[]{:S(2)}) collective-permute-start(f32[328,128]{1,0:T(8,128)S(1)} %get-tuple-element.27), channel_id=1, source_target_pairs={{0,0},{7,7},{1,2},{2,1},{3,4},{4,3},{5,6},{6,5},{8,8},{15,15},{9,1... | collective-permute-start | bytes 503816 | tf_op jit(solution)/shard_map/ppermute | solution.py:592
  15.1 3.0 %collective-permute-start.3 = (f32[328,128]{1,0:T(8,128)S(1)}, f32[328,128]{1,0:T(8,128)S(1)}, u32[]{:S(2)}, u32[]{:S(2)}) collective-permute-start(f32[328,128]{1,0:T(8,128)S(1)} %get-tuple-element.28), channel_id=1, source_target_pairs={{0,1},{1,0},{2,3},{3,2},{4,5},{5,4},{6,7},{7,6},{8,9},{9,8},{10,11... | collective-permute-start | bytes 503816 | tf_op jit(solution)/shard_map/ppermute | solution.py:592
  20.7 5.2 %collective-permute-start.4 = (f32[21,8,128]{2,1,0:T(8,128)S(1)}, f32[21,8,128]{2,1,0:T(8,128)S(1)}, u32[]{:S(2)}, u32[]{:S(2)}) collective-permute-start(f32[21,8,128]{2,1,0:T(8,128)S(1)} %get-tuple-element.33), channel_id=1, source_target_pairs={{0,8},{8,16},{16,24},{24,0},{1,9},{9,17},{17,25},{25,1},{2,10},{10... | collective-permute-start | bytes 258056 | tf_op jit(solution)/shard_map/ppermute | solution.py:584
  21.9 4.5 %collective-permute-start.5 = (f32[21,8,128]{2,1,0:T(8,128)S(1)}, f32[21,8,128]{2,1,0:T(8,128)S(1)}, u32[]{:S(2)}, u32[]{:S(2)}) collective-permute-start(f32[21,8,128]{2,1,0:T(8,128)S(1)} %get-tuple-element.34), channel_id=1, source_target_pairs={{8,0},{16,8},{24,16},{0,24},{9,1},{17,9},{25,17},{1,25},{10,2},{18... | collective-permute-start | bytes 258056 | tf_op jit(solution)/shard_map/ppermute | solution.py:584
  23.1 8.4 %collective-permute-start.8 = (f32[12,16,128]{2,1,0:T(8,128)S(1)}, f32[12,16,128]{2,1,0:T(8,128)S(1)}, u32[]{:S(2)}, u32[]{:S(2)}) collective-permute-start(f32[12,16,128]{2,1,0:T(8,128)S(1)} %get-tuple-element.37), channel_id=1, source_target_pairs={{0,8},{8,16},{16,24},{24,0},{1,9},{9,17},{17,25},{25,1},{2,10},{10... | collective-permute-start | bytes 294920 | tf_op jit(solution)/shard_map/ppermute | solution.py:584
  23.4 8.1 %collective-permute-start.9 = (f32[12,16,128]{2,1,0:T(8,128)S(1)}, f32[12,16,128]{2,1,0:T(8,128)S(1)}, u32[]{:S(2)}, u32[]{:S(2)}) collective-permute-start(f32[12,16,128]{2,1,0:T(8,128)S(1)} %get-tuple-element.38), channel_id=1, source_target_pairs={{8,0},{16,8},{24,16},{0,24},{9,1},{17,9},{25,17},{1,25},{10,2},{18... | collective-permute-start | bytes 294920 | tf_op jit(solution)/shard_map/ppermute | solution.py:584
  26.5 8.8 %collective-permute-start.6 = (f32[280,128]{1,0:T(8,128)S(1)}, f32[280,128]{1,0:T(8,128)S(1)}, u32[]{:S(2)}, u32[]{:S(2)}) collective-permute-start(f32[280,128]{1,0:T(8,128)S(1)} %get-tuple-element.35.after_ref), channel_id=1, source_target_pairs={{0,0},{7,7},{1,2},{2,1},{3,4},{4,3},{5,6},{6,5},{8,8},{15,15},{9,1... | collective-permute-start | bytes 430088 | tf_op jit(solution)/shard_map/ppermute | solution.py:592
  31.4 3.8 %collective-permute-start.7 = (f32[280,128]{1,0:T(8,128)S(1)}, f32[280,128]{1,0:T(8,128)S(1)}, u32[]{:S(2)}, u32[]{:S(2)}) collective-permute-start(f32[280,128]{1,0:T(8,128)S(1)} %get-tuple-element.36), channel_id=1, source_target_pairs={{0,1},{1,0},{2,3},{3,2},{4,5},{5,4},{6,7},{7,6},{8,9},{9,8},{10,11... | collective-permute-start | bytes 430088 | tf_op jit(solution)/shard_map/ppermute | solution.py:592
  31.6 6.3 %collective-permute-start.10 = (f32[232,128]{1,0:T(8,128)S(1)}, f32[232,128]{1,0:T(8,128)S(1)}, u32[]{:S(2)}, u32[]{:S(2)}) collective-permute-start(f32[232,128]{1,0:T(8,128)S(1)} %get-tuple-element.39), channel_id=1, source_target_pairs={{0,0},{7,7},{1,2},{2,1},{3,4},{4,3},{5,6},{6,5},{8,8},{15,15},{9,1... | collective-permute-start | bytes 356360 | tf_op jit(solution)/shard_map/ppermute | solution.py:592
  35.2 2.7 %collective-permute-start.11 = (f32[232,128]{1,0:T(8,128)S(1)}, f32[232,128]{1,0:T(8,128)S(1)}, u32[]{:S(2)}, u32[]{:S(2)}) collective-permute-start(f32[232,128]{1,0:T(8,128)S(1)} %get-tuple-element.40), channel_id=1, source_target_pairs={{0,1},{1,0},{2,3},{3,2},{4,5},{5,4},{6,7},{7,6},{8,9},{9,8},{10,11... | collective-permute-start | bytes 356360 | tf_op jit(solution)/shard_map/ppermute | solution.py:592
